TPU v7x, 32 devices: a whole 2x2x4 slice. The times are simulated.
32 devices in a mesh: parts: 2 (over y), leaf: 4 (over z), sub: 4 (over x, core).
Axes of the slice: x: 2, y: 2, z: 4, core: 2. Of those that a mesh axis runs over, the one named last changes fastest.
Arguments:
- points: float32 [6, 65536], P(None, ('parts', 'leaf', 'sub')), parts along dimension 1
- targets: float32 [64, 65536], P(None, ('parts', 'leaf', 'sub')), parts along dimension 1
- leaf_skel: int32 [32, 256], P(('parts', 'leaf', 'sub')), parts along dimension 0, may hold values from 0 to 2047, as said below
- node_keep: int32 [30, 256], P('parts'), parts along dimension 0, may hold values from 0 to 511, as said below
- lengthscales: float32 [12], P('parts'), parts along dimension 0, may hold values from 0.25 to 0.35
- noise_var: float32 [2], P('parts'), parts along dimension 0, may hold values from 0.5 to 1.5
Outputs:
- solution: float32 [64, 65536], P(None, ('parts', 'leaf', 'sub')), parts along dimension 1
- residual: float32 [64, 65536], P(None, ('parts', 'leaf', 'sub')), parts along dimension 1
There are 2 independent parts, one for each index of `parts`. A program takes and returns all parts, laid end to end along the dimension named above; each array names one. Nothing has to cross between parts.
Inputs may be any that keep to these rules, and one draw needn't show every extreme that they name: `leaf_skel`: row t lists 256 distinct positions among the 2048 points of leaf t. `node_keep`: row n lists 256 distinct positions in the concatenation of the skeletons of heap nodes 2n+1 and 2n+2, the first node's 256 points before the second's.
All inputs are finite; a program needn't handle non-finite values.
Results may differ from a plain program's by a relative error of at most 0.0004.
Values sent between devices are 32-bit elements; how exact they have to be, the bound alone decides.
No kernel may reach another device: no remote copies, remote signals or barrier semaphores. Data moves between devices by JAX's collectives and lax.ppermute only.
A program may use at most 128 MiB of HBM per device.

v0:
```python
import jax
import jax.numpy as jnp
from jax import lax
from jax.sharding import PartitionSpec as P

ITERS = 3


def from_partner(shard, axis, stride):
    return lax.ppermute(shard, axis, [(i, i ^ 1 << stride) for i in range(lax.axis_size(axis))])


def kernel(left, right, inverse_scale):
    squared = jnp.zeros((left.shape[1], right.shape[1]), jnp.float32)
    for axis_number in range(left.shape[0]):
        offset = (left[axis_number][:, None] - right[axis_number][None, :]) * inverse_scale[
            axis_number
        ]
        squared = squared + offset * offset
    return jnp.exp(-0.5 * squared)


def product(first, second):
    return jnp.dot(
        first, second, precision=lax.Precision.HIGHEST, preferred_element_type=jnp.float32
    )


def merged(own_part, their_part, on_right):
    return jnp.concatenate(
        [jnp.where(on_right, their_part, own_part), jnp.where(on_right, own_part, their_part)],
        axis=-1,
    )


def climb_up(packed, sibling, on_right, chosen, dims, inverse_scale):
    joined = merged(packed, sibling, on_right)
    joined_coords = joined[:dims]
    parent = jnp.take(joined_coords, chosen, axis=1)
    transfer = kernel(joined_coords, parent, inverse_scale)
    return (parent, product(joined[dims:], transfer), transfer)


def body(points, targets, leaf_skel, node_keep, lengthscales, noise_var):
    dims = points.shape[0]
    leaf_size = points.shape[1]
    skeleton_rank = leaf_skel.shape[1]
    rhs_count = targets.shape[0]
    inverse_scale = 1.0 / lengthscales
    sub_count = lax.axis_size("sub")
    leaf_count = lax.axis_size("leaf")
    sub_levels = sub_count.bit_length() - 1
    levels = sub_levels + leaf_count.bit_length() - 1
    leaf_number = lax.axis_index("leaf") * sub_count + lax.axis_index("sub")
    own_coords = jnp.take(points, leaf_skel[0], axis=1)
    leaf_basis = kernel(points, own_coords, inverse_scale)
    block_width = min(256, leaf_size)
    blocks = leaf_size // block_width

    def pick_rows(tree_level):
        heap_index = (1 << levels - tree_level) - 1 + (leaf_number >> tree_level)
        return lax.dynamic_index_in_dim(node_keep, heap_index, 0, keepdims=False)

    def side_of(tree_level):
        return leaf_number >> tree_level - 1 & 1 == 1

    solution = jnp.zeros_like(targets)
    residual = targets
    direction = targets
    norm_now = lax.psum(jnp.sum(residual * residual, axis=1), ("leaf", "sub"))
    for iteration in range(ITERS):
        node_weight = product(direction, leaf_basis)
        coords = own_coords
        ancestry = []
        for apply_tree_level in range(1, sub_levels + 1):
            on_right = side_of(apply_tree_level)
            packed = jnp.concatenate([coords, node_weight], axis=0)
            sibling = from_partner(packed, "sub", apply_tree_level - 1)
            crossing = kernel(sibling[:dims], coords, inverse_scale)
            sibling_w = sibling[dims:]
            coords, node_weight, transfer = climb_up(
                packed, sibling, on_right, pick_rows(apply_tree_level), dims, inverse_scale
            )
            ancestry.append((transfer, crossing, sibling_w, on_right))
        for apply_tree_level in range(sub_levels + 1, levels + 1):
            on_right = side_of(apply_tree_level)
            packed = jnp.concatenate([coords, node_weight], axis=0)
            sibling = from_partner(packed, "leaf", apply_tree_level - 1 - sub_levels)
            crossing = kernel(sibling[:dims], coords, inverse_scale)
            sibling_w = sibling[dims:]
            coords, node_weight, transfer = climb_up(
                packed, sibling, on_right, pick_rows(apply_tree_level), dims, inverse_scale
            )
            ancestry.append((transfer, crossing, sibling_w, on_right))
        search_vector = jnp.zeros((rhs_count, skeleton_rank), jnp.float32)
        for apply_tree_level in range(levels, 0, -1):
            transfer, crossing, sibling_w, on_right = ancestry[apply_tree_level - 1]
            downward_sweep = product(search_vector, transfer.T)
            own_half = jnp.where(
                on_right, downward_sweep[:, skeleton_rank:], downward_sweep[:, :skeleton_rank]
            )
            search_vector = product(sibling_w, crossing) + own_half
        far_term = product(search_vector, leaf_basis.T)
        values = direction

        def one_block(block_index):
            columns = lax.dynamic_slice_in_dim(points, block_index * block_width, block_width, 1)
            return product(values, kernel(points, columns, inverse_scale))

        pieces = lax.map(one_block, jnp.arange(blocks))
        image = noise_var[0] * direction + (
            jnp.transpose(pieces, (1, 0, 2)).reshape(values.shape[0], leaf_size) + far_term
        )
        curve = lax.psum(jnp.sum(direction * image, axis=1), ("leaf", "sub"))
        step_size = norm_now / curve
        solution = solution + step_size[:, None] * direction
        residual = residual - step_size[:, None] * image
        if iteration + 1 < ITERS:
            norm_next = lax.psum(jnp.sum(residual * residual, axis=1), ("leaf", "sub"))
        if iteration + 1 < ITERS:
            direction = residual + (norm_next / norm_now)[:, None] * direction
            norm_now = norm_next
    return (solution, residual)


def solution(mesh):
    in_specs = (
        P(None, ("parts", "leaf", "sub")),
        P(None, ("parts", "leaf", "sub")),
        P(("parts", "leaf", "sub"), None),
        P("parts", None),
        P("parts"),
        P("parts"),
    )
    out_specs = (P(None, ("parts", "leaf", "sub")), P(None, ("parts", "leaf", "sub")))
    return jax.shard_map(body, mesh=mesh, in_specs=in_specs, out_specs=out_specs, check_vma=False)
```

profile of v0, /device:TPU:0, one launch (start us, length us, event | category | flops | bytes accessed | tf_op | source)
XLA Modules:
  0.0 633.5 jit_solution(1695092716191772870)
XLA Ops:
  4.5 7.0 %convolution_bitcast_fusion = f32[64,256]{1,0:T(8,128)S(1)} fusion(f32[64,2048]{1,0:T(8,128)S(1)} %copy-done.1, f32[]{:T(128)} %bitcast.86, f32[256]{0:T(256)S(1)} %bitcast.707, f32[2048]{0:T(1024)S(1)} %bitcast.534, f32[]{:T(128)} %bitcast.83, f32[256]{0:T(256)S(1)} %bitcast.716, f32[2048]{0:T(1024)S(1)} %bitcast.540, f32[]{:T(128)} %bitcast.80, ...), kind=kOutput, calls=%fused_computation.179 | convolution fusion | flops 415236096 | bytes 645144 | tf_op jit(solution)/shard_map/dot_general | solution.py:24
  12.3 72.7 %while.30 = (s32[]{:T(128)}, f32[8,64,256]{2,1,0:T(8,128)S(1)}, f32[6,2048]{1,0:T(8,128)S(1)}, s32[8]{0:T(128)S(1)}, f32[6]{0:T(128)S(1)}, /*index=5*/f32[64,204...) while((s32[]{:T(128)}, f32[8,64,256]{2,1,0:T(8,128)S(1)}, ...), condition=%wide.region_3.4_spmd, body=%wide.region_2.3_spmd.sunk | while | flops 415236096 | bytes 756071 | solution.py:110
  14.4 6.9 %fusion.1032 = f32[8,64,256]{2,1,0:T(8,128)S(1)} fusion(f32[8,64,256]{2,1,0:T(8,128)S(1)} %get-tuple-element.708, s32[]{:T(128)} %get-tuple-element.707, f32[64,2048]{1,0:T(8,128)S(1)} %get-tuple-element.727, f32[]{:T(128)} %bitcast.420, f32[256]{0:T(256)S(1)} %bitcast.513, f32[2048]{0:T(1024)S(1)} %bitcast.491, f32[]{:T(128)} %bitcast.424, ...), kind=kOutput, calls=%fused_computation.40.clone.1 | convolution fusion | flops 415236096 | bytes 645148 | tf_op jit(solution)/shard_map/while/body/eval_jaxpr/dot_general | solution.py:24
  23.5 6.9 %fusion.1032 = f32[8,64,256]{2,1,0:T(8,128)S(1)} fusion(f32[8,64,256]{2,1,0:T(8,128)S(1)} %get-tuple-element.708, s32[]{:T(128)} %get-tuple-element.707, f32[64,2048]{1,0:T(8,128)S(1)} %get-tuple-element.727, f32[]{:T(128)} %bitcast.420, f32[256]{0:T(256)S(1)} %bitcast.513, f32[2048]{0:T(1024)S(1)} %bitcast.491, f32[]{:T(128)} %bitcast.424, ...), kind=kOutput, calls=%fused_computation.40.clone.1 | convolution fusion | flops 415236096 | bytes 645148 | tf_op jit(solution)/shard_map/while/body/eval_jaxpr/dot_general | solution.py:24
  32.5 6.9 %fusion.1032 = f32[8,64,256]{2,1,0:T(8,128)S(1)} fusion(f32[8,64,256]{2,1,0:T(8,128)S(1)} %get-tuple-element.708, s32[]{:T(128)} %get-tuple-element.707, f32[64,2048]{1,0:T(8,128)S(1)} %get-tuple-element.727, f32[]{:T(128)} %bitcast.420, f32[256]{0:T(256)S(1)} %bitcast.513, f32[2048]{0:T(1024)S(1)} %bitcast.491, f32[]{:T(128)} %bitcast.424, ...), kind=kOutput, calls=%fused_computation.40.clone.1 | convolution fusion | flops 415236096 | bytes 645148 | tf_op jit(solution)/shard_map/while/body/eval_jaxpr/dot_general | solution.py:24
  41.6 6.9 %fusion.1032 = f32[8,64,256]{2,1,0:T(8,128)S(1)} fusion(f32[8,64,256]{2,1,0:T(8,128)S(1)} %get-tuple-element.708, s32[]{:T(128)} %get-tuple-element.707, f32[64,2048]{1,0:T(8,128)S(1)} %get-tuple-element.727, f32[]{:T(128)} %bitcast.420, f32[256]{0:T(256)S(1)} %bitcast.513, f32[2048]{0:T(1024)S(1)} %bitcast.491, f32[]{:T(128)} %bitcast.424, ...), kind=kOutput, calls=%fused_computation.40.clone.1 | convolution fusion | flops 415236096 | bytes 645148 | tf_op jit(solution)/shard_map/while/body/eval_jaxpr/dot_general | solution.py:24
  50.7 6.9 %fusion.1032 = f32[8,64,256]{2,1,0:T(8,128)S(1)} fusion(f32[8,64,256]{2,1,0:T(8,128)S(1)} %get-tuple-element.708, s32[]{:T(128)} %get-tuple-element.707, f32[64,2048]{1,0:T(8,128)S(1)} %get-tuple-element.727, f32[]{:T(128)} %bitcast.420, f32[256]{0:T(256)S(1)} %bitcast.513, f32[2048]{0:T(1024)S(1)} %bitcast.491, f32[]{:T(128)} %bitcast.424, ...), kind=kOutput, calls=%fused_computation.40.clone.1 | convolution fusion | flops 415236096 | bytes 645148 | tf_op jit(solution)/shard_map/while/body/eval_jaxpr/dot_general | solution.py:24
  59.7 6.9 %fusion.1032 = f32[8,64,256]{2,1,0:T(8,128)S(1)} fusion(f32[8,64,256]{2,1,0:T(8,128)S(1)} %get-tuple-element.708, s32[]{:T(128)} %get-tuple-element.707, f32[64,2048]{1,0:T(8,128)S(1)} %get-tuple-element.727, f32[]{:T(128)} %bitcast.420, f32[256]{0:T(256)S(1)} %bitcast.513, f32[2048]{0:T(1024)S(1)} %bitcast.491, f32[]{:T(128)} %bitcast.424, ...), kind=kOutput, calls=%fused_computation.40.clone.1 | convolution fusion | flops 415236096 | bytes 645148 | tf_op jit(solution)/shard_map/while/body/eval_jaxpr/dot_general | solution.py:24
  68.8 6.9 %fusion.1032 = f32[8,64,256]{2,1,0:T(8,128)S(1)} fusion(f32[8,64,256]{2,1,0:T(8,128)S(1)} %get-tuple-element.708, s32[]{:T(128)} %get-tuple-element.707, f32[64,2048]{1,0:T(8,128)S(1)} %get-tuple-element.727, f32[]{:T(128)} %bitcast.420, f32[256]{0:T(256)S(1)} %bitcast.513, f32[2048]{0:T(1024)S(1)} %bitcast.491, f32[]{:T(128)} %bitcast.424, ...), kind=kOutput, calls=%fused_computation.40.clone.1 | convolution fusion | flops 415236096 | bytes 645148 | tf_op jit(solution)/shard_map/while/body/eval_jaxpr/dot_general | solution.py:24
  77.8 6.9 %fusion.1032 = f32[8,64,256]{2,1,0:T(8,128)S(1)} fusion(f32[8,64,256]{2,1,0:T(8,128)S(1)} %get-tuple-element.708, s32[]{:T(128)} %get-tuple-element.707, f32[64,2048]{1,0:T(8,128)S(1)} %get-tuple-element.727, f32[]{:T(128)} %bitcast.420, f32[256]{0:T(256)S(1)} %bitcast.513, f32[2048]{0:T(1024)S(1)} %bitcast.491, f32[]{:T(128)} %bitcast.424, ...), kind=kOutput, calls=%fused_computation.40.clone.1 | convolution fusion | flops 415236096 | bytes 645148 | tf_op jit(solution)/shard_map/while/body/eval_jaxpr/dot_general | solution.py:24
  156.5 8.1 %multiply_reduce_fusion.4 = (f32[64]{0:T(128)S(1)}, f32[64]{0:T(128)S(1)}, f32[64,2048]{1,0:T(8,128)S(1)}) fusion(f32[64,2048]{1,0:T(8,128)S(1)} %get-tuple-element.829, f32[64,2048]{1,0:T(8,128)S(1)} %bitcast.488, f32[64,256]{1,0:T(8,128)S(1)} %convolution_add_fusion.14, f32[]{:T(128)} %bitcast.86, f32[256]{0:T(256)S(1)} %bitcast.709, ...), kind=kOutput, calls=%fused_computation.248 | convolution fusion | flops 416153472 | bytes 1694236 | tf_op jit(solution)/shard_map/dot_general | solution.py:24
  164.5 31.9 %all-reduce = (f32[64]{0:T(128)S(1)}, f32[64]{0:T(128)S(1)}) all-reduce(f32[64]{0:T(128)S(1)} %get-tuple-element.103, f32[64]{0:T(128)S(1)} %get-tuple-element.102), channel_id=1, replica_groups=mesh['parts'=2,'leaf'=4,'sub'=4] {'leaf','sub'}, use_global_device_ids=true, to_apply=%region_1.2 | all-reduce | flops 128 | bytes 1024 | tf_op jit(solution)/shard_map/psum | solution.py:70
  196.7 29.5 %psum.44 = f32[64]{0:T(128)S(1)} all-reduce(f32[64]{0:T(128)S(1)} %multiply_reduce_fusion.3), channel_id=1, replica_groups=mesh['parts'=2,'leaf'=4,'sub'=4] {'leaf','sub'}, use_global_device_ids=true, to_apply=%region_7.9 | all-reduce | flops 64 | bytes 512 | tf_op jit(solution)/shard_map/psum | solution.py:119
  233.3 72.7 %while.31 = (s32[]{:T(128)}, f32[8,64,256]{2,1,0:T(8,128)S(1)}, f32[6,2048]{1,0:T(8,128)S(1)}, s32[8]{0:T(128)S(1)}, f32[6]{0:T(128)S(1)}, /*index=5*/f32[64,204...) while((s32[]{:T(128)}, f32[8,64,256]{2,1,0:T(8,128)S(1)}, ...), condition=%wide.region_9.11_spmd, body=%wide.region_8.10_spmd.sunk | while | flops 415236096 | bytes 756071 | solution.py:110
  235.5 6.9 %fusion.1037 = f32[8,64,256]{2,1,0:T(8,128)S(1)} fusion(f32[8,64,256]{2,1,0:T(8,128)S(1)} %get-tuple-element.753, s32[]{:T(128)} %get-tuple-element.752, f32[64,2048]{1,0:T(8,128)S(1)} %get-tuple-element.772, f32[]{:T(128)} %bitcast.441, f32[256]{0:T(256)S(1)} %bitcast.519, f32[2048]{0:T(1024)S(1)} %bitcast.497, f32[]{:T(128)} %bitcast.445, ...), kind=kOutput, calls=%fused_computation.89.clone.1 | convolution fusion | flops 415236096 | bytes 645148 | tf_op jit(solution)/shard_map/while/body/eval_jaxpr/dot_general | solution.py:24
  376.3 7.9 %multiply_reduce_fusion.2 = (f32[64]{0:T(128)S(1)}, f32[64,2048]{1,0:T(8,128)S(1)}) fusion(f32[64,2048]{1,0:T(8,128)S(1)} %get-tuple-element.832, f32[64,2048]{1,0:T(8,128)S(1)} %bitcast.489, f32[64,256]{1,0:T(8,128)S(1)} %convolution_add_fusion.10, f32[]{:T(128)} %bitcast.86, f32[256]{0:T(256)S(1)} %bitcast.712, f32[2048]{0:T(1024)S(1)} %bitcast.537, ...), kind=kOutput, calls=%fused_computation.215 | convolution fusion | flops 415891392 | bytes 1693980 | tf_op jit(solution)/shard_map/dot_general | solution.py:24
  384.2 29.5 %psum.45 = f32[64]{0:T(128)S(1)} all-reduce(f32[64]{0:T(128)S(1)} %get-tuple-element.463), channel_id=1, replica_groups=mesh['parts'=2,'leaf'=4,'sub'=4] {'leaf','sub'}, use_global_device_ids=true, to_apply=%region_11.13 | all-reduce | flops 64 | bytes 512 | tf_op jit(solution)/shard_map/psum | solution.py:114
  414.3 29.5 %psum.46 = f32[64]{0:T(128)S(1)} all-reduce(f32[64]{0:T(128)S(1)} %get-tuple-element.160), channel_id=1, replica_groups=mesh['parts'=2,'leaf'=4,'sub'=4] {'leaf','sub'}, use_global_device_ids=true, to_apply=%region_13.15 | all-reduce | flops 64 | bytes 512 | tf_op jit(solution)/shard_map/psum | solution.py:119
  451.4 72.2 %while.32 = (s32[]{:T(128)}, f32[8,64,256]{2,1,0:T(8,128)S(1)}, f32[6,2048]{1,0:T(8,128)S(1)}, s32[8]{0:T(128)S(1)}, f32[6]{0:T(128)S(1)}, /*index=5*/f32[64,204...) while((s32[]{:T(128)}, f32[8,64,256]{2,1,0:T(8,128)S(1)}, ...), condition=%wide.region_15.17_spmd, body=%wide.region_14.16_spmd.sunk | while | flops 415236096 | bytes 756071 | solution.py:110
  453.5 6.9 %fusion.1042 = f32[8,64,256]{2,1,0:T(8,128)S(1)} fusion(f32[8,64,256]{2,1,0:T(8,128)S(1)} %get-tuple-element.798, s32[]{:T(128)} %get-tuple-element.797, f32[64,2048]{1,0:T(8,128)S(1)} %get-tuple-element.817, f32[]{:T(128)} %bitcast.462, f32[256]{0:T(256)S(1)} %bitcast.525, f32[2048]{0:T(1024)S(1)} %bitcast.503, f32[]{:T(128)} %bitcast.466, ...), kind=kOutput, calls=%fused_computation.138.clone.1 | convolution fusion | flops 415236096 | bytes 645148 | tf_op jit(solution)/shard_map/while/body/eval_jaxpr/dot_general | solution.py:24
  471.5 6.9 %fusion.1042 = f32[8,64,256]{2,1,0:T(8,128)S(1)} fusion(f32[8,64,256]{2,1,0:T(8,128)S(1)} %get-tuple-element.798, s32[]{:T(128)} %get-tuple-element.797, f32[64,2048]{1,0:T(8,128)S(1)} %get-tuple-element.817, f32[]{:T(128)} %bitcast.462, f32[256]{0:T(256)S(1)} %bitcast.525, f32[2048]{0:T(1024)S(1)} %bitcast.503, f32[]{:T(128)} %bitcast.466, ...), kind=kOutput, calls=%fused_computation.138.clone.1 | convolution fusion | flops 415236096 | bytes 645148 | tf_op jit(solution)/shard_map/while/body/eval_jaxpr/dot_general | solution.py:24
  498.5 6.9 %fusion.1042 = f32[8,64,256]{2,1,0:T(8,128)S(1)} fusion(f32[8,64,256]{2,1,0:T(8,128)S(1)} %get-tuple-element.798, s32[]{:T(128)} %get-tuple-element.797, f32[64,2048]{1,0:T(8,128)S(1)} %get-tuple-element.817, f32[]{:T(128)} %bitcast.462, f32[256]{0:T(256)S(1)} %bitcast.525, f32[2048]{0:T(1024)S(1)} %bitcast.503, f32[]{:T(128)} %bitcast.466, ...), kind=kOutput, calls=%fused_computation.138.clone.1 | convolution fusion | flops 415236096 | bytes 645148 | tf_op jit(solution)/shard_map/while/body/eval_jaxpr/dot_general | solution.py:24
  594.7 7.6 %multiply_reduce_fusion = (f32[64]{0:T(128)S(1)}, f32[64,2048]{1,0:T(8,128)S(1)}) fusion(f32[64,2048]{1,0:T(8,128)S(1)} %get-tuple-element.833, f32[64,2048]{1,0:T(8,128)S(1)} %bitcast.487, f32[64,256]{1,0:T(8,128)S(1)} %convolution_add_fusion.6, f32[]{:T(128)} %bitcast.86, f32[256]{0:T(256)S(1)} %bitcast.715, f32[2048]{0:T(1024)S(1)} %bitcast.539, ...), kind=kOutput, calls=%fused_computation.182 | convolution fusion | flops 415891392 | bytes 1693980 | tf_op jit(solution)/shard_map/dot_general | solution.py:24
  602.3 29.5 %psum.47 = f32[64]{0:T(128)S(1)} all-reduce(f32[64]{0:T(128)S(1)} %get-tuple-element.465), channel_id=1, replica_groups=mesh['parts'=2,'leaf'=4,'sub'=4] {'leaf','sub'}, use_global_device_ids=true, to_apply=%region_17.19 | all-reduce | flops 64 | bytes 512 | tf_op jit(solution)/shard_map/psum | solution.py:114
  (428 shorter events, 349.2 us)
Async XLA Ops:
  2.0 442.4 %copy-start.2 = (f32[1,2048]{1,0:T(1,128)}, f32[1,2048]{1,0:T(1,128)S(1)}, u32[]{:S(2)}) copy-start(f32[1,2048]{1,0:T(1,128)S(1)} %get-tuple-element.388) | copy-start | bytes 24580
  2.0 442.4 %copy-start.4 = (f32[1,2048]{1,0:T(1,128)}, f32[1,2048]{1,0:T(1,128)S(1)}, u32[]{:S(2)}) copy-start(f32[1,2048]{1,0:T(1,128)S(1)} %get-tuple-element.389) | copy-start | bytes 24580
  3.8 440.6 %copy-start.13 = (f32[1,256]{1,0:T(1,128)}, f32[1,256]{1,0:T(1,128)S(1)}, u32[]{:S(2)}) copy-start(f32[1,256]{1,0:T(1,128)S(1)} %get-tuple-element.448) | copy-start | bytes 3076
  3.8 440.6 %copy-start.15 = (f32[1,256]{1,0:T(1,128)}, f32[1,256]{1,0:T(1,128)S(1)}, u32[]{:S(2)}) copy-start(f32[1,256]{1,0:T(1,128)S(1)} %get-tuple-element.449) | copy-start | bytes 3076
  3.8 440.6 %copy-start.17 = (f32[1,256]{1,0:T(1,128)}, f32[1,256]{1,0:T(1,128)S(1)}, u32[]{:S(2)}) copy-start(f32[1,256]{1,0:T(1,128)S(1)} %get-tuple-element.450) | copy-start | bytes 3076
  3.8 440.6 %copy-start.19 = (f32[1,256]{1,0:T(1,128)}, f32[1,256]{1,0:T(1,128)S(1)}, u32[]{:S(2)}) copy-start(f32[1,256]{1,0:T(1,128)S(1)} %get-tuple-element.451) | copy-start | bytes 3076
  3.8 440.6 %copy-start.21 = (f32[1,256]{1,0:T(1,128)}, f32[1,256]{1,0:T(1,128)S(1)}, u32[]{:S(2)}) copy-start(f32[1,256]{1,0:T(1,128)S(1)} %get-tuple-element.452) | copy-start | bytes 3076
  3.8 440.6 %copy-start.23 = (f32[1,256]{1,0:T(1,128)}, f32[1,256]{1,0:T(1,128)S(1)}, u32[]{:S(2)}) copy-start(f32[1,256]{1,0:T(1,128)S(1)} %get-tuple-element.453) | copy-start | bytes 3076
  11.6 74.1 %collective-permute-start = (f32[70,256]{1,0:T(8,128)S(1)}, f32[70,256]{1,0:T(8,128)S(1)}, u32[]{:S(2)}, u32[]{:S(2)}) collective-permute-start(f32[70,256]{1,0:T(8,128)S(1)} %pad_maximum_fusion.2), channel_id=1, source_target_pairs={{0,1},{1,0},{2,3},{3,2},{4,5},{5,4},{6,7},{7,6},{8,9},{9,8},{10,11... | collective-permute-start | bytes 215048 | tf_op jit(solution)/shard_map/ppermute | solution.py:10
  12.1 295.0 %copy-start.8 = (pred[256]{0:T(512)(128)(4,1)}, pred[256]{0:T(512)(128)(4,1)S(1)}, u32[]{:S(2)}) copy-start(pred[256]{0:T(512)(128)(4,1)S(1)} %compare_and_fusion.3) | copy-start | bytes 772
  12.1 305.5 %copy-start.6 = (pred[256]{0:T(512)(128)(4,1)}, pred[256]{0:T(512)(128)(4,1)S(1)}, u32[]{:S(2)}) copy-start(pred[256]{0:T(512)(128)(4,1)S(1)} %compare_and_fusion.2) | copy-start | bytes 772
  91.5 5.5 collective-permute-start.1
  102.7 4.4 collective-permute-start.2
  112.8 5.3 collective-permute-start.3
  233.2 72.9 %collective-permute-start.4 = (f32[70,256]{1,0:T(8,128)S(1)}, f32[70,256]{1,0:T(8,128)S(1)}, u32[]{:S(2)}, u32[]{:S(2)}) collective-permute-start(f32[70,256]{1,0:T(8,128)S(1)} %pad_maximum_fusion.1), channel_id=1, source_target_pairs={{0,1},{1,0},{2,3},{3,2},{4,5},{5,4},{6,7},{7,6},{8,9},{9,8},{10,11... | collective-permute-start | bytes 215048 | tf_op jit(solution)/shard_map/ppermute | solution.py:10
  311.8 4.7 collective-permute-start.5
  322.3 4.4 collective-permute-start.6
  332.5 5.6 collective-permute-start.7
  451.3 72.4 %collective-permute-start.8 = (f32[70,256]{1,0:T(8,128)S(1)}, f32[70,256]{1,0:T(8,128)S(1)}, u32[]{:S(2)}, u32[]{:S(2)}) collective-permute-start(f32[70,256]{1,0:T(8,128)S(1)} %pad_maximum_fusion), channel_id=1, source_target_pairs={{0,1},{1,0},{2,3},{3,2},{4,5},{5,4},{6,7},{7,6},{8,9},{9,8},{10,11... | collective-permute-start | bytes 215048 | tf_op jit(solution)/shard_map/ppermute | solution.py:10
  529.5 4.7 collective-permute-start.9
  540.1 4.4 collective-permute-start.10
  550.3 5.6 collective-permute-start.11
  594.6 37.2 %copy-start.51 = (f32[64]{0:T(128)S(1)}, f32[64]{0:T(128)}, u32[]{:S(2)}) copy-start(f32[64]{0:T(128)} %copy-done.50) | copy-start | bytes 772
  594.6 37.2 %copy-start.12 = (f32[64]{0:T(128)S(1)}, f32[64]{0:T(128)}, u32[]{:S(2)}) copy-start(f32[64]{0:T(128)} %copy-done.11) | copy-start | bytes 772
  (40 other events, 174.4 us)
where the time goes:
time: 643 us; the launch traced here: 633 us
  matrix products  362 us (56%)
  blocking collectives  150 us (23%)
  local copies, waits for them, and re-layouts  53.5 us (8%)
  waiting for transfers between devices  35.5 us (6%)
  loops' own time  17.4 us (3%)
  starting transfers between devices  8.43 us (1%)
    dot_general x63, matrix products, product(): jnp.dot(first, second, precision=lax.Precision.HIGHEST, preferred_element...  362 us
    psum x2, blocking collectives, body(): curve = lax.psum(jnp.sum(direction * image, axis=1), ('leaf', 'sub'))  59 us
    psum x2, blocking collectives, body(): norm_next = lax.psum(jnp.sum(residual * residual, axis=1), ('leaf', 'sub'))  59 us
    ppermute x12, waiting for transfers between devices, from_partner(): lax.ppermute(shard, axis, [(i, i ^ 1 << stride) for i in range(lax.axis_s...  35.5 us
    psum x1, blocking collectives, body(): norm_now = lax.psum(jnp.sum(residual * residual, axis=1), ('leaf', 'sub'))  31.9 us
    another operation x3, loops' own time, body(): pieces = lax.map(one_block, jnp.arange(blocks))  17.4 us
    slice x25, local copies, waits for them, and re-layouts, kernel(): inverse_scale[axis_number]  16.8 us
    dynamic_slice x24, local copies, waits for them, and re-layouts, body(): pieces = lax.map(one_block, jnp.arange(blocks))  15.3 us
  transfers between devices with their start and end apart: 12, of which 9 were waited for; matrix products, arithmetic and copies ran while one was open for 32% of the time, Pallas kernels for 0%

commit v1 on v0

v1 whole, which is shorter than its diff:
```python
import functools
import math

import jax
import jax.numpy as jnp
from jax import lax
from jax.experimental import pallas as pl
from jax.experimental.pallas import tpu as pltpu
from jax.sharding import PartitionSpec as P

F32 = jnp.float32
BF16 = jnp.bfloat16
VMEM = pl.BlockSpec(memory_space=pltpu.VMEM)
ANY = pl.BlockSpec(memory_space=pl.ANY)
NN = (((1,), (0,)), ((), ()))
NT = (((1,), (1,)), ((), ()))
SCALE = math.sqrt(0.5 * math.log2(math.e))
STRIP = 128
BLOCK = 256


def call(kernel, out_shape, args, anywhere=(), scratch=(), name=None, cost=None):
    total = sum(a.size * a.dtype.itemsize for i, a in enumerate(args) if i not in anywhere)
    total += sum(math.prod(s.shape) * s.dtype.itemsize for s in out_shape)
    if cost is not None:
        cost = pl.CostEstimate(flops=cost[0], transcendentals=cost[1], bytes_accessed=total)
    results = pl.pallas_call(
        kernel,
        out_shape=list(out_shape),
        in_specs=[ANY if i in anywhere else VMEM for i in range(len(args))],
        out_specs=[VMEM] * len(out_shape),
        scratch_shapes=list(scratch),
        compiler_params=pltpu.CompilerParams(vmem_limit_bytes=total + (8 << 20)),
        cost_estimate=cost,
        name=name,
    )(*args)
    return list(results)


def f32_shape(*shape):
    return jax.ShapeDtypeStruct(shape, F32)


def bf16_shape(*shape):
    return jax.ShapeDtypeStruct(shape, BF16)


def split(value):
    high = value.astype(BF16)
    return high, (value - high.astype(F32)).astype(BF16)


def split3(value):
    high = value.astype(BF16)
    rest = value - high.astype(F32)
    middle = rest.astype(BF16)
    return high, middle, (rest - middle.astype(F32)).astype(BF16)


def dot3(value, high, low, dims=NN):
    rows = value.shape[0]
    vh, vl = split(value)
    both = lax.dot_general(
        jnp.concatenate([vh, vl], axis=0), high, dims, preferred_element_type=F32
    )
    return both[:rows] + both[rows:] + lax.dot_general(vh, low, dims, preferred_element_type=F32)


def gauss(left, right, dims):
    squared = None
    for d in range(dims):
        offset = left[:, d : d + 1] - right[d : d + 1, :]
        squared = offset * offset if squared is None else squared + offset * offset
    return jnp.exp2(-squared)


def pick(table, chosen):
    rows, pool = table.shape
    hit = lax.broadcasted_iota(jnp.int32, (pool, chosen.shape[1]), 0) == chosen
    onehot = jnp.where(hit, 1.0, 0.0).astype(BF16)
    parts = [lax.dot_general(t, onehot, NN, preferred_element_type=F32) for t in split3(table)]
    return parts[0] + parts[1] + parts[2]


def to_rows(columns, width):
    rows = columns[0].shape[0]
    lane = lax.broadcasted_iota(jnp.int32, (rows, 128), 1)
    block = jnp.zeros((rows, 128), F32)
    for i, column in enumerate(columns):
        block = jnp.where(lane == i, column, block)
    if rows < 128:
        block = jnp.concatenate([block, jnp.zeros((128 - rows, 128), F32)], axis=0)
    flipped = block.T[:8]
    return jnp.concatenate([flipped, jnp.zeros((8, width - 128), F32)], axis=1)


def to_columns(block, rows):
    square = jnp.concatenate([block[:, :128], jnp.zeros((120, 128), F32)], axis=0)
    return square.T[:rows]


def row_sum(value):
    return jnp.sum(value, axis=1, keepdims=True)


def setup_kernel(stages, total, anchors, *refs):
    sources, refs = refs[:6], refs[6:]
    message, rhs, pts_row, basis_h, basis_l, chosen_out, params = refs[:7]
    pts, skel, keep, scales, noise, pts_col, sems = refs[7:]
    targets = (pts, rhs, skel, keep, scales, noise)
    copies = [
        pltpu.make_async_copy(source, target, sems.at[i])
        for i, (source, target) in enumerate(zip(sources, targets))
    ]
    for copy in copies:
        copy.start()
    for i in (0, 2, 4):
        copies[i].wait()
    dims, count = pts.shape
    points = jnp.concatenate([pts[...], jnp.zeros((8 - dims, count), F32)], axis=0)
    row = lax.broadcasted_iota(jnp.int32, (8, dims), 0)
    lane = lax.broadcasted_iota(jnp.int32, (8, dims), 1)
    spread = jnp.broadcast_to(scales[...], (8, dims))
    length = row_sum(jnp.where(row == lane, spread, 0.0))
    valid = lax.broadcasted_iota(jnp.int32, (8, 1), 0) < dims
    inverse = SCALE / jnp.where(valid, length, 1.0)
    shift = points[:, 0:1]
    chosen = pick(points, skel[...])
    rows = rhs.shape[0]
    message[rows + 8 :, :] = chosen
    scaled = (points - shift) * inverse
    own = (chosen - shift) * inverse
    pts_row[...] = scaled
    pts_col[...] = scaled.T
    for i in range(count // STRIP):
        strip = slice(i * STRIP, (i + 1) * STRIP)
        high, low = split(gauss(pts_col[strip, :], own, dims))
        basis_h[strip, :] = high
        basis_l[strip, :] = low
    copies[1].wait()
    value = rhs[...]
    message[:rows, :] = dot3(value, basis_h[...], basis_l[...])
    message[rows : rows + 8, :] = to_rows([row_sum(value * value)], chosen.shape[1])
    copies[3].wait()
    copies[5].wait()
    params[...] = column_state([inverse, shift, jnp.broadcast_to(noise[...], (8, 1))])
    number = lax.axis_index("leaf") * anchors + lax.axis_index("sub")
    rank = keep.shape[1]
    slot = 0
    for base, bits in stages:
        for level in range(1, bits + 1):
            depth = base + level
            swap = (number >> (depth - 1)) & 1
            for p in range(1 << (bits - level)):
                heap = (1 << (total - depth)) - 1 + ((number >> depth) ^ p)
                row_chosen = keep[pl.ds(heap, 1), :]
                other = jnp.where(row_chosen < rank, row_chosen + rank, row_chosen - rank)
                chosen_out[slot : slot + 1, :] = jnp.where(swap == 1, other, row_chosen)
                slot += 1


def part_offsets(size, first, last):
    offsets = [0]
    for i in range(first, last):
        offsets.append(offsets[-1] + size - i * BLOCK)
    return offsets


def near_blocks(value, parts):
    rows, size = value.shape
    vh, vl = split(value)
    both = jnp.concatenate([vh, vl], axis=0)
    sums = [None] * (size // BLOCK)

    def three(cut, high, low, dims):
        wide = lax.dot_general(both[:, cut], high, dims, preferred_element_type=F32)
        thin = lax.dot_general(vh[:, cut], low, dims, preferred_element_type=F32)
        return wide[:rows] + wide[rows:] + thin

    def add(j, term):
        sums[j] = term if sums[j] is None else sums[j] + term

    for first, last, high, low in parts:
        offsets = part_offsets(size, first, last)
        for i in range(first, last):
            start, stop = offsets[i - first], offsets[i - first + 1]
            cut = slice(i * BLOCK, (i + 1) * BLOCK)
            out = three(cut, high[:, start:stop], low[:, start:stop], NN)
            for j in range(i, size // BLOCK):
                add(j, out[:, (j - i) * BLOCK : (j - i + 1) * BLOCK])
            if i + 1 < size // BLOCK:
                start += BLOCK
                add(i, three(slice((i + 1) * BLOCK, size), high[:, start:stop], low[:, start:stop], NT))
    zero = jnp.zeros((rows, BLOCK), F32)
    return jnp.concatenate([zero if s is None else s for s in sums], axis=1)


def dense_kernel(dims, first, last, more, *refs):
    pts_row, rhs = refs[:2]
    before, params = (refs[2], refs[3]) if more else (None, None)
    high, low, near, pts_col = refs[-4:]
    size = pts_row.shape[1]
    offsets = part_offsets(size, first, last)
    pts_col[...] = pts_row[...].T
    for i in range(first, last):
        start = offsets[i - first]

        def body(k, carry):
            strip = pl.ds(pl.multiple_of(k * STRIP, STRIP), STRIP)
            left = pts_col[pl.ds(pl.multiple_of(i * BLOCK + k * STRIP, STRIP), STRIP), :]
            for j in range(i, size // BLOCK):
                right = pts_row[:, j * BLOCK : (j + 1) * BLOCK]
                h, l = split(gauss(left, right, dims))
                part = slice(start + (j - i) * BLOCK, start + (j - i + 1) * BLOCK)
                high[strip, part] = h
                low[strip, part] = l
            return carry

        lax.fori_loop(0, BLOCK // STRIP, body, 0)
    value = rhs[...]
    out = near_blocks(value, [(first, last, high, low)])
    if more:
        out = out + before[...] + params[0:1, 2:3] * value
    near[...] = out


def levels_of(count):
    return count.bit_length() - 1


def tree_slots(count):
    slots = {}
    for level in range(1, levels_of(count) + 1):
        for p in range(count >> level):
            slots[level, p] = len(slots)
    return slots


def sweep_up(weights, transfer, couple, top):
    count = len(weights)
    slots = tree_slots(count)
    own_terms = []
    energy = None
    for level in range(1, levels_of(count) + 1):
        parents = []
        for p in range(count >> level):
            slot = slots[level, p]
            first, second = weights[2 * p], weights[2 * p + 1]
            crossed = dot3(second, couple[0][slot], couple[1][slot])
            term = row_sum(first * crossed)
            energy = term if energy is None else energy + term
            if p == 0:
                own_terms.append(crossed)
            if level < levels_of(count) or top:
                joined = jnp.concatenate([first, second], axis=1)
                parents.append(dot3(joined, transfer[0][slot], transfer[1][slot]))
        weights = parents
    return weights, own_terms, 2.0 * energy


def sweep_down(search, own_terms, transfer, count):
    slots = tree_slots(count)
    for level in range(levels_of(count), 0, -1):
        own = own_terms[level - 1]
        if search is not None:
            slot = slots[level, 0]
            half = own.shape[1]
            own = own + dot3(search, transfer[0][slot, :half], transfer[1][slot, :half], NT)
        search = own
    return search


def build_tree(dims, coords, chosen, params, transfer, couple, top):
    count = len(coords)
    slots = tree_slots(count)
    rank = coords[0].shape[1]
    inverse, shift = params[:, 0:1], params[:, 1:2]
    scaled = [(c - shift) * inverse for c in coords]
    for level in range(1, levels_of(count) + 1):
        parents, parents_scaled = [], []
        for p in range(count >> level):
            slot = slots[level, p]
            columns = scaled[2 * p].T, scaled[2 * p + 1].T
            for i in range(rank // STRIP):
                strip = slice(i * STRIP, (i + 1) * STRIP)
                high, low = split(gauss(columns[1][strip, :], scaled[2 * p], dims))
                couple[0][slot, strip, :] = high
                couple[1][slot, strip, :] = low
            if level == levels_of(count) and not top:
                continue
            joined = jnp.concatenate([coords[2 * p], coords[2 * p + 1]], axis=1)
            parent = pick(joined, chosen[slot : slot + 1, :])
            parent_scaled = (parent - shift) * inverse
            for side, column in enumerate(columns):
                for i in range(rank // STRIP):
                    strip = slice(i * STRIP, (i + 1) * STRIP)
                    target = slice(side * rank + i * STRIP, side * rank + (i + 1) * STRIP)
                    high, low = split(gauss(column[strip, :], parent_scaled, dims))
                    transfer[0][slot, target, :] = high
                    transfer[1][slot, target, :] = low
            parents.append(parent)
            parents_scaled.append(parent_scaled)
        coords, scaled = parents, parents_scaled
    return coords


def add_rows(messages, rows):
    total = messages[0][rows : rows + 8, :]
    for message in messages[1:]:
        total = total + message[rows : rows + 8, :]
    return total


def lower_first_kernel(dims, rows, count, offset, refs):
    messages = refs[:count]
    params, chosen = refs[count : count + 2]
    message, terms, transfer_h, transfer_l, couple_h, couple_l = refs[-6:]
    transfer, couple = (transfer_h, transfer_l), (couple_h, couple_l)
    coords = [m[rows + 8 :, :] for m in messages]
    picks = chosen[offset : offset + count - 1, :]
    coords = build_tree(dims, coords, picks, params, transfer, couple, True)
    lower_finish(rows, messages, message, terms, transfer, couple, True)
    message[rows + 8 :, :] = coords[0]


def lower_finish(rows, messages, message, terms, transfer, couple, top):
    weights, own_terms, energy = sweep_up([m[:rows, :] for m in messages], transfer, couple, top)
    for i, term in enumerate(own_terms):
        terms[i] = term
    dots = add_rows(messages, rows)
    message[:rows, :] = weights[0]
    extra = to_rows([jnp.zeros_like(energy)] * 7 + [energy], dots.shape[1])
    message[rows : rows + 8, :] = dots + extra


def lower_kernel(rows, count, top, refs):
    messages = refs[:count]
    transfer_h, transfer_l, couple_h, couple_l = refs[count : count + 4]
    message, terms = refs[count + 4 :]
    lower_finish(
        rows, messages, message, terms, (transfer_h, transfer_l), (couple_h, couple_l), top
    )


def upper_build(dims, rows, count, offset, refs):
    messages = refs[:count]
    params, chosen, transfer_h, transfer_l, couple_h, couple_l = refs[count:]
    coords = [m[rows + 8 :, :] for m in messages]
    picks = chosen[offset : offset + count - 1, :]
    build_tree(
        dims, coords, picks, params, (transfer_h, transfer_l), (couple_h, couple_l), False
    )


def far_field(rows, messages, upper, lower):
    count = len(messages)
    weights = [m[:rows, :] for m in messages]
    _, own_terms, energy = sweep_up(weights, upper[:2], upper[2:], False)
    search = sweep_down(None, own_terms, upper[:2], count)
    for terms, high, low in reversed(lower):
        depth = terms.shape[0]
        own_terms = [terms[i] for i in range(depth)]
        search = sweep_down(search, own_terms, (high, low), 1 << depth)
    sums = to_columns(add_rows(messages, rows), rows)
    return search, sums, sums[:, 7:8] + energy


def near_field(value, params, parts):
    return params[0:1, 2:3] * value + near_blocks(value, parts)


def column_state(columns):
    rows = columns[0].shape[0]
    lane = lax.broadcasted_iota(jnp.int32, (rows, 128), 1)
    block = jnp.zeros((rows, 128), F32)
    for i, column in enumerate(columns):
        block = jnp.where(lane == i, column, block)
    return block


def take_refs(refs, *sizes):
    groups = []
    position = 0
    for size in sizes:
        groups.append(refs[position : position + size])
        position += size
    groups.append(refs[position:])
    return groups


def open_refs(rows, count, stages, refs):
    messages, lower, upper, basis, rest = take_refs(refs, count, 3 * stages, 4, 2)
    lower = [lower[i : i + 3] for i in range(0, 3 * stages, 3)]
    return far_field(rows, messages, upper, lower), basis, rest


def dense_parts(cuts, refs):
    return [(*cut, refs[2 * i], refs[2 * i + 1]) for i, cut in enumerate(cuts)]


def first_kernel(rows, count, stages, cuts, refs):
    (search, sums, far), basis, rest = open_refs(rows, count, stages, refs)
    dense, rest = take_refs(rest, 2 * len(cuts))
    params, rhs, near_in, message, q_out, near_out, state = rest
    norm = sums[:, 0:1]
    rate = norm / (params[0:1, 2:3] * norm + jnp.abs(far))
    q = rate * (near_in[...] + dot3(search, basis[0][...], basis[1][...], NT))
    q_out[...] = q
    message[:rows, :] = dot3(q, basis[0][...], basis[1][...])
    near_q = near_field(q, params, dense_parts(cuts, dense))
    near_out[...] = near_q
    dots = [row_sum(rhs[...] * q), row_sum(q * q), row_sum(q * near_q)]
    message[rows:, :] = to_rows(dots, message.shape[1])
    state[...] = column_state([norm, rate])


def second_kernel(rows, count, stages, cuts, refs):
    (search, sums, far), basis, rest = open_refs(rows, count, stages, refs)
    dense, rest = take_refs(rest, 2 * len(cuts))
    params, rhs, q_in, near_in, state_in = rest[:5]
    message, x_out, r_out, d_out, q_out, near_out, state = rest[5:]
    norm0, rate = state_in[:, 0:1], state_in[:, 1:2]
    bq, qq, qaq = sums[:, 0:1], sums[:, 1:2], sums[:, 2:3] + far
    step = norm0 / bq
    alpha0 = step * rate
    norm1 = step * step * qq - norm0
    beta = norm1 / norm0
    back = 1.0 / rate
    rhs_v, q = rhs[...], q_in[...]
    r1 = rhs_v - step * q
    d1 = r1 + beta * rhs_v
    q0 = back * q
    aq = near_in[...] + dot3(search, basis[0][...], basis[1][...], NT)
    q1 = (1.0 + beta) * q0 - step * aq
    rar = back * (bq - 2.0 * step * qq) + step * step * qaq
    cross = back * (bq - step * qq)
    curve = rar + 2.0 * beta * cross + beta * beta * (back * bq)
    alpha1 = norm1 / curve
    x_out[...] = alpha0 * rhs_v + alpha1 * d1
    r2 = r1 - alpha1 * q1
    r_out[...] = r2
    d_out[...] = d1
    q_out[...] = q1
    message[:rows, :] = dot3(r2, basis[0][...], basis[1][...])
    near = near_field(r2, params, dense_parts(cuts, dense))
    near_out[...] = near
    dots = [row_sum(r2 * r2), row_sum(r2 * q1), row_sum(r2 * near)]
    message[rows:, :] = to_rows(dots, message.shape[1])
    state[...] = column_state([norm1, curve])


def last_kernel(rows, count, stages, refs):
    (search, sums, far), basis, rest = open_refs(rows, count, stages, refs)
    x_in, r_in, d_in, q_in, near_in, state_in, x_out, r_out = rest
    norm1, curve1 = state_in[:, 0:1], state_in[:, 1:2]
    norm2, cross, rar = sums[:, 0:1], sums[:, 1:2], sums[:, 2:3] + far
    beta = norm2 / norm1
    curve = rar + 2.0 * beta * cross + beta * beta * curve1
    alpha = norm2 / curve
    image = near_in[...] + dot3(search, basis[0][...], basis[1][...], NT) + beta * q_in[...]
    r2 = r_in[...]
    x_out[...] = x_in[...] + alpha * (r2 + beta * d_in[...])
    r_out[...] = r2 - alpha * image


def gather(value, stage):
    axis, shift, bits = stage
    size = lax.axis_size(axis)
    pairs = [[(i, i ^ (s << shift)) for i in range(size)] for s in range(1, 1 << bits)]
    return [value] + [lax.ppermute(value, axis, pair) for pair in pairs]


def refs_of(kernel, *args):
    return lambda *refs: kernel(*args, refs)


def body(points, targets, leaf_skel, node_keep, lengthscales, noise_var):
    dims, size = points.shape
    rows = targets.shape[0]
    rank = leaf_skel.shape[1]
    subs = lax.axis_size("sub")
    stages = []
    total = 0
    for axis in ("sub", "leaf"):
        axis_bits = levels_of(lax.axis_size(axis))
        for shift in range(0, axis_bits, 3):
            bits = min(3, axis_bits - shift)
            stages.append((total + shift, axis, shift, bits))
        total += axis_bits
    bases = tuple((base, bits) for base, _, _, bits in stages)
    hops = [stage[1:] for stage in stages]
    counts = [1 << bits for _, bits in bases]
    slots = sum(counts) - len(counts)
    offsets = [sum(counts[:i]) - i for i in range(len(counts))]
    stage_count = len(stages) - 1

    message, rhs, pts_row, basis_h, basis_l, chosen, params = call(
        functools.partial(setup_kernel, bases, total, subs),
        [
            f32_shape(rows + 16, rank),
            f32_shape(rows, size),
            f32_shape(8, size),
            bf16_shape(size, rank),
            bf16_shape(size, rank),
            jax.ShapeDtypeStruct((slots, rank), jnp.int32),
            f32_shape(8, 128),
        ],
        [
            points,
            targets,
            leaf_skel,
            node_keep,
            jnp.reshape(lengthscales, (1, dims)),
            jnp.reshape(noise_var, (1, 1)),
        ],
        anywhere=range(6),
        scratch=[
            pltpu.VMEM((dims, size), F32),
            pltpu.VMEM((1, rank), jnp.int32),
            pltpu.VMEM(node_keep.shape, jnp.int32),
            pltpu.VMEM((1, dims), F32),
            pltpu.VMEM((1, 1), F32),
            pltpu.VMEM((size, 8), F32),
            pltpu.SemaphoreType.DMA((6,)),
        ],
        name="setup",
    )
    basis = [basis_h, basis_l]

    def tree_shapes(count):
        nodes = count - 1
        return [bf16_shape(nodes, 2 * rank, rank)] * 2 + [bf16_shape(nodes, rank, rank)] * 2

    blocks = size // BLOCK
    cuts = [(0, blocks // 4), (blocks // 4, blocks)]
    dense = []

    def build_dense(cut, extra):
        width = part_offsets(size, *cut)[-1]
        high, low, near = call(
            functools.partial(dense_kernel, dims, *cut, len(extra) > 1),
            [bf16_shape(BLOCK, width), bf16_shape(BLOCK, width), f32_shape(rows, size)],
            [pts_row, rhs] + extra,
            scratch=[pltpu.VMEM((size, 8), F32)],
            cost=(12 * rows * BLOCK * width, BLOCK * width),
            name="dense",
        )
        dense.extend([high, low])
        return near

    trees = []
    terms_all = []
    near = None
    for i in range(stage_count):
        messages = gather(message, hops[i])
        extra = []
        if i == 0:
            near = build_dense(cuts[0], [])
            extra = [near]
        message, terms, *tree = call(
            refs_of(lower_first_kernel, dims, rows, counts[i], offsets[i]),
            [f32_shape(rows + 16, rank), f32_shape(bases[i][1], rows, rank)]
            + tree_shapes(counts[i]),
            messages + [params, chosen] + extra,
            name="lower_first",
        )
        trees.append(tree)
        terms_all.append(terms)
    messages = gather(message, hops[-1])
    near = build_dense(cuts[1], [near, params, message])
    upper = call(
        refs_of(upper_build, dims, rows, counts[-1], offsets[-1]),
        tree_shapes(counts[-1]),
        messages + [params, chosen],
        name="upper_build",
    )

    state_shape = f32_shape(rows, 128)
    vector = f32_shape(rows, size)
    message_shape = f32_shape(rows + 8, rank)

    def lower_of(terms_all):
        return [a for terms, tree in zip(terms_all, trees) for a in (terms, tree[0], tree[1])]

    def exchange(message):
        terms_all = []
        for i in range(stage_count):
            messages = gather(message, hops[i])
            message, terms = call(
                refs_of(lower_kernel, rows, counts[i], True),
                [message_shape, f32_shape(bases[i][1], rows, rank)],
                messages + trees[i],
                name="lower",
            )
            terms_all.append(terms)
        return gather(message, hops[-1]) + lower_of(terms_all)

    fixed = (rows, counts[-1], stage_count)
    message, q, near, state = call(
        refs_of(first_kernel, *fixed, cuts),
        [message_shape, vector, vector, state_shape],
        messages + lower_of(terms_all) + upper + basis + dense + [params, rhs, near],
        name="first",
    )
    arrived = exchange(message)
    message, x, r, d, q, near, state = call(
        refs_of(second_kernel, *fixed, cuts),
        [message_shape, vector, vector, vector, vector, vector, state_shape],
        arrived + upper + basis + dense + [params, rhs, q, near, state],
        name="second",
    )
    arrived = exchange(message)
    return tuple(
        call(
            refs_of(last_kernel, *fixed),
            [vector, vector],
            arrived + upper + basis + [x, r, d, q, near, state],
            name="last",
        )
    )


def solution(mesh):
    in_specs = (
        P(None, ("parts", "leaf", "sub")),
        P(None, ("parts", "leaf", "sub")),
        P(("parts", "leaf", "sub"), None),
        P("parts", None),
        P("parts"),
        P("parts"),
    )
    out_specs = (P(None, ("parts", "leaf", "sub")), P(None, ("parts", "leaf", "sub")))
    return jax.shard_map(body, mesh=mesh, in_specs=in_specs, out_specs=out_specs, check_vma=False)
```

time: 643 us -> 84.2 us (0.13); the launches traced: 633 us -> 83.9 us
  matrix products: 362 us -> 0 us
  blocking collectives: 150 us -> 0 us
  local copies, waits for them, and re-layouts: 53.5 us -> 3.92 us
  Pallas kernels: 0 us -> 39.3 us
  loops' own time: 17.4 us -> 0 us
  waiting for transfers between devices: 35.5 us -> 18.9 us
  starting transfers between devices: 8.43 us -> 20.4 us
    dot_general x63 -> x0, matrix products: 362 us -> none  [product(): jnp.dot(first, second, precision=lax.Precision.HIGHEST, preferred_element...]
    psum x5 -> x0, blocking collectives: 150 us -> none  [the longest x2 59 us: body(): curve = lax.psum(jnp.sum(direction * image, axis=1), ('leaf', 'sub'))]
    pallas_call x0 -> x10, Pallas kernels: none -> 39.3 us  [call(): pl.pallas_call(kernel, out_shape=list(out_shape), in_specs=[ANY if i in a...]
    slice x111 -> x0, local copies, waits for them, and re-layouts: 24.4 us -> none  [the longest x25 16.8 us: kernel(): inverse_scale[axis_number]]
    another operation x3 -> x0, loops' own time: 17.4 us -> none  [body(): pieces = lax.map(one_block, jnp.arange(blocks))]
    ppermute x12 -> x18, waiting for transfers between devices: 35.5 us -> 18.9 us  [gather(): return [value] + [lax.ppermute(value, axis, pair) for pair in pairs]]
    dynamic_slice x25 -> x0, local copies, waits for them, and re-layouts: 16.2 us -> none  [the longest x24 15.3 us: body(): pieces = lax.map(one_block, jnp.arange(blocks))]
    ppermute x12 -> x18, starting transfers between devices: 8.43 us -> 20.4 us  [gather(): return [value] + [lax.ppermute(value, axis, pair) for pair in pairs]]
  transfers between devices with their start and end apart: 12 -> 18, of which waited for: 9 -> 8; matrix products, arithmetic and copies ran while one was open for 32% -> 0% of each run, Pallas kernels for 0% -> 16%
where the time goes in v1:
time: 84.2 us; the launch traced here: 83.9 us
  Pallas kernels  39.3 us (47%)
  starting transfers between devices  20.4 us (24%)
  waiting for transfers between devices  18.9 us (22%)
  local copies, waits for them, and re-layouts  3.92 us (5%)
  between operations  1.41 us (2%)
    pallas_call x10, Pallas kernels, call(): pl.pallas_call(kernel, out_shape=list(out_shape), in_specs=[ANY if i in a...  39.3 us
    ppermute x18, starting transfers between devices, gather(): return [value] + [lax.ppermute(value, axis, pair) for pair in pairs]  20.4 us
    ppermute x18, waiting for transfers between devices, gather(): return [value] + [lax.ppermute(value, axis, pair) for pair in pairs]  18.9 us
    unnamed x10, local copies, waits for them, and re-layouts  3.92 us
  transfers between devices with their start and end apart: 18, of which 8 were waited for; matrix products, arithmetic and copies ran while one was open for 0% of the time, Pallas kernels for 16%

profile of v1, /device:TPU:0, one launch (start us, length us, event | category | flops | bytes accessed | tf_op | source)
XLA Modules:
  0.0 83.9 jit_solution(898257369041773541)
XLA Ops:
  1.3 1.0 %copy-done = f32[64,2048]{1,0:T(8,128)S(1)} copy-done((f32[64,2048]{1,0:T(8,128)S(1)}, f32[64,2048]{1,0:T(8,128)}, u32[]{:S(2)}) %copy-start) | copy-done | bytes 524312
  5.2 3.6 %setup.1 = (f32[80,256]{1,0:T(8,128)S(1)}, f32[64,2048]{1,0:T(8,128)S(1)}, f32[8,2048]{1,0:T(8,128)S(1)}, bf16[2048,256]{1,0:T(8,128)(2,1)S(1)}, bf16[2048,256]{...) custom-call(f32[6,2048]{1,0:T(8,128)S(1)} %copy-done.1, f32[64,2048]{1,0:T(8,128)S(1)} %copy-done, ...), custom_call_target="tpu_custom_call" | custom-call | tf_op jit(solution)/shard_map/setup/pallas_call | solution.py:27
  8.8 2.4 %collective-permute-start.2 = (f32[80,256]{1,0:T(8,128)S(1)}, f32[80,256]{1,0:T(8,128)S(1)}, u32[]{:S(2)}, u32[]{:S(2)}) collective-permute-start(f32[80,256]{1,0:T(8,128)S(1)} %get-tuple-element.40.refs_0_), channel_id=1, source_target_pairs={{0,3},{1,2},{2,1},{3,0},{4,7},{5,6},{6,5},{7,4},{8,11},{9,10},{10,... | collective-permute-start | bytes 245768 | tf_op jit(solution)/shard_map/ppermute | solution.py:470
  11.9 5.5 %dense.2 = (bf16[256,3840]{1,0:T(8,128)(2,1)S(1)}, bf16[256,3840]{1,0:T(8,128)(2,1)S(1)}, f32[64,2048]{1,0:T(8,128)S(1)}) custom-call(f32[8,2048]{1,0:T(8,128)S(1)} %get-tuple-element.43.refs_0_, f32[64,2048]{1,0:T(8,128)S(1)} %get-tuple-element.44.refs_1_.refs_18_), custom_call_target="tpu_custom_call" | custom-call | flops 754974720 | bytes 5046272 | tf_op jit(solution)/shard_map/dense/pallas_call | solution.py:27
  17.5 2.9 %lower_first.1 = (f32[80,256]{1,0:T(8,128)S(1)}, f32[2,64,256]{2,1,0:T(8,128)S(1)}, bf16[3,512,256]{2,1,0:T(8,128)(2,1)S(1)}, bf16[3,512,256]{2,1,0:T(8,128)(2,1...) custom-call(f32[80,256]{1,0:T(8,128)S(1)} %get-tuple-element.40.refs_0_, ...), custom_call_target="tpu_custom_call" | custom-call | tf_op jit(solution)/shard_map/lower_first/pallas_call | solution.py:27
  20.3 3.9 %collective-permute-start.5 = (f32[80,256]{1,0:T(8,128)S(1)}, f32[80,256]{1,0:T(8,128)S(1)}, u32[]{:S(2)}, u32[]{:S(2)}) collective-permute-start(f32[80,256]{1,0:T(8,128)S(1)} %get-tuple-element.46.refs_0_.refs_4_), channel_id=1, source_target_pairs={{0,12},{4,8},{8,4},{12,0},{1,13},{5,9},{9,5},{13,1},{2,14},{6,10},... | collective-permute-start | bytes 245768 | tf_op jit(solution)/shard_map/ppermute | solution.py:470
  24.9 7.9 %dense.3 = (bf16[256,5376]{1,0:T(8,128)(2,1)S(1)}, bf16[256,5376]{1,0:T(8,128)(2,1)S(1)}, f32[64,2048]{1,0:T(8,128)S(1)}) custom-call(f32[8,2048]{1,0:T(8,128)S(1)} %get-tuple-element.43.refs_0_, f32[64,2048]{1,0:T(8,128)S(1)} %get-tuple-element.44.refs_1_.refs_18_, f32[64,2048]{1,0:T(8,128)S(1)} %get-tuple-element.45.refs_6_.refs_2_, ...), custom_call_target="tpu_custom_call" | custom-call | flops 1056964608 | bytes 7229440 | tf_op jit(solution)/shard_map/dense/pallas_call | solution.py:27
  32.9 2.1 %upper_build.1 = (bf16[3,512,256]{2,1,0:T(8,128)(2,1)S(1)}, bf16[3,512,256]{2,1,0:T(8,128)(2,1)S(1)}, bf16[3,256,256]{2,1,0:T(8,128)(2,1)S(1)}, bf16[3,256,256]{2,1,0:T(8,128)(2,1)S(1)}) custom-call(f32[80,256]{1,0:T(8,128)S(1)} %get-tuple-element.46.refs_0_.refs_4_, f32[80,256]{1,0:T(8,128)S(1)} %collective-permute-done.3.refs_1_, ...), custom_call_target="tpu_custom_call" | custom-call | tf_op jit(solution)/shard_map/upper_build/pallas_call | solution.py:27
  34.9 6.5 %first.1 = (f32[72,256]{1,0:T(8,128)S(1)}, f32[64,2048]{1,0:T(8,128)S(1)}, f32[64,2048]{1,0:T(8,128)S(1)}, f32[64,128]{1,0:T(8,128)S(1)}) custom-call(f32[80,256]{1,0:T(8,128)S(1)} %get-tuple-element.46.refs_0_.refs_4_, f32[80,256]{1,0:T(8,128)S(1)} %collective-permute-done.3.refs_1_, f32[80,256]{1,0:T(8,128)S(1)} %collective-permute-done.4.refs_2_, ...), custom_call_target="tpu_custom_call" | custom-call | tf_op jit(solution)/shard_map/first/pallas_call | solution.py:27
  42.1 1.1 %collective-permute-start.7 = (f32[72,256]{1,0:T(8,128)S(1)}, f32[72,256]{1,0:T(8,128)S(1)}, u32[]{:S(2)}, u32[]{:S(2)}) collective-permute-start(f32[72,256]{1,0:T(8,128)S(1)} %get-tuple-element.61.refs_0_), channel_id=1, source_target_pairs={{0,2},{1,3},{2,0},{3,1},{4,6},{5,7},{6,4},{7,5},{8,10},{9,11},{10,... | collective-permute-start | bytes 221192 | tf_op jit(solution)/shard_map/ppermute | solution.py:470
  43.3 2.5 %collective-permute-done.8.refs_3_ = f32[72,256]{1,0:T(8,128)S(1)} collective-permute-done((f32[72,256]{1,0:T(8,128)S(1)}, f32[72,256]{1,0:T(8,128)S(1)}, u32[]{:S(2)}, u32[]{:S(2)}) %collective-permute-start.8) | collective-permute-done | bytes 73760 | tf_op jit(solution)/shard_map/ppermute | solution.py:470
  45.8 1.8 %collective-permute-done.7.refs_2_ = f32[72,256]{1,0:T(8,128)S(1)} collective-permute-done((f32[72,256]{1,0:T(8,128)S(1)}, f32[72,256]{1,0:T(8,128)S(1)}, u32[]{:S(2)}, u32[]{:S(2)}) %collective-permute-start.7) | collective-permute-done | bytes 73760 | tf_op jit(solution)/shard_map/ppermute | solution.py:470
  48.4 3.8 %collective-permute-start.11 = (f32[72,256]{1,0:T(8,128)S(1)}, f32[72,256]{1,0:T(8,128)S(1)}, u32[]{:S(2)}, u32[]{:S(2)}) collective-permute-start(f32[72,256]{1,0:T(8,128)S(1)} %get-tuple-element.64.refs_0_), channel_id=1, source_target_pairs={{0,12},{4,8},{8,4},{12,0},{1,13},{5,9},{9,5},{13,1},{2,14},{6,10},... | collective-permute-start | bytes 221192 | tf_op jit(solution)/shard_map/ppermute | solution.py:470
  52.8 2.6 %collective-permute-done.11.refs_3_ = f32[72,256]{1,0:T(8,128)S(1)} collective-permute-done((f32[72,256]{1,0:T(8,128)S(1)}, f32[72,256]{1,0:T(8,128)S(1)}, u32[]{:S(2)}, u32[]{:S(2)}) %collective-permute-start.11) | collective-permute-done | bytes 73760 | tf_op jit(solution)/shard_map/ppermute | solution.py:470
  55.5 2.9 %collective-permute-done.10.refs_2_ = f32[72,256]{1,0:T(8,128)S(1)} collective-permute-done((f32[72,256]{1,0:T(8,128)S(1)}, f32[72,256]{1,0:T(8,128)S(1)}, u32[]{:S(2)}, u32[]{:S(2)}) %collective-permute-start.10) | collective-permute-done | bytes 73760 | tf_op jit(solution)/shard_map/ppermute | solution.py:470
  58.4 6.7 %second.1 = (f32[72,256]{1,0:T(8,128)S(1)}, f32[64,2048]{1,0:T(8,128)S(1)}, f32[64,2048]{1,0:T(8,128)S(1)}, f32[64,2048]{1,0:T(8,128)S(1)}, f32[64,2048]{1,0:T(8...) custom-call(f32[72,256]{1,0:T(8,128)S(1)} %get-tuple-element.64.refs_0_, ...), custom_call_target="tpu_custom_call" | custom-call | tf_op jit(solution)/shard_map/second/pallas_call | solution.py:27
  65.1 1.3 %collective-permute-start.13 = (f32[72,256]{1,0:T(8,128)S(1)}, f32[72,256]{1,0:T(8,128)S(1)}, u32[]{:S(2)}, u32[]{:S(2)}) collective-permute-start(f32[72,256]{1,0:T(8,128)S(1)} %get-tuple-element.69.refs_0_), channel_id=1, source_target_pairs={{0,2},{1,3},{2,0},{3,1},{4,6},{5,7},{6,4},{7,5},{8,10},{9,11},{10,... | collective-permute-start | bytes 221192 | tf_op jit(solution)/shard_map/ppermute | solution.py:470
  66.9 2.7 %collective-permute-done.14.refs_3_ = f32[72,256]{1,0:T(8,128)S(1)} collective-permute-done((f32[72,256]{1,0:T(8,128)S(1)}, f32[72,256]{1,0:T(8,128)S(1)}, u32[]{:S(2)}, u32[]{:S(2)}) %collective-permute-start.14) | collective-permute-done | bytes 73760 | tf_op jit(solution)/shard_map/ppermute | solution.py:470
  69.6 1.5 %collective-permute-done.13.refs_2_ = f32[72,256]{1,0:T(8,128)S(1)} collective-permute-done((f32[72,256]{1,0:T(8,128)S(1)}, f32[72,256]{1,0:T(8,128)S(1)}, u32[]{:S(2)}, u32[]{:S(2)}) %collective-permute-start.13) | collective-permute-done | bytes 73760 | tf_op jit(solution)/shard_map/ppermute | solution.py:470
  71.9 1.9 %collective-permute-start.17 = (f32[72,256]{1,0:T(8,128)S(1)}, f32[72,256]{1,0:T(8,128)S(1)}, u32[]{:S(2)}, u32[]{:S(2)}) collective-permute-start(f32[72,256]{1,0:T(8,128)S(1)} %get-tuple-element.70.refs_0_), channel_id=1, source_target_pairs={{0,12},{4,8},{8,4},{12,0},{1,13},{5,9},{9,5},{13,1},{2,14},{6,10},... | collective-permute-start | bytes 221192 | tf_op jit(solution)/shard_map/ppermute | solution.py:470
  73.8 2.5 %collective-permute-start.15 = (f32[72,256]{1,0:T(8,128)S(1)}, f32[72,256]{1,0:T(8,128)S(1)}, u32[]{:S(2)}, u32[]{:S(2)}) collective-permute-start(f32[72,256]{1,0:T(8,128)S(1)} %get-tuple-element.70.refs_0_), channel_id=1, source_target_pairs={{0,4},{4,0},{8,12},{12,8},{1,5},{5,1},{9,13},{13,9},{2,6},{6,2},{1... | collective-permute-start | bytes 221192 | tf_op jit(solution)/shard_map/ppermute | solution.py:470
  76.3 2.6 %collective-permute-done.17.refs_3_ = f32[72,256]{1,0:T(8,128)S(1)} collective-permute-done((f32[72,256]{1,0:T(8,128)S(1)}, f32[72,256]{1,0:T(8,128)S(1)}, u32[]{:S(2)}, u32[]{:S(2)}) %collective-permute-start.17) | collective-permute-done | bytes 73760 | tf_op jit(solution)/shard_map/ppermute | solution.py:470
  78.9 2.3 %collective-permute-done.16.refs_2_ = f32[72,256]{1,0:T(8,128)S(1)} collective-permute-done((f32[72,256]{1,0:T(8,128)S(1)}, f32[72,256]{1,0:T(8,128)S(1)}, u32[]{:S(2)}, u32[]{:S(2)}) %collective-permute-start.16) | collective-permute-done | bytes 73760 | tf_op jit(solution)/shard_map/ppermute | solution.py:470
  81.2 2.7 %last.1 = (f32[64,2048]{1,0:T(8,128)}, f32[64,2048]{1,0:T(8,128)}) custom-call(f32[72,256]{1,0:T(8,128)S(1)} %get-tuple-element.70.refs_0_, f32[72,256]{1,0:T(8,128)S(1)} %collective-permute-done.15.refs_1_, f32[72,256]{1,0:T(8,128)S(1)} %collective-permute-done.16.refs_2_, f32[72,256]{1,0:T(8,128)S(1)} %collective-permute-done.17.refs_3_, ...), custom_call_target="tpu_custom_call" | custom-call | tf_op jit(solution)/shard_map/last/pallas_call | solution.py:27
  (32 shorter events, 7.8 us)
Async XLA Ops:
  1.3 1.0 %copy-start = (f32[64,2048]{1,0:T(8,128)S(1)}, f32[64,2048]{1,0:T(8,128)}, u32[]{:S(2)}) copy-start(f32[64,2048]{1,0:T(8,128)} %refs_1_.1) | copy-start | bytes 1572868
  2.3 0.8 %copy-start.1 = (f32[6,2048]{1,0:T(8,128)S(1)}, f32[6,2048]{1,0:T(8,128)}, u32[]{:S(2)}) copy-start(f32[6,2048]{1,0:T(8,128)} %refs_0_.1) | copy-start | bytes 147460
  3.2 0.7 copy-start.2
  3.9 0.7 copy-start.3
  4.6 0.7 copy-start.4
  8.8 8.7 %collective-permute-start.2 = (f32[80,256]{1,0:T(8,128)S(1)}, f32[80,256]{1,0:T(8,128)S(1)}, u32[]{:S(2)}, u32[]{:S(2)}) collective-permute-start(f32[80,256]{1,0:T(8,128)S(1)} %get-tuple-element.40.refs_0_), channel_id=1, source_target_pairs={{0,3},{1,2},{2,1},{3,0},{4,7},{5,6},{6,5},{7,4},{8,11},{9,10},{10,... | collective-permute-start | bytes 245768 | tf_op jit(solution)/shard_map/ppermute | solution.py:470
  11.2 6.2 %collective-permute-start.1 = (f32[80,256]{1,0:T(8,128)S(1)}, f32[80,256]{1,0:T(8,128)S(1)}, u32[]{:S(2)}, u32[]{:S(2)}) collective-permute-start(f32[80,256]{1,0:T(8,128)S(1)} %get-tuple-element.40.refs_0_), channel_id=1, source_target_pairs={{0,2},{1,3},{2,0},{3,1},{4,6},{5,7},{6,4},{7,5},{8,10},{9,11},{10,... | collective-permute-start | bytes 245768 | tf_op jit(solution)/shard_map/ppermute | solution.py:470
  11.9 5.6 %collective-permute-start = (f32[80,256]{1,0:T(8,128)S(1)}, f32[80,256]{1,0:T(8,128)S(1)}, u32[]{:S(2)}, u32[]{:S(2)}) collective-permute-start(f32[80,256]{1,0:T(8,128)S(1)} %get-tuple-element.40.refs_0_), channel_id=1, source_target_pairs={{0,1},{1,0},{2,3},{3,2},{4,5},{5,4},{6,7},{7,6},{8,9},{9,8},{10,11... | collective-permute-start | bytes 245768 | tf_op jit(solution)/shard_map/ppermute | solution.py:470
  20.3 12.5 %collective-permute-start.5 = (f32[80,256]{1,0:T(8,128)S(1)}, f32[80,256]{1,0:T(8,128)S(1)}, u32[]{:S(2)}, u32[]{:S(2)}) collective-permute-start(f32[80,256]{1,0:T(8,128)S(1)} %get-tuple-element.46.refs_0_.refs_4_), channel_id=1, source_target_pairs={{0,12},{4,8},{8,4},{12,0},{1,13},{5,9},{9,5},{13,1},{2,14},{6,10},... | collective-permute-start | bytes 245768 | tf_op jit(solution)/shard_map/ppermute | solution.py:470
  24.2 8.6 %collective-permute-start.4 = (f32[80,256]{1,0:T(8,128)S(1)}, f32[80,256]{1,0:T(8,128)S(1)}, u32[]{:S(2)}, u32[]{:S(2)}) collective-permute-start(f32[80,256]{1,0:T(8,128)S(1)} %get-tuple-element.46.refs_0_.refs_4_), channel_id=1, source_target_pairs={{0,8},{4,12},{8,0},{12,4},{1,9},{5,13},{9,1},{13,5},{2,10},{6,14},... | collective-permute-start | bytes 245768 | tf_op jit(solution)/shard_map/ppermute | solution.py:470
  24.2 8.6 %collective-permute-start.3 = (f32[80,256]{1,0:T(8,128)S(1)}, f32[80,256]{1,0:T(8,128)S(1)}, u32[]{:S(2)}, u32[]{:S(2)}) collective-permute-start(f32[80,256]{1,0:T(8,128)S(1)} %get-tuple-element.46.refs_0_.refs_4_), channel_id=1, source_target_pairs={{0,4},{4,0},{8,12},{12,8},{1,5},{5,1},{9,13},{13,9},{2,6},{6,2},{1... | collective-permute-start | bytes 245768 | tf_op jit(solution)/shard_map/ppermute | solution.py:470
  41.4 4.4 %collective-permute-start.8 = (f32[72,256]{1,0:T(8,128)S(1)}, f32[72,256]{1,0:T(8,128)S(1)}, u32[]{:S(2)}, u32[]{:S(2)}) collective-permute-start(f32[72,256]{1,0:T(8,128)S(1)} %get-tuple-element.61.refs_0_), channel_id=1, source_target_pairs={{0,3},{1,2},{2,1},{3,0},{4,7},{5,6},{6,5},{7,4},{8,11},{9,10},{10,... | collective-permute-start | bytes 221192 | tf_op jit(solution)/shard_map/ppermute | solution.py:470
  42.1 5.5 %collective-permute-start.7 = (f32[72,256]{1,0:T(8,128)S(1)}, f32[72,256]{1,0:T(8,128)S(1)}, u32[]{:S(2)}, u32[]{:S(2)}) collective-permute-start(f32[72,256]{1,0:T(8,128)S(1)} %get-tuple-element.61.refs_0_), channel_id=1, source_target_pairs={{0,2},{1,3},{2,0},{3,1},{4,6},{5,7},{6,4},{7,5},{8,10},{9,11},{10,... | collective-permute-start | bytes 221192 | tf_op jit(solution)/shard_map/ppermute | solution.py:470
  43.2 4.4 %collective-permute-start.6 = (f32[72,256]{1,0:T(8,128)S(1)}, f32[72,256]{1,0:T(8,128)S(1)}, u32[]{:S(2)}, u32[]{:S(2)}) collective-permute-start(f32[72,256]{1,0:T(8,128)S(1)} %get-tuple-element.61.refs_0_), channel_id=1, source_target_pairs={{0,1},{1,0},{2,3},{3,2},{4,5},{5,4},{6,7},{7,6},{8,9},{9,8},{10,11... | collective-permute-start | bytes 221192 | tf_op jit(solution)/shard_map/ppermute | solution.py:470
  48.4 7.1 %collective-permute-start.11 = (f32[72,256]{1,0:T(8,128)S(1)}, f32[72,256]{1,0:T(8,128)S(1)}, u32[]{:S(2)}, u32[]{:S(2)}) collective-permute-start(f32[72,256]{1,0:T(8,128)S(1)} %get-tuple-element.64.refs_0_), channel_id=1, source_target_pairs={{0,12},{4,8},{8,4},{12,0},{1,13},{5,9},{9,5},{13,1},{2,14},{6,10},... | collective-permute-start | bytes 221192 | tf_op jit(solution)/shard_map/ppermute | solution.py:470
  52.2 6.2 %collective-permute-start.10 = (f32[72,256]{1,0:T(8,128)S(1)}, f32[72,256]{1,0:T(8,128)S(1)}, u32[]{:S(2)}, u32[]{:S(2)}) collective-permute-start(f32[72,256]{1,0:T(8,128)S(1)} %get-tuple-element.64.refs_0_), channel_id=1, source_target_pairs={{0,8},{4,12},{8,0},{12,4},{1,9},{5,13},{9,1},{13,5},{2,10},{6,14},... | collective-permute-start | bytes 221192 | tf_op jit(solution)/shard_map/ppermute | solution.py:470
  52.2 6.2 %collective-permute-start.9 = (f32[72,256]{1,0:T(8,128)S(1)}, f32[72,256]{1,0:T(8,128)S(1)}, u32[]{:S(2)}, u32[]{:S(2)}) collective-permute-start(f32[72,256]{1,0:T(8,128)S(1)} %get-tuple-element.64.refs_0_), channel_id=1, source_target_pairs={{0,4},{4,0},{8,12},{12,8},{1,5},{5,1},{9,13},{13,9},{2,6},{6,2},{1... | collective-permute-start | bytes 221192 | tf_op jit(solution)/shard_map/ppermute | solution.py:470
  65.0 4.6 %collective-permute-start.14 = (f32[72,256]{1,0:T(8,128)S(1)}, f32[72,256]{1,0:T(8,128)S(1)}, u32[]{:S(2)}, u32[]{:S(2)}) collective-permute-start(f32[72,256]{1,0:T(8,128)S(1)} %get-tuple-element.69.refs_0_), channel_id=1, source_target_pairs={{0,3},{1,2},{2,1},{3,0},{4,7},{5,6},{6,5},{7,4},{8,11},{9,10},{10,... | collective-permute-start | bytes 221192 | tf_op jit(solution)/shard_map/ppermute | solution.py:470
  65.1 6.0 %collective-permute-start.13 = (f32[72,256]{1,0:T(8,128)S(1)}, f32[72,256]{1,0:T(8,128)S(1)}, u32[]{:S(2)}, u32[]{:S(2)}) collective-permute-start(f32[72,256]{1,0:T(8,128)S(1)} %get-tuple-element.69.refs_0_), channel_id=1, source_target_pairs={{0,2},{1,3},{2,0},{3,1},{4,6},{5,7},{6,4},{7,5},{8,10},{9,11},{10,... | collective-permute-start | bytes 221192 | tf_op jit(solution)/shard_map/ppermute | solution.py:470
  66.4 4.6 %collective-permute-start.12 = (f32[72,256]{1,0:T(8,128)S(1)}, f32[72,256]{1,0:T(8,128)S(1)}, u32[]{:S(2)}, u32[]{:S(2)}) collective-permute-start(f32[72,256]{1,0:T(8,128)S(1)} %get-tuple-element.69.refs_0_), channel_id=1, source_target_pairs={{0,1},{1,0},{2,3},{3,2},{4,5},{5,4},{6,7},{7,6},{8,9},{9,8},{10,11... | collective-permute-start | bytes 221192 | tf_op jit(solution)/shard_map/ppermute | solution.py:470
  71.9 7.0 %collective-permute-start.17 = (f32[72,256]{1,0:T(8,128)S(1)}, f32[72,256]{1,0:T(8,128)S(1)}, u32[]{:S(2)}, u32[]{:S(2)}) collective-permute-start(f32[72,256]{1,0:T(8,128)S(1)} %get-tuple-element.70.refs_0_), channel_id=1, source_target_pairs={{0,12},{4,8},{8,4},{12,0},{1,13},{5,9},{9,5},{13,1},{2,14},{6,10},... | collective-permute-start | bytes 221192 | tf_op jit(solution)/shard_map/ppermute | solution.py:470
  73.8 7.4 %collective-permute-start.16 = (f32[72,256]{1,0:T(8,128)S(1)}, f32[72,256]{1,0:T(8,128)S(1)}, u32[]{:S(2)}, u32[]{:S(2)}) collective-permute-start(f32[72,256]{1,0:T(8,128)S(1)} %get-tuple-element.70.refs_0_), channel_id=1, source_target_pairs={{0,8},{4,12},{8,0},{12,4},{1,9},{5,13},{9,1},{13,5},{2,10},{6,14},... | collective-permute-start | bytes 221192 | tf_op jit(solution)/shard_map/ppermute | solution.py:470
  73.8 7.4 %collective-permute-start.15 = (f32[72,256]{1,0:T(8,128)S(1)}, f32[72,256]{1,0:T(8,128)S(1)}, u32[]{:S(2)}, u32[]{:S(2)}) collective-permute-start(f32[72,256]{1,0:T(8,128)S(1)} %get-tuple-element.70.refs_0_), channel_id=1, source_target_pairs={{0,4},{4,0},{8,12},{12,8},{1,5},{5,1},{9,13},{13,9},{2,6},{6,2},{1... | collective-permute-start | bytes 221192 | tf_op jit(solution)/shard_map/ppermute | solution.py:470

commit v2 on v1

--- a/solution.py
+++ b/solution.py
@@ -12,25 +12,39 @@
 BF16 = jnp.bfloat16
 VMEM = pl.BlockSpec(memory_space=pltpu.VMEM)
 ANY = pl.BlockSpec(memory_space=pl.ANY)
+HBM = pltpu.MemorySpace.HBM
 NN = (((1,), (0,)), ((), ()))
 NT = (((1,), (1,)), ((), ()))
 SCALE = math.sqrt(0.5 * math.log2(math.e))
-STRIP = 128
+STRIP = 256
 BLOCK = 256
 
 
-def call(kernel, out_shape, args, anywhere=(), scratch=(), name=None, cost=None):
+def resident_shape(*shape):
+    return pltpu.VMEM(shape, BF16)
+
+
+def is_resident(shape):
+    return not isinstance(shape, jax.ShapeDtypeStruct)
+
+
+def call(kernel, out_shape, args, anywhere=(), pinned=(), resident=(), scratch=(), name=None, cost=None):
     total = sum(a.size * a.dtype.itemsize for i, a in enumerate(args) if i not in anywhere)
     total += sum(math.prod(s.shape) * s.dtype.itemsize for s in out_shape)
+    held = sum(a.size * a.dtype.itemsize for a in args if any(a is kept for kept in resident))
+    held += sum(math.prod(s.shape) * s.dtype.itemsize for s in out_shape if is_resident(s))
     if cost is not None:
         cost = pl.CostEstimate(flops=cost[0], transcendentals=cost[1], bytes_accessed=total)
+    args = [
+        pltpu.with_memory_space_constraint(a, HBM) if i in pinned else a for i, a in enumerate(args)
+    ]
     results = pl.pallas_call(
         kernel,
         out_shape=list(out_shape),
         in_specs=[ANY if i in anywhere else VMEM for i in range(len(args))],
         out_specs=[VMEM] * len(out_shape),
         scratch_shapes=list(scratch),
-        compiler_params=pltpu.CompilerParams(vmem_limit_bytes=total + (8 << 20)),
+        compiler_params=pltpu.CompilerParams(vmem_limit_bytes=total - held + (6 << 20)),
         cost_estimate=cost,
         name=name,
     )(*args)
@@ -66,12 +80,50 @@
     return both[:rows] + both[rows:] + lax.dot_general(vh, low, dims, preferred_element_type=F32)
 
 
-def gauss(left, right, dims):
-    squared = None
-    for d in range(dims):
-        offset = left[:, d : d + 1] - right[d : d + 1, :]
-        squared = offset * offset if squared is None else squared + offset * offset
-    return jnp.exp2(-squared)
+def stack_scalars(first, second):
+    row = lax.broadcasted_iota(jnp.int32, (8, first[0].shape[1]), 0)
+    block = jnp.zeros(row.shape, F32)
+    for i, value in enumerate(first + second):
+        block = jnp.where(row == i, value, block)
+    return block
+
+
+def features(scaled, unit):
+    value = scaled * (1.0 / unit)
+    whole = jnp.floor(value + 0.5)
+    part = value - whole
+    f1, f2, f3 = (f.astype(F32) for f in split3(part))
+    norm = jnp.sum(whole * whole, axis=0, keepdims=True)
+    rest = jnp.sum(part * (2.0 * whole + part), axis=0, keepdims=True)
+    norms = [-f.astype(F32) for f in split3(norm)]
+    rests = [-f.astype(F32) for f in split3(rest)]
+    ones = [jnp.ones_like(norm)] * 3
+    twice = 2.0 * whole
+    g1, g2, g3 = 2.0 * f1, 2.0 * f2, 2.0 * f3
+    left = (
+        jnp.concatenate([twice, stack_scalars(norms, ones)], axis=0),
+        jnp.concatenate(
+            [twice, twice, twice, g1, g2, g3, g1, g1, g2, stack_scalars(rests, ones)], axis=0
+        ),
+    )
+    right = (
+        jnp.concatenate([whole, stack_scalars(ones, norms)], axis=0),
+        jnp.concatenate(
+            [f1, f2, f3, whole, whole, whole, f1, f2, f1, stack_scalars(ones, rests)], axis=0
+        ),
+    )
+    return tuple(a.T.astype(BF16) for a in left), tuple(a.astype(BF16) for a in right)
+
+
+def unit_of(scaled):
+    peak = jnp.max(jnp.max(jnp.abs(scaled), axis=1, keepdims=True), axis=0, keepdims=True)
+    return jnp.maximum(peak, 1e-6) * (1.0 / 128.0)
+
+
+def gauss(left, right, unit):
+    squared = lax.dot_general(left[0], right[0], NN, preferred_element_type=F32)
+    squared = squared + lax.dot_general(left[1], right[1], NN, preferred_element_type=F32)
+    return jnp.exp2(squared * (unit * unit))
 
 
 def pick(table, chosen):
@@ -105,8 +157,8 @@
 
 def setup_kernel(stages, total, anchors, *refs):
     sources, refs = refs[:6], refs[6:]
-    message, rhs, pts_row, basis_h, basis_l, chosen_out, params = refs[:7]
-    pts, skel, keep, scales, noise, pts_col, sems = refs[7:]
+    message, rhs, la, lb, ra, rb, basis_h, basis_l, chosen_out, params = refs[:10]
+    pts, skel, keep, scales, noise, sems = refs[10:]
     targets = (pts, rhs, skel, keep, scales, noise)
     copies = [
         pltpu.make_async_copy(source, target, sems.at[i])
@@ -124,17 +176,18 @@
     length = row_sum(jnp.where(row == lane, spread, 0.0))
     valid = lax.broadcasted_iota(jnp.int32, (8, 1), 0) < dims
     inverse = SCALE / jnp.where(valid, length, 1.0)
-    shift = points[:, 0:1]
+    low_end = jnp.min(points, axis=1, keepdims=True)
+    shift = low_end + 0.5 * (jnp.max(points, axis=1, keepdims=True) - low_end)
     chosen = pick(points, skel[...])
     rows = rhs.shape[0]
     message[rows + 8 :, :] = chosen
     scaled = (points - shift) * inverse
-    own = (chosen - shift) * inverse
-    pts_row[...] = scaled
-    pts_col[...] = scaled.T
+    unit = unit_of(scaled)
+    (la[...], lb[...]), (ra[...], rb[...]) = features(scaled, unit)
+    _, own = features((chosen - shift) * inverse, unit)
     for i in range(count // STRIP):
         strip = slice(i * STRIP, (i + 1) * STRIP)
-        high, low = split(gauss(pts_col[strip, :], own, dims))
+        high, low = split(gauss((la[strip, :], lb[strip, :]), own, unit))
         basis_h[strip, :] = high
         basis_l[strip, :] = low
     copies[1].wait()
@@ -143,7 +196,9 @@
     message[rows : rows + 8, :] = to_rows([row_sum(value * value)], chosen.shape[1])
     copies[3].wait()
     copies[5].wait()
-    params[...] = column_state([inverse, shift, jnp.broadcast_to(noise[...], (8, 1))])
+    params[...] = column_state(
+        [inverse, shift, jnp.broadcast_to(noise[...], (8, 1)), jnp.broadcast_to(unit, (8, 1))]
+    )
     number = lax.axis_index("leaf") * anchors + lax.axis_index("sub")
     rank = keep.shape[1]
     slot = 0
@@ -159,69 +214,29 @@
                 slot += 1
 
 
-def part_offsets(size, first, last):
-    offsets = [0]
-    for i in range(first, last):
-        offsets.append(offsets[-1] + size - i * BLOCK)
-    return offsets
-
-
 def near_blocks(value, parts):
-    rows, size = value.shape
-    vh, vl = split(value)
-    both = jnp.concatenate([vh, vl], axis=0)
-    sums = [None] * (size // BLOCK)
-
-    def three(cut, high, low, dims):
-        wide = lax.dot_general(both[:, cut], high, dims, preferred_element_type=F32)
-        thin = lax.dot_general(vh[:, cut], low, dims, preferred_element_type=F32)
-        return wide[:rows] + wide[rows:] + thin
-
-    def add(j, term):
-        sums[j] = term if sums[j] is None else sums[j] + term
-
-    for first, last, high, low in parts:
-        offsets = part_offsets(size, first, last)
-        for i in range(first, last):
-            start, stop = offsets[i - first], offsets[i - first + 1]
-            cut = slice(i * BLOCK, (i + 1) * BLOCK)
-            out = three(cut, high[:, start:stop], low[:, start:stop], NN)
-            for j in range(i, size // BLOCK):
-                add(j, out[:, (j - i) * BLOCK : (j - i + 1) * BLOCK])
-            if i + 1 < size // BLOCK:
-                start += BLOCK
-                add(i, three(slice((i + 1) * BLOCK, size), high[:, start:stop], low[:, start:stop], NT))
-    zero = jnp.zeros((rows, BLOCK), F32)
-    return jnp.concatenate([zero if s is None else s for s in sums], axis=1)
-
-
-def dense_kernel(dims, first, last, more, *refs):
-    pts_row, rhs = refs[:2]
-    before, params = (refs[2], refs[3]) if more else (None, None)
-    high, low, near, pts_col = refs[-4:]
-    size = pts_row.shape[1]
-    offsets = part_offsets(size, first, last)
-    pts_col[...] = pts_row[...].T
-    for i in range(first, last):
-        start = offsets[i - first]
-
-        def body(k, carry):
-            strip = pl.ds(pl.multiple_of(k * STRIP, STRIP), STRIP)
-            left = pts_col[pl.ds(pl.multiple_of(i * BLOCK + k * STRIP, STRIP), STRIP), :]
-            for j in range(i, size // BLOCK):
-                right = pts_row[:, j * BLOCK : (j + 1) * BLOCK]
-                h, l = split(gauss(left, right, dims))
-                part = slice(start + (j - i) * BLOCK, start + (j - i + 1) * BLOCK)
-                high[strip, part] = h
-                low[strip, part] = l
-            return carry
-
-        lax.fori_loop(0, BLOCK // STRIP, body, 0)
+    return jnp.concatenate([dot3(value, high[...], low[...]) for high, low in parts], axis=1)
+
+
+def dense_kernel(start, la, lb, ra, rb, rhs, params, tie, high, low, near):
+    size = la.shape[0]
+    width = high.shape[1]
+    unit = params[0:1, 3:4]
+
+    def body(k, carry):
+        strip = pl.ds(pl.multiple_of(k * STRIP, STRIP), STRIP)
+        left = la[strip, :], lb[strip, :]
+        for j in range(0, width, BLOCK):
+            cut = slice(start + j, start + j + BLOCK)
+            h, l = split(gauss(left, (ra[:, cut], rb[:, cut]), unit))
+            high[strip, j : j + BLOCK] = h
+            low[strip, j : j + BLOCK] = l
+        return carry
+
+    lax.fori_loop(0, size // STRIP, body, 0)
     value = rhs[...]
-    out = near_blocks(value, [(first, last, high, low)])
-    if more:
-        out = out + before[...] + params[0:1, 2:3] * value
-    near[...] = out
+    here = value[:, start : start + width]
+    near[...] = params[0:1, 2:3] * here + dot3(value, high[...], low[...])
 
 
 def levels_of(count):
@@ -270,37 +285,33 @@
     return search
 
 
-def build_tree(dims, coords, chosen, params, transfer, couple, top):
+def build_tree(coords, chosen, params, transfer, couple, top):
     count = len(coords)
     slots = tree_slots(count)
     rank = coords[0].shape[1]
     inverse, shift = params[:, 0:1], params[:, 1:2]
     scaled = [(c - shift) * inverse for c in coords]
+    unit = unit_of(jnp.concatenate(scaled, axis=1))
+    sides = [features(c, unit) for c in scaled]
     for level in range(1, levels_of(count) + 1):
-        parents, parents_scaled = [], []
+        parents, parent_sides = [], []
         for p in range(count >> level):
             slot = slots[level, p]
-            columns = scaled[2 * p].T, scaled[2 * p + 1].T
-            for i in range(rank // STRIP):
-                strip = slice(i * STRIP, (i + 1) * STRIP)
-                high, low = split(gauss(columns[1][strip, :], scaled[2 * p], dims))
-                couple[0][slot, strip, :] = high
-                couple[1][slot, strip, :] = low
+            high, low = split(gauss(sides[2 * p + 1][0], sides[2 * p][1], unit))
+            couple[0][slot] = high
+            couple[1][slot] = low
             if level == levels_of(count) and not top:
                 continue
             joined = jnp.concatenate([coords[2 * p], coords[2 * p + 1]], axis=1)
             parent = pick(joined, chosen[slot : slot + 1, :])
-            parent_scaled = (parent - shift) * inverse
-            for side, column in enumerate(columns):
-                for i in range(rank // STRIP):
-                    strip = slice(i * STRIP, (i + 1) * STRIP)
-                    target = slice(side * rank + i * STRIP, side * rank + (i + 1) * STRIP)
-                    high, low = split(gauss(column[strip, :], parent_scaled, dims))
-                    transfer[0][slot, target, :] = high
-                    transfer[1][slot, target, :] = low
+            parent_side = features((parent - shift) * inverse, unit)
+            for side in range(2):
+                high, low = split(gauss(sides[2 * p + side][0], parent_side[1], unit))
+                transfer[0][slot, side * rank : (side + 1) * rank, :] = high
+                transfer[1][slot, side * rank : (side + 1) * rank, :] = low
             parents.append(parent)
-            parents_scaled.append(parent_scaled)
-        coords, scaled = parents, parents_scaled
+            parent_sides.append(parent_side)
+        coords, sides = parents, parent_sides
     return coords
 
 
@@ -311,14 +322,14 @@
     return total
 
 
-def lower_first_kernel(dims, rows, count, offset, refs):
+def lower_first_kernel(rows, count, offset, refs):
     messages = refs[:count]
     params, chosen = refs[count : count + 2]
     message, terms, transfer_h, transfer_l, couple_h, couple_l = refs[-6:]
     transfer, couple = (transfer_h, transfer_l), (couple_h, couple_l)
     coords = [m[rows + 8 :, :] for m in messages]
     picks = chosen[offset : offset + count - 1, :]
-    coords = build_tree(dims, coords, picks, params, transfer, couple, True)
+    coords = build_tree(coords, picks, params, transfer, couple, True)
     lower_finish(rows, messages, message, terms, transfer, couple, True)
     message[rows + 8 :, :] = coords[0]
 
@@ -342,13 +353,13 @@
     )
 
 
-def upper_build(dims, rows, count, offset, refs):
+def upper_build(rows, count, offset, refs):
     messages = refs[:count]
     params, chosen, transfer_h, transfer_l, couple_h, couple_l = refs[count:]
     coords = [m[rows + 8 :, :] for m in messages]
     picks = chosen[offset : offset + count - 1, :]
     build_tree(
-        dims, coords, picks, params, (transfer_h, transfer_l), (couple_h, couple_l), False
+        coords, picks, params, (transfer_h, transfer_l), (couple_h, couple_l), False
     )
 
 
@@ -394,29 +405,31 @@
     return far_field(rows, messages, upper, lower), basis, rest
 
 
-def dense_parts(cuts, refs):
-    return [(*cut, refs[2 * i], refs[2 * i + 1]) for i, cut in enumerate(cuts)]
-
-
-def first_kernel(rows, count, stages, cuts, refs):
+def dense_parts(refs):
+    return list(zip(refs[0::2], refs[1::2]))
+
+
+def first_kernel(rows, count, stages, parts, refs):
     (search, sums, far), basis, rest = open_refs(rows, count, stages, refs)
-    dense, rest = take_refs(rest, 2 * len(cuts))
-    params, rhs, near_in, message, q_out, near_out, state = rest
+    dense, rest = take_refs(rest, 2 * parts)
+    params, rhs = rest[:2]
+    near_parts, (message, q_out, near_out, state) = take_refs(rest[2:], parts)
+    near_b = jnp.concatenate([n[...] for n in near_parts], axis=1)
     norm = sums[:, 0:1]
     rate = norm / (params[0:1, 2:3] * norm + jnp.abs(far))
-    q = rate * (near_in[...] + dot3(search, basis[0][...], basis[1][...], NT))
+    q = rate * (near_b + dot3(search, basis[0][...], basis[1][...], NT))
     q_out[...] = q
     message[:rows, :] = dot3(q, basis[0][...], basis[1][...])
-    near_q = near_field(q, params, dense_parts(cuts, dense))
+    near_q = near_field(q, params, dense_parts(dense))
     near_out[...] = near_q
     dots = [row_sum(rhs[...] * q), row_sum(q * q), row_sum(q * near_q)]
     message[rows:, :] = to_rows(dots, message.shape[1])
     state[...] = column_state([norm, rate])
 
 
-def second_kernel(rows, count, stages, cuts, refs):
+def second_kernel(rows, count, stages, parts, refs):
     (search, sums, far), basis, rest = open_refs(rows, count, stages, refs)
-    dense, rest = take_refs(rest, 2 * len(cuts))
+    dense, rest = take_refs(rest, 2 * parts)
     params, rhs, q_in, near_in, state_in = rest[:5]
     message, x_out, r_out, d_out, q_out, near_out, state = rest[5:]
     norm0, rate = state_in[:, 0:1], state_in[:, 1:2]
@@ -442,7 +455,7 @@
     d_out[...] = d1
     q_out[...] = q1
     message[:rows, :] = dot3(r2, basis[0][...], basis[1][...])
-    near = near_field(r2, params, dense_parts(cuts, dense))
+    near = near_field(r2, params, dense_parts(dense))
     near_out[...] = near
     dots = [row_sum(r2 * r2), row_sum(r2 * q1), row_sum(r2 * near)]
     message[rows:, :] = to_rows(dots, message.shape[1])
@@ -494,12 +507,15 @@
     offsets = [sum(counts[:i]) - i for i in range(len(counts))]
     stage_count = len(stages) - 1
 
-    message, rhs, pts_row, basis_h, basis_l, chosen, params = call(
+    message, rhs, la, lb, ra, rb, basis_h, basis_l, chosen, params = call(
         functools.partial(setup_kernel, bases, total, subs),
         [
             f32_shape(rows + 16, rank),
             f32_shape(rows, size),
-            f32_shape(8, size),
+            bf16_shape(size, 16),
+            bf16_shape(size, 80),
+            bf16_shape(16, size),
+            bf16_shape(80, size),
             bf16_shape(size, rank),
             bf16_shape(size, rank),
             jax.ShapeDtypeStruct((slots, rank), jnp.int32),
@@ -514,13 +530,13 @@
             jnp.reshape(noise_var, (1, 1)),
         ],
         anywhere=range(6),
+        pinned=range(5),
         scratch=[
             pltpu.VMEM((dims, size), F32),
             pltpu.VMEM((1, rank), jnp.int32),
             pltpu.VMEM(node_keep.shape, jnp.int32),
             pltpu.VMEM((1, dims), F32),
             pltpu.VMEM((1, 1), F32),
-            pltpu.VMEM((size, 8), F32),
             pltpu.SemaphoreType.DMA((6,)),
         ],
         name="setup",
@@ -531,34 +547,31 @@
         nodes = count - 1
         return [bf16_shape(nodes, 2 * rank, rank)] * 2 + [bf16_shape(nodes, rank, rank)] * 2
 
-    blocks = size // BLOCK
-    cuts = [(0, blocks // 4), (blocks // 4, blocks)]
-    dense = []
-
-    def build_dense(cut, extra):
-        width = part_offsets(size, *cut)[-1]
+    first_width = size // BLOCK * 3 // 8 * BLOCK
+    widths = [first_width, size - first_width]
+    dense, near_parts = [], []
+
+    def build_dense(start, width, tie):
         high, low, near = call(
-            functools.partial(dense_kernel, dims, *cut, len(extra) > 1),
-            [bf16_shape(BLOCK, width), bf16_shape(BLOCK, width), f32_shape(rows, size)],
-            [pts_row, rhs] + extra,
-            scratch=[pltpu.VMEM((size, 8), F32)],
-            cost=(12 * rows * BLOCK * width, BLOCK * width),
+            functools.partial(dense_kernel, start),
+            [resident_shape(size, width)] * 2 + [f32_shape(rows, width)],
+            [la, lb, ra, rb, rhs, params, tie],
+            cost=(6 * rows * size * width + 192 * size * width, size * width),
             name="dense",
         )
         dense.extend([high, low])
-        return near
+        near_parts.append(near)
 
     trees = []
     terms_all = []
-    near = None
     for i in range(stage_count):
         messages = gather(message, hops[i])
         extra = []
         if i == 0:
-            near = build_dense(cuts[0], [])
-            extra = [near]
+            build_dense(0, widths[0], params)
+            extra = near_parts[:1]
         message, terms, *tree = call(
-            refs_of(lower_first_kernel, dims, rows, counts[i], offsets[i]),
+            refs_of(lower_first_kernel, rows, counts[i], offsets[i]),
             [f32_shape(rows + 16, rank), f32_shape(bases[i][1], rows, rank)]
             + tree_shapes(counts[i]),
             messages + [params, chosen] + extra,
@@ -567,9 +580,9 @@
         trees.append(tree)
         terms_all.append(terms)
     messages = gather(message, hops[-1])
-    near = build_dense(cuts[1], [near, params, message])
+    build_dense(widths[0], widths[1], message)
     upper = call(
-        refs_of(upper_build, dims, rows, counts[-1], offsets[-1]),
+        refs_of(upper_build, rows, counts[-1], offsets[-1]),
         tree_shapes(counts[-1]),
         messages + [params, chosen],
         name="upper_build",
@@ -597,16 +610,18 @@
 
     fixed = (rows, counts[-1], stage_count)
     message, q, near, state = call(
-        refs_of(first_kernel, *fixed, cuts),
+        refs_of(first_kernel, *fixed, len(widths)),
         [message_shape, vector, vector, state_shape],
-        messages + lower_of(terms_all) + upper + basis + dense + [params, rhs, near],
+        messages + lower_of(terms_all) + upper + basis + dense + [params, rhs] + near_parts,
+        resident=dense,
         name="first",
     )
     arrived = exchange(message)
     message, x, r, d, q, near, state = call(
-        refs_of(second_kernel, *fixed, cuts),
+        refs_of(second_kernel, *fixed, len(widths)),
         [message_shape, vector, vector, vector, vector, vector, state_shape],
         arrived + upper + basis + dense + [params, rhs, q, near, state],
+        resident=dense,
         name="second",
     )
     arrived = exchange(message)

time: 84.2 us -> 73.1 us (0.87)
  Pallas kernels: 39.3 us -> 31.8 us
  local copies, waits for them, and re-layouts: 3.92 us -> 0 us
    pallas_call x10, Pallas kernels: 39.3 us -> 31.8 us  [call(): pl.pallas_call(kernel, out_shape=list(out_shape), in_specs=[ANY if i in a...]
    unnamed x10 -> x0, local copies, waits for them, and re-layouts: 3.92 us -> none
  transfers between devices with their start and end apart: 18 -> 18, of which waited for: 8 -> 10; matrix products, arithmetic and copies ran while one was open for 0% -> 0% of each run, Pallas kernels for 16% -> 14%
where the time goes in v2:
time: 73.1 us; the launch traced here: 72.9 us
  Pallas kernels  31.8 us (44%)
  starting transfers between devices  20.7 us (28%)
  waiting for transfers between devices  19.1 us (26%)
  between operations  1.36 us (2%)
    pallas_call x10, Pallas kernels, call(): pl.pallas_call(kernel, out_shape=list(out_shape), in_specs=[ANY if i in a...  31.8 us
    ppermute x18, starting transfers between devices, gather(): return [value] + [lax.ppermute(value, axis, pair) for pair in pairs]  20.7 us
    ppermute x18, waiting for transfers between devices, gather(): return [value] + [lax.ppermute(value, axis, pair) for pair in pairs]  19.1 us
  transfers between devices with their start and end apart: 18, of which 10 were waited for; matrix products, arithmetic and copies ran while one was open for 0% of the time, Pallas kernels for 14%

profile of v2, /device:TPU:0, one launch (start us, length us, event | category | flops | bytes accessed | tf_op | source)
XLA Modules:
  0.0 72.9 jit_solution(11199931125247651304)
XLA Ops:
  1.3 3.8 %setup.1 = (f32[80,256]{1,0:T(8,128)S(1)}, f32[64,2048]{1,0:T(8,128)S(1)}, bf16[2048,16]{1,0:T(8,128)(2,1)S(1)}, bf16[2048,80]{1,0:T(8,128)(2,1)S(1)}, bf16[16,2...) custom-call(f32[6,2048]{1,0:T(8,128)} %refs_0_.1, ...), custom_call_target="tpu_custom_call" | custom-call | tf_op jit(solution)/shard_map/setup/pallas_call | solution.py:41
  5.1 2.4 %collective-permute-start.2 = (f32[80,256]{1,0:T(8,128)S(1)}, f32[80,256]{1,0:T(8,128)S(1)}, u32[]{:S(2)}, u32[]{:S(2)}) collective-permute-start(f32[80,256]{1,0:T(8,128)S(1)} %get-tuple-element.43.refs_0_), channel_id=1, source_target_pairs={{0,3},{1,2},{2,1},{3,0},{4,7},{5,6},{6,5},{7,4},{8,11},{9,10},{10,... | collective-permute-start | bytes 245768 | tf_op jit(solution)/shard_map/ppermute | solution.py:483
  8.2 4.2 %dense.2 = (bf16[2048,768]{1,0:T(8,128)(2,1)S(1)}, bf16[2048,768]{1,0:T(8,128)(2,1)S(1)}, f32[64,768]{1,0:T(8,128)S(1)}) custom-call(bf16[2048,16]{1,0:T(8,128)(2,1)S(1)} %get-tuple-element.46.la, bf16[2048,80]{1,0:T(8,128)(2,1)S(1)} %get-tuple-element.47.lb, bf16[16,2048]{1,0:T(8,128)(2,1)S(1)} %get-tuple-element.48.ra, ...), custom_call_target="tpu_custom_call" | custom-call | flops 905969664 | bytes 7806976 | tf_op jit(solution)/shard_map/dense/pallas_call | solution.py:41
  12.5 2.1 %lower_first.1 = (f32[80,256]{1,0:T(8,128)S(1)}, f32[2,64,256]{2,1,0:T(8,128)S(1)}, bf16[3,512,256]{2,1,0:T(8,128)(2,1)S(1)}, bf16[3,512,256]{2,1,0:T(8,128)(2,1...) custom-call(f32[80,256]{1,0:T(8,128)S(1)} %get-tuple-element.43.refs_0_, ...), custom_call_target="tpu_custom_call" | custom-call | tf_op jit(solution)/shard_map/lower_first/pallas_call | solution.py:41
  14.7 4.2 %collective-permute-start.5 = (f32[80,256]{1,0:T(8,128)S(1)}, f32[80,256]{1,0:T(8,128)S(1)}, u32[]{:S(2)}, u32[]{:S(2)}) collective-permute-start(f32[80,256]{1,0:T(8,128)S(1)} %get-tuple-element.52.refs_0_.tie), channel_id=1, source_target_pairs={{0,12},{4,8},{8,4},{12,0},{1,13},{5,9},{9,5},{13,1},{2,14},{6,10},... | collective-permute-start | bytes 245768 | tf_op jit(solution)/shard_map/ppermute | solution.py:483
  19.5 6.1 %dense.3 = (bf16[2048,1280]{1,0:T(8,128)(2,1)S(1)}, bf16[2048,1280]{1,0:T(8,128)(2,1)S(1)}, f32[64,1280]{1,0:T(8,128)S(1)}) custom-call(bf16[2048,16]{1,0:T(8,128)(2,1)S(1)} %get-tuple-element.46.la, bf16[2048,80]{1,0:T(8,128)(2,1)S(1)} %get-tuple-element.47.lb, bf16[16,2048]{1,0:T(8,128)(2,1)S(1)} %get-tuple-element.48.ra, ...), custom_call_target="tpu_custom_call" | custom-call | flops 1509949440 | bytes 12210176 | tf_op jit(solution)/shard_map/dense/pallas_call | solution.py:41
  26.0 1.3 %upper_build.1 = (bf16[3,512,256]{2,1,0:T(8,128)(2,1)S(1)}, bf16[3,512,256]{2,1,0:T(8,128)(2,1)S(1)}, bf16[3,256,256]{2,1,0:T(8,128)(2,1)S(1)}, bf16[3,256,256]{2,1,0:T(8,128)(2,1)S(1)}) custom-call(f32[80,256]{1,0:T(8,128)S(1)} %get-tuple-element.52.refs_0_.tie, f32[80,256]{1,0:T(8,128)S(1)} %collective-permute-done.3.refs_1_, ...), custom_call_target="tpu_custom_call" | custom-call | tf_op jit(solution)/shard_map/upper_build/pallas_call | solution.py:41
  27.3 5.0 %first.1 = (f32[72,256]{1,0:T(8,128)S(1)}, f32[64,2048]{1,0:T(8,128)S(1)}, f32[64,2048]{1,0:T(8,128)S(1)}, f32[64,128]{1,0:T(8,128)S(1)}) custom-call(f32[80,256]{1,0:T(8,128)S(1)} %get-tuple-element.52.refs_0_.tie, f32[80,256]{1,0:T(8,128)S(1)} %collective-permute-done.3.refs_1_, f32[80,256]{1,0:T(8,128)S(1)} %collective-permute-done.4.refs_2_, ...), custom_call_target="tpu_custom_call" | custom-call | tf_op jit(solution)/shard_map/first/pallas_call | solution.py:41
  32.7 1.2 %collective-permute-start.7 = (f32[72,256]{1,0:T(8,128)S(1)}, f32[72,256]{1,0:T(8,128)S(1)}, u32[]{:S(2)}, u32[]{:S(2)}) collective-permute-start(f32[72,256]{1,0:T(8,128)S(1)} %get-tuple-element.67.refs_0_), channel_id=1, source_target_pairs={{0,2},{1,3},{2,0},{3,1},{4,6},{5,7},{6,4},{7,5},{8,10},{9,11},{10,... | collective-permute-start | bytes 221192 | tf_op jit(solution)/shard_map/ppermute | solution.py:483
  34.1 2.6 %collective-permute-done.8.refs_3_ = f32[72,256]{1,0:T(8,128)S(1)} collective-permute-done((f32[72,256]{1,0:T(8,128)S(1)}, f32[72,256]{1,0:T(8,128)S(1)}, u32[]{:S(2)}, u32[]{:S(2)}) %collective-permute-start.8) | collective-permute-done | bytes 73760 | tf_op jit(solution)/shard_map/ppermute | solution.py:483
  36.8 1.7 %collective-permute-done.7.refs_2_ = f32[72,256]{1,0:T(8,128)S(1)} collective-permute-done((f32[72,256]{1,0:T(8,128)S(1)}, f32[72,256]{1,0:T(8,128)S(1)}, u32[]{:S(2)}, u32[]{:S(2)}) %collective-permute-start.7) | collective-permute-done | bytes 73760 | tf_op jit(solution)/shard_map/ppermute | solution.py:483
  39.2 3.5 %collective-permute-start.11 = (f32[72,256]{1,0:T(8,128)S(1)}, f32[72,256]{1,0:T(8,128)S(1)}, u32[]{:S(2)}, u32[]{:S(2)}) collective-permute-start(f32[72,256]{1,0:T(8,128)S(1)} %get-tuple-element.70.refs_0_), channel_id=1, source_target_pairs={{0,12},{4,8},{8,4},{12,0},{1,13},{5,9},{9,5},{13,1},{2,14},{6,10},... | collective-permute-start | bytes 221192 | tf_op jit(solution)/shard_map/ppermute | solution.py:483
  42.7 1.0 %collective-permute-start.9 = (f32[72,256]{1,0:T(8,128)S(1)}, f32[72,256]{1,0:T(8,128)S(1)}, u32[]{:S(2)}, u32[]{:S(2)}) collective-permute-start(f32[72,256]{1,0:T(8,128)S(1)} %get-tuple-element.70.refs_0_), channel_id=1, source_target_pairs={{0,4},{4,0},{8,12},{12,8},{1,5},{5,1},{9,13},{13,9},{2,6},{6,2},{1... | collective-permute-start | bytes 221192 | tf_op jit(solution)/shard_map/ppermute | solution.py:483
  43.6 2.6 %collective-permute-done.11.refs_3_ = f32[72,256]{1,0:T(8,128)S(1)} collective-permute-done((f32[72,256]{1,0:T(8,128)S(1)}, f32[72,256]{1,0:T(8,128)S(1)}, u32[]{:S(2)}, u32[]{:S(2)}) %collective-permute-start.11) | collective-permute-done | bytes 73760 | tf_op jit(solution)/shard_map/ppermute | solution.py:483
  46.3 2.6 %collective-permute-done.10.refs_2_ = f32[72,256]{1,0:T(8,128)S(1)} collective-permute-done((f32[72,256]{1,0:T(8,128)S(1)}, f32[72,256]{1,0:T(8,128)S(1)}, u32[]{:S(2)}, u32[]{:S(2)}) %collective-permute-start.10) | collective-permute-done | bytes 73760 | tf_op jit(solution)/shard_map/ppermute | solution.py:483
  48.9 5.1 %second.1 = (f32[72,256]{1,0:T(8,128)S(1)}, f32[64,2048]{1,0:T(8,128)S(1)}, f32[64,2048]{1,0:T(8,128)S(1)}, f32[64,2048]{1,0:T(8,128)S(1)}, f32[64,2048]{1,0:T(8...) custom-call(f32[72,256]{1,0:T(8,128)S(1)} %get-tuple-element.70.refs_0_, ...), custom_call_target="tpu_custom_call" | custom-call | tf_op jit(solution)/shard_map/second/pallas_call | solution.py:41
  54.2 1.3 %collective-permute-start.13 = (f32[72,256]{1,0:T(8,128)S(1)}, f32[72,256]{1,0:T(8,128)S(1)}, u32[]{:S(2)}, u32[]{:S(2)}) collective-permute-start(f32[72,256]{1,0:T(8,128)S(1)} %get-tuple-element.75.refs_0_), channel_id=1, source_target_pairs={{0,2},{1,3},{2,0},{3,1},{4,6},{5,7},{6,4},{7,5},{8,10},{9,11},{10,... | collective-permute-start | bytes 221192 | tf_op jit(solution)/shard_map/ppermute | solution.py:483
  55.9 2.7 %collective-permute-done.14.refs_3_ = f32[72,256]{1,0:T(8,128)S(1)} collective-permute-done((f32[72,256]{1,0:T(8,128)S(1)}, f32[72,256]{1,0:T(8,128)S(1)}, u32[]{:S(2)}, u32[]{:S(2)}) %collective-permute-start.14) | collective-permute-done | bytes 73760 | tf_op jit(solution)/shard_map/ppermute | solution.py:483
  58.5 1.6 %collective-permute-done.13.refs_2_ = f32[72,256]{1,0:T(8,128)S(1)} collective-permute-done((f32[72,256]{1,0:T(8,128)S(1)}, f32[72,256]{1,0:T(8,128)S(1)}, u32[]{:S(2)}, u32[]{:S(2)}) %collective-permute-start.13) | collective-permute-done | bytes 73760 | tf_op jit(solution)/shard_map/ppermute | solution.py:483
  60.9 1.8 %collective-permute-start.17 = (f32[72,256]{1,0:T(8,128)S(1)}, f32[72,256]{1,0:T(8,128)S(1)}, u32[]{:S(2)}, u32[]{:S(2)}) collective-permute-start(f32[72,256]{1,0:T(8,128)S(1)} %get-tuple-element.76.refs_0_), channel_id=1, source_target_pairs={{0,12},{4,8},{8,4},{12,0},{1,13},{5,9},{9,5},{13,1},{2,14},{6,10},... | collective-permute-start | bytes 221192 | tf_op jit(solution)/shard_map/ppermute | solution.py:483
  62.7 2.7 %collective-permute-start.15 = (f32[72,256]{1,0:T(8,128)S(1)}, f32[72,256]{1,0:T(8,128)S(1)}, u32[]{:S(2)}, u32[]{:S(2)}) collective-permute-start(f32[72,256]{1,0:T(8,128)S(1)} %get-tuple-element.76.refs_0_), channel_id=1, source_target_pairs={{0,4},{4,0},{8,12},{12,8},{1,5},{5,1},{9,13},{13,9},{2,6},{6,2},{1... | collective-permute-start | bytes 221192 | tf_op jit(solution)/shard_map/ppermute | solution.py:483
  65.4 2.6 %collective-permute-done.17.refs_3_ = f32[72,256]{1,0:T(8,128)S(1)} collective-permute-done((f32[72,256]{1,0:T(8,128)S(1)}, f32[72,256]{1,0:T(8,128)S(1)}, u32[]{:S(2)}, u32[]{:S(2)}) %collective-permute-start.17) | collective-permute-done | bytes 73760 | tf_op jit(solution)/shard_map/ppermute | solution.py:483
  68.0 2.3 %collective-permute-done.16.refs_2_ = f32[72,256]{1,0:T(8,128)S(1)} collective-permute-done((f32[72,256]{1,0:T(8,128)S(1)}, f32[72,256]{1,0:T(8,128)S(1)}, u32[]{:S(2)}, u32[]{:S(2)}) %collective-permute-start.16) | collective-permute-done | bytes 73760 | tf_op jit(solution)/shard_map/ppermute | solution.py:483
  70.2 2.7 %last.1 = (f32[64,2048]{1,0:T(8,128)}, f32[64,2048]{1,0:T(8,128)}) custom-call(f32[72,256]{1,0:T(8,128)S(1)} %get-tuple-element.76.refs_0_, f32[72,256]{1,0:T(8,128)S(1)} %collective-permute-done.15.refs_1_, f32[72,256]{1,0:T(8,128)S(1)} %collective-permute-done.16.refs_2_, f32[72,256]{1,0:T(8,128)S(1)} %collective-permute-done.17.refs_3_, ...), custom_call_target="tpu_custom_call" | custom-call | tf_op jit(solution)/shard_map/last/pallas_call | solution.py:41
  (22 shorter events, 4.7 us)
Async XLA Ops:
  5.1 7.3 %collective-permute-start.2 = (f32[80,256]{1,0:T(8,128)S(1)}, f32[80,256]{1,0:T(8,128)S(1)}, u32[]{:S(2)}, u32[]{:S(2)}) collective-permute-start(f32[80,256]{1,0:T(8,128)S(1)} %get-tuple-element.43.refs_0_), channel_id=1, source_target_pairs={{0,3},{1,2},{2,1},{3,0},{4,7},{5,6},{6,5},{7,4},{8,11},{9,10},{10,... | collective-permute-start | bytes 245768 | tf_op jit(solution)/shard_map/ppermute | solution.py:483
  7.5 5.0 %collective-permute-start.1 = (f32[80,256]{1,0:T(8,128)S(1)}, f32[80,256]{1,0:T(8,128)S(1)}, u32[]{:S(2)}, u32[]{:S(2)}) collective-permute-start(f32[80,256]{1,0:T(8,128)S(1)} %get-tuple-element.43.refs_0_), channel_id=1, source_target_pairs={{0,2},{1,3},{2,0},{3,1},{4,6},{5,7},{6,4},{7,5},{8,10},{9,11},{10,... | collective-permute-start | bytes 245768 | tf_op jit(solution)/shard_map/ppermute | solution.py:483
  8.2 4.4 %collective-permute-start = (f32[80,256]{1,0:T(8,128)S(1)}, f32[80,256]{1,0:T(8,128)S(1)}, u32[]{:S(2)}, u32[]{:S(2)}) collective-permute-start(f32[80,256]{1,0:T(8,128)S(1)} %get-tuple-element.43.refs_0_), channel_id=1, source_target_pairs={{0,1},{1,0},{2,3},{3,2},{4,5},{5,4},{6,7},{7,6},{8,9},{9,8},{10,11... | collective-permute-start | bytes 245768 | tf_op jit(solution)/shard_map/ppermute | solution.py:483
  14.7 11.0 %collective-permute-start.5 = (f32[80,256]{1,0:T(8,128)S(1)}, f32[80,256]{1,0:T(8,128)S(1)}, u32[]{:S(2)}, u32[]{:S(2)}) collective-permute-start(f32[80,256]{1,0:T(8,128)S(1)} %get-tuple-element.52.refs_0_.tie), channel_id=1, source_target_pairs={{0,12},{4,8},{8,4},{12,0},{1,13},{5,9},{9,5},{13,1},{2,14},{6,10},... | collective-permute-start | bytes 245768 | tf_op jit(solution)/shard_map/ppermute | solution.py:483
  18.9 7.1 %collective-permute-start.4 = (f32[80,256]{1,0:T(8,128)S(1)}, f32[80,256]{1,0:T(8,128)S(1)}, u32[]{:S(2)}, u32[]{:S(2)}) collective-permute-start(f32[80,256]{1,0:T(8,128)S(1)} %get-tuple-element.52.refs_0_.tie), channel_id=1, source_target_pairs={{0,8},{4,12},{8,0},{12,4},{1,9},{5,13},{9,1},{13,5},{2,10},{6,14},... | collective-permute-start | bytes 245768 | tf_op jit(solution)/shard_map/ppermute | solution.py:483
  18.9 7.1 %collective-permute-start.3 = (f32[80,256]{1,0:T(8,128)S(1)}, f32[80,256]{1,0:T(8,128)S(1)}, u32[]{:S(2)}, u32[]{:S(2)}) collective-permute-start(f32[80,256]{1,0:T(8,128)S(1)} %get-tuple-element.52.refs_0_.tie), channel_id=1, source_target_pairs={{0,4},{4,0},{8,12},{12,8},{1,5},{5,1},{9,13},{13,9},{2,6},{6,2},{1... | collective-permute-start | bytes 245768 | tf_op jit(solution)/shard_map/ppermute | solution.py:483
  32.2 4.5 %collective-permute-start.8 = (f32[72,256]{1,0:T(8,128)S(1)}, f32[72,256]{1,0:T(8,128)S(1)}, u32[]{:S(2)}, u32[]{:S(2)}) collective-permute-start(f32[72,256]{1,0:T(8,128)S(1)} %get-tuple-element.67.refs_0_), channel_id=1, source_target_pairs={{0,3},{1,2},{2,1},{3,0},{4,7},{5,6},{6,5},{7,4},{8,11},{9,10},{10,... | collective-permute-start | bytes 221192 | tf_op jit(solution)/shard_map/ppermute | solution.py:483
  32.7 5.7 %collective-permute-start.7 = (f32[72,256]{1,0:T(8,128)S(1)}, f32[72,256]{1,0:T(8,128)S(1)}, u32[]{:S(2)}, u32[]{:S(2)}) collective-permute-start(f32[72,256]{1,0:T(8,128)S(1)} %get-tuple-element.67.refs_0_), channel_id=1, source_target_pairs={{0,2},{1,3},{2,0},{3,1},{4,6},{5,7},{6,4},{7,5},{8,10},{9,11},{10,... | collective-permute-start | bytes 221192 | tf_op jit(solution)/shard_map/ppermute | solution.py:483
  33.9 4.5 %collective-permute-start.6 = (f32[72,256]{1,0:T(8,128)S(1)}, f32[72,256]{1,0:T(8,128)S(1)}, u32[]{:S(2)}, u32[]{:S(2)}) collective-permute-start(f32[72,256]{1,0:T(8,128)S(1)} %get-tuple-element.67.refs_0_), channel_id=1, source_target_pairs={{0,1},{1,0},{2,3},{3,2},{4,5},{5,4},{6,7},{7,6},{8,9},{9,8},{10,11... | collective-permute-start | bytes 221192 | tf_op jit(solution)/shard_map/ppermute | solution.py:483
  39.2 7.1 %collective-permute-start.11 = (f32[72,256]{1,0:T(8,128)S(1)}, f32[72,256]{1,0:T(8,128)S(1)}, u32[]{:S(2)}, u32[]{:S(2)}) collective-permute-start(f32[72,256]{1,0:T(8,128)S(1)} %get-tuple-element.70.refs_0_), channel_id=1, source_target_pairs={{0,12},{4,8},{8,4},{12,0},{1,13},{5,9},{9,5},{13,1},{2,14},{6,10},... | collective-permute-start | bytes 221192 | tf_op jit(solution)/shard_map/ppermute | solution.py:483
  42.7 6.2 %collective-permute-start.10 = (f32[72,256]{1,0:T(8,128)S(1)}, f32[72,256]{1,0:T(8,128)S(1)}, u32[]{:S(2)}, u32[]{:S(2)}) collective-permute-start(f32[72,256]{1,0:T(8,128)S(1)} %get-tuple-element.70.refs_0_), channel_id=1, source_target_pairs={{0,8},{4,12},{8,0},{12,4},{1,9},{5,13},{9,1},{13,5},{2,10},{6,14},... | collective-permute-start | bytes 221192 | tf_op jit(solution)/shard_map/ppermute | solution.py:483
  42.7 6.2 %collective-permute-start.9 = (f32[72,256]{1,0:T(8,128)S(1)}, f32[72,256]{1,0:T(8,128)S(1)}, u32[]{:S(2)}, u32[]{:S(2)}) collective-permute-start(f32[72,256]{1,0:T(8,128)S(1)} %get-tuple-element.70.refs_0_), channel_id=1, source_target_pairs={{0,4},{4,0},{8,12},{12,8},{1,5},{5,1},{9,13},{13,9},{2,6},{6,2},{1... | collective-permute-start | bytes 221192 | tf_op jit(solution)/shard_map/ppermute | solution.py:483
  54.0 4.6 %collective-permute-start.14 = (f32[72,256]{1,0:T(8,128)S(1)}, f32[72,256]{1,0:T(8,128)S(1)}, u32[]{:S(2)}, u32[]{:S(2)}) collective-permute-start(f32[72,256]{1,0:T(8,128)S(1)} %get-tuple-element.75.refs_0_), channel_id=1, source_target_pairs={{0,3},{1,2},{2,1},{3,0},{4,7},{5,6},{6,5},{7,4},{8,11},{9,10},{10,... | collective-permute-start | bytes 221192 | tf_op jit(solution)/shard_map/ppermute | solution.py:483
  54.2 6.0 %collective-permute-start.13 = (f32[72,256]{1,0:T(8,128)S(1)}, f32[72,256]{1,0:T(8,128)S(1)}, u32[]{:S(2)}, u32[]{:S(2)}) collective-permute-start(f32[72,256]{1,0:T(8,128)S(1)} %get-tuple-element.75.refs_0_), channel_id=1, source_target_pairs={{0,2},{1,3},{2,0},{3,1},{4,6},{5,7},{6,4},{7,5},{8,10},{9,11},{10,... | collective-permute-start | bytes 221192 | tf_op jit(solution)/shard_map/ppermute | solution.py:483
  55.5 4.7 %collective-permute-start.12 = (f32[72,256]{1,0:T(8,128)S(1)}, f32[72,256]{1,0:T(8,128)S(1)}, u32[]{:S(2)}, u32[]{:S(2)}) collective-permute-start(f32[72,256]{1,0:T(8,128)S(1)} %get-tuple-element.75.refs_0_), channel_id=1, source_target_pairs={{0,1},{1,0},{2,3},{3,2},{4,5},{5,4},{6,7},{7,6},{8,9},{9,8},{10,11... | collective-permute-start | bytes 221192 | tf_op jit(solution)/shard_map/ppermute | solution.py:483
  60.9 7.0 %collective-permute-start.17 = (f32[72,256]{1,0:T(8,128)S(1)}, f32[72,256]{1,0:T(8,128)S(1)}, u32[]{:S(2)}, u32[]{:S(2)}) collective-permute-start(f32[72,256]{1,0:T(8,128)S(1)} %get-tuple-element.76.refs_0_), channel_id=1, source_target_pairs={{0,12},{4,8},{8,4},{12,0},{1,13},{5,9},{9,5},{13,1},{2,14},{6,10},... | collective-permute-start | bytes 221192 | tf_op jit(solution)/shard_map/ppermute | solution.py:483
  62.7 7.5 %collective-permute-start.16 = (f32[72,256]{1,0:T(8,128)S(1)}, f32[72,256]{1,0:T(8,128)S(1)}, u32[]{:S(2)}, u32[]{:S(2)}) collective-permute-start(f32[72,256]{1,0:T(8,128)S(1)} %get-tuple-element.76.refs_0_), channel_id=1, source_target_pairs={{0,8},{4,12},{8,0},{12,4},{1,9},{5,13},{9,1},{13,5},{2,10},{6,14},... | collective-permute-start | bytes 221192 | tf_op jit(solution)/shard_map/ppermute | solution.py:483
  62.7 7.5 %collective-permute-start.15 = (f32[72,256]{1,0:T(8,128)S(1)}, f32[72,256]{1,0:T(8,128)S(1)}, u32[]{:S(2)}, u32[]{:S(2)}) collective-permute-start(f32[72,256]{1,0:T(8,128)S(1)} %get-tuple-element.76.refs_0_), channel_id=1, source_target_pairs={{0,4},{4,0},{8,12},{12,8},{1,5},{5,1},{9,13},{13,9},{2,6},{6,2},{1... | collective-permute-start | bytes 221192 | tf_op jit(solution)/shard_map/ppermute | solution.py:483

commit v3 on v2

--- a/solution.py
+++ b/solution.py
@@ -17,6 +17,7 @@
 NT = (((1,), (1,)), ((), ()))
 SCALE = math.sqrt(0.5 * math.log2(math.e))
 STRIP = 256
+LANES = 128
 BLOCK = 256
 
 
@@ -28,7 +29,7 @@
     return not isinstance(shape, jax.ShapeDtypeStruct)
 
 
-def call(kernel, out_shape, args, anywhere=(), pinned=(), resident=(), scratch=(), name=None, cost=None):
+def call(kernel, out_shape, args, anywhere=(), pinned=(), resident=(), copied=False, scratch=(), name=None, cost=None):
     total = sum(a.size * a.dtype.itemsize for i, a in enumerate(args) if i not in anywhere)
     total += sum(math.prod(s.shape) * s.dtype.itemsize for s in out_shape)
     held = sum(a.size * a.dtype.itemsize for a in args if any(a is kept for kept in resident))
@@ -42,7 +43,7 @@
         kernel,
         out_shape=list(out_shape),
         in_specs=[ANY if i in anywhere else VMEM for i in range(len(args))],
-        out_specs=[VMEM] * len(out_shape),
+        out_specs=[ANY if copied else VMEM] * len(out_shape),
         scratch_shapes=list(scratch),
         compiler_params=pltpu.CompilerParams(vmem_limit_bytes=total - held + (6 << 20)),
         cost_estimate=cost,
@@ -130,24 +131,41 @@
     rows, pool = table.shape
     hit = lax.broadcasted_iota(jnp.int32, (pool, chosen.shape[1]), 0) == chosen
     onehot = jnp.where(hit, 1.0, 0.0).astype(BF16)
-    parts = [lax.dot_general(t, onehot, NN, preferred_element_type=F32) for t in split3(table)]
-    return parts[0] + parts[1] + parts[2]
-
-
-def to_rows(columns, width):
+    stacked = jnp.concatenate([t.astype(F32) for t in split3(table)], axis=0).astype(BF16)
+    parts = lax.dot_general(stacked, onehot, NN, preferred_element_type=F32)
+    return parts[:rows] + parts[rows : 2 * rows] + parts[2 * rows :]
+
+
+def write_wide(message, top, value):
+    rows = value.shape[0]
+    for k in range(value.shape[1] // LANES):
+        start = top + k * rows
+        message[start : start + rows, :] = value[:, k * LANES : (k + 1) * LANES]
+
+
+def read_wide(message, top, rows, rank):
+    starts = [top + k * rows for k in range(rank // LANES)]
+    return jnp.concatenate([message[start : start + rows, :] for start in starts], axis=1)
+
+
+def dots_at(rows, rank):
+    return rows * (rank // LANES)
+
+
+def message_rows(rows, rank, coords):
+    return dots_at(rows, rank) + 8 + (dots_at(8, rank) if coords else 0)
+
+
+def to_rows(columns):
     rows = columns[0].shape[0]
-    lane = lax.broadcasted_iota(jnp.int32, (rows, 128), 1)
-    block = jnp.zeros((rows, 128), F32)
-    for i, column in enumerate(columns):
-        block = jnp.where(lane == i, column, block)
-    if rows < 128:
-        block = jnp.concatenate([block, jnp.zeros((128 - rows, 128), F32)], axis=0)
-    flipped = block.T[:8]
-    return jnp.concatenate([flipped, jnp.zeros((8, width - 128), F32)], axis=1)
+    block = column_state(columns)
+    if rows < LANES:
+        block = jnp.concatenate([block, jnp.zeros((LANES - rows, LANES), F32)], axis=0)
+    return block.T[:8]
 
 
 def to_columns(block, rows):
-    square = jnp.concatenate([block[:, :128], jnp.zeros((120, 128), F32)], axis=0)
+    square = jnp.concatenate([block, jnp.zeros((120, 128), F32)], axis=0)
     return square.T[:rows]
 
 
@@ -180,7 +198,9 @@
     shift = low_end + 0.5 * (jnp.max(points, axis=1, keepdims=True) - low_end)
     chosen = pick(points, skel[...])
     rows = rhs.shape[0]
-    message[rows + 8 :, :] = chosen
+    rank = chosen.shape[1]
+    dots = dots_at(rows, rank)
+    write_wide(message, dots + 8, chosen)
     scaled = (points - shift) * inverse
     unit = unit_of(scaled)
     (la[...], lb[...]), (ra[...], rb[...]) = features(scaled, unit)
@@ -192,15 +212,14 @@
         basis_l[strip, :] = low
     copies[1].wait()
     value = rhs[...]
-    message[:rows, :] = dot3(value, basis_h[...], basis_l[...])
-    message[rows : rows + 8, :] = to_rows([row_sum(value * value)], chosen.shape[1])
+    write_wide(message, 0, dot3(value, basis_h[...], basis_l[...]))
+    message[dots : dots + 8, :] = to_rows([row_sum(value * value)])
     copies[3].wait()
     copies[5].wait()
     params[...] = column_state(
         [inverse, shift, jnp.broadcast_to(noise[...], (8, 1)), jnp.broadcast_to(unit, (8, 1))]
     )
     number = lax.axis_index("leaf") * anchors + lax.axis_index("sub")
-    rank = keep.shape[1]
     slot = 0
     for base, bits in stages:
         for level in range(1, bits + 1):
@@ -315,11 +334,20 @@
     return coords
 
 
-def add_rows(messages, rows):
-    total = messages[0][rows : rows + 8, :]
+def add_dots(messages, rows, rank):
+    dots = slice(dots_at(rows, rank), dots_at(rows, rank) + 8)
+    total = messages[0][dots, :]
     for message in messages[1:]:
-        total = total + message[rows : rows + 8, :]
+        total = total + message[dots, :]
     return total
+
+
+def coords_of(messages, rows, rank):
+    return [read_wide(m, dots_at(rows, rank) + 8, 8, rank) for m in messages]
+
+
+def weights_of(messages, rows, rank):
+    return [read_wide(m, 0, rows, rank) for m in messages]
 
 
 def lower_first_kernel(rows, count, offset, refs):
@@ -327,21 +355,24 @@
     params, chosen = refs[count : count + 2]
     message, terms, transfer_h, transfer_l, couple_h, couple_l = refs[-6:]
     transfer, couple = (transfer_h, transfer_l), (couple_h, couple_l)
-    coords = [m[rows + 8 :, :] for m in messages]
+    rank = couple_h.shape[2]
+    coords = coords_of(messages, rows, rank)
     picks = chosen[offset : offset + count - 1, :]
     coords = build_tree(coords, picks, params, transfer, couple, True)
     lower_finish(rows, messages, message, terms, transfer, couple, True)
-    message[rows + 8 :, :] = coords[0]
+    write_wide(message, dots_at(rows, rank) + 8, coords[0])
 
 
 def lower_finish(rows, messages, message, terms, transfer, couple, top):
-    weights, own_terms, energy = sweep_up([m[:rows, :] for m in messages], transfer, couple, top)
+    rank = couple[0].shape[2]
+    weights = weights_of(messages, rows, rank)
+    weights, own_terms, energy = sweep_up(weights, transfer, couple, top)
     for i, term in enumerate(own_terms):
         terms[i] = term
-    dots = add_rows(messages, rows)
-    message[:rows, :] = weights[0]
-    extra = to_rows([jnp.zeros_like(energy)] * 7 + [energy], dots.shape[1])
-    message[rows : rows + 8, :] = dots + extra
+    write_wide(message, 0, weights[0])
+    dots = dots_at(rows, rank)
+    extra = to_rows([jnp.zeros_like(energy)] * 7 + [energy])
+    message[dots : dots + 8, :] = add_dots(messages, rows, rank) + extra
 
 
 def lower_kernel(rows, count, top, refs):
@@ -356,23 +387,54 @@
 def upper_build(rows, count, offset, refs):
     messages = refs[:count]
     params, chosen, transfer_h, transfer_l, couple_h, couple_l = refs[count:]
-    coords = [m[rows + 8 :, :] for m in messages]
+    coords = coords_of(messages, rows, couple_h.shape[2])
     picks = chosen[offset : offset + count - 1, :]
     build_tree(
         coords, picks, params, (transfer_h, transfer_l), (couple_h, couple_l), False
     )
 
 
-def far_field(rows, messages, upper, lower):
+def own_chain(upper, lower):
+    halves = []
+    for high, low, count in lower + [upper]:
+        slots = tree_slots(count)
+        half = high.shape[2]
+        for level in range(1, levels_of(count) + 1):
+            slot = slots[level, 0]
+            halves.append((high[slot, :half], low[slot, :half]))
+    return halves[:-1]
+
+
+def compose_kernel(counts, refs):
+    high_out, low_out = refs[-2:]
+    trees = [(refs[2 * i], refs[2 * i + 1], count) for i, count in enumerate(counts)]
+    chain = own_chain(trees[-1], trees[:-1])
+    rank = chain[0][0].shape[0]
+    high, low = chain[0]
+    for i in range(len(chain)):
+        if i:
+            product = high.astype(F32) + low.astype(F32)
+            high, low = split(dot3(product, *chain[i]))
+        high_out[:, i * rank : (i + 1) * rank] = high
+        low_out[:, i * rank : (i + 1) * rank] = low
+
+
+def far_field(rows, messages, upper, lower, path=None):
     count = len(messages)
-    weights = [m[:rows, :] for m in messages]
+    rank = upper[2].shape[2]
+    weights = weights_of(messages, rows, rank)
     _, own_terms, energy = sweep_up(weights, upper[:2], upper[2:], False)
-    search = sweep_down(None, own_terms, upper[:2], count)
-    for terms, high, low in reversed(lower):
-        depth = terms.shape[0]
-        own_terms = [terms[i] for i in range(depth)]
-        search = sweep_down(search, own_terms, (high, low), 1 << depth)
-    sums = to_columns(add_rows(messages, rows), rows)
+    sums = to_columns(add_dots(messages, rows, rank), rows)
+    if path is None:
+        search = sweep_down(None, own_terms, upper[:2], count)
+        for terms, high, low in reversed(lower):
+            depth = terms.shape[0]
+            below = [terms[i] for i in range(depth)]
+            search = sweep_down(search, below, (high, low), 1 << depth)
+    else:
+        below = [terms[i] for terms in lower for i in range(terms.shape[0])]
+        search, *above = below + own_terms
+        search = search + dot3(jnp.concatenate(above, axis=1), path[0][...], path[1][...], NT)
     return search, sums, sums[:, 7:8] + energy
 
 
@@ -403,6 +465,11 @@
     messages, lower, upper, basis, rest = take_refs(refs, count, 3 * stages, 4, 2)
     lower = [lower[i : i + 3] for i in range(0, 3 * stages, 3)]
     return far_field(rows, messages, upper, lower), basis, rest
+
+
+def open_composed(rows, count, stages, refs):
+    messages, terms, upper, path, basis, rest = take_refs(refs, count, stages, 4, 2, 2)
+    return far_field(rows, messages, upper, terms, path), basis, rest
 
 
 def dense_parts(refs):
@@ -419,16 +486,16 @@
     rate = norm / (params[0:1, 2:3] * norm + jnp.abs(far))
     q = rate * (near_b + dot3(search, basis[0][...], basis[1][...], NT))
     q_out[...] = q
-    message[:rows, :] = dot3(q, basis[0][...], basis[1][...])
+    write_wide(message, 0, dot3(q, basis[0][...], basis[1][...]))
     near_q = near_field(q, params, dense_parts(dense))
     near_out[...] = near_q
     dots = [row_sum(rhs[...] * q), row_sum(q * q), row_sum(q * near_q)]
-    message[rows:, :] = to_rows(dots, message.shape[1])
+    message[message.shape[0] - 8 :, :] = to_rows(dots)
     state[...] = column_state([norm, rate])
 
 
 def second_kernel(rows, count, stages, parts, refs):
-    (search, sums, far), basis, rest = open_refs(rows, count, stages, refs)
+    (search, sums, far), basis, rest = open_composed(rows, count, stages, refs)
     dense, rest = take_refs(rest, 2 * parts)
     params, rhs, q_in, near_in, state_in = rest[:5]
     message, x_out, r_out, d_out, q_out, near_out, state = rest[5:]
@@ -454,26 +521,32 @@
     r_out[...] = r2
     d_out[...] = d1
     q_out[...] = q1
-    message[:rows, :] = dot3(r2, basis[0][...], basis[1][...])
+    write_wide(message, 0, dot3(r2, basis[0][...], basis[1][...]))
     near = near_field(r2, params, dense_parts(dense))
     near_out[...] = near
     dots = [row_sum(r2 * r2), row_sum(r2 * q1), row_sum(r2 * near)]
-    message[rows:, :] = to_rows(dots, message.shape[1])
+    message[message.shape[0] - 8 :, :] = to_rows(dots)
     state[...] = column_state([norm1, curve])
 
 
 def last_kernel(rows, count, stages, refs):
-    (search, sums, far), basis, rest = open_refs(rows, count, stages, refs)
-    x_in, r_in, d_in, q_in, near_in, state_in, x_out, r_out = rest
+    (search, sums, far), basis, rest = open_composed(rows, count, stages, refs)
+    x_in, r_in, d_in, q_in, near_in, state_in, x_out, r_out, x_done, r_done, sems = rest
     norm1, curve1 = state_in[:, 0:1], state_in[:, 1:2]
     norm2, cross, rar = sums[:, 0:1], sums[:, 1:2], sums[:, 2:3] + far
     beta = norm2 / norm1
     curve = rar + 2.0 * beta * cross + beta * beta * curve1
     alpha = norm2 / curve
+    r2 = r_in[...]
+    x_done[...] = x_in[...] + alpha * (r2 + beta * d_in[...])
+    x_copy = pltpu.make_async_copy(x_done, x_out, sems.at[0])
+    x_copy.start()
     image = near_in[...] + dot3(search, basis[0][...], basis[1][...], NT) + beta * q_in[...]
-    r2 = r_in[...]
-    x_out[...] = x_in[...] + alpha * (r2 + beta * d_in[...])
-    r_out[...] = r2 - alpha * image
+    r_done[...] = r2 - alpha * image
+    r_copy = pltpu.make_async_copy(r_done, r_out, sems.at[1])
+    r_copy.start()
+    x_copy.wait()
+    r_copy.wait()
 
 
 def gather(value, stage):
@@ -510,7 +583,7 @@
     message, rhs, la, lb, ra, rb, basis_h, basis_l, chosen, params = call(
         functools.partial(setup_kernel, bases, total, subs),
         [
-            f32_shape(rows + 16, rank),
+            f32_shape(message_rows(rows, rank, True), LANES),
             f32_shape(rows, size),
             bf16_shape(size, 16),
             bf16_shape(size, 80),
@@ -572,7 +645,7 @@
             extra = near_parts[:1]
         message, terms, *tree = call(
             refs_of(lower_first_kernel, rows, counts[i], offsets[i]),
-            [f32_shape(rows + 16, rank), f32_shape(bases[i][1], rows, rank)]
+            [f32_shape(message_rows(rows, rank, True), LANES), f32_shape(bases[i][1], rows, rank)]
             + tree_shapes(counts[i]),
             messages + [params, chosen] + extra,
             name="lower_first",
@@ -590,15 +663,18 @@
 
     state_shape = f32_shape(rows, 128)
     vector = f32_shape(rows, size)
-    message_shape = f32_shape(rows + 8, rank)
+    message_shape = f32_shape(message_rows(rows, rank, False), LANES)
 
     def lower_of(terms_all):
         return [a for terms, tree in zip(terms_all, trees) for a in (terms, tree[0], tree[1])]
 
-    def exchange(message):
+    def exchange(message, shadow=None):
         terms_all = []
+        made = None
         for i in range(stage_count):
             messages = gather(message, hops[i])
+            if i == 0 and shadow is not None:
+                made = shadow()
             message, terms = call(
                 refs_of(lower_kernel, rows, counts[i], True),
                 [message_shape, f32_shape(bases[i][1], rows, rank)],
@@ -606,7 +682,7 @@
                 name="lower",
             )
             terms_all.append(terms)
-        return gather(message, hops[-1]) + lower_of(terms_all)
+        return gather(message, hops[-1]) + terms_all, made
 
     fixed = (rows, counts[-1], stage_count)
     message, q, near, state = call(
@@ -616,20 +692,37 @@
         resident=dense,
         name="first",
     )
-    arrived = exchange(message)
+
+    def compose():
+        pairs = [a for tree in trees + [upper] for a in tree[:2]]
+        return call(
+            refs_of(compose_kernel, counts),
+            [bf16_shape(rank, (total - 1) * rank)] * 2,
+            pairs + [state],
+            cost=(12 * rank * rank * rank, 0),
+            name="compose",
+        )
+
+    arrived, path = exchange(message, compose)
     message, x, r, d, q, near, state = call(
         refs_of(second_kernel, *fixed, len(widths)),
         [message_shape, vector, vector, vector, vector, vector, state_shape],
-        arrived + upper + basis + dense + [params, rhs, q, near, state],
+        arrived + upper + path + basis + dense + [params, rhs, q, near, state],
         resident=dense,
         name="second",
     )
-    arrived = exchange(message)
+    arrived, _ = exchange(message)
     return tuple(
         call(
             refs_of(last_kernel, *fixed),
             [vector, vector],
-            arrived + upper + basis + [x, r, d, q, near, state],
+            arrived + upper + path + basis + [x, r, d, q, near, state],
+            copied=True,
+            scratch=[
+                pltpu.VMEM((rows, size), F32),
+                pltpu.VMEM((rows, size), F32),
+                pltpu.SemaphoreType.DMA((2,)),
+            ],
             name="last",
         )
     )

time: 73.1 us -> 71.8 us (0.982)
  waiting for transfers between devices: 19.1 us -> 17.5 us
    ppermute x18, waiting for transfers between devices: 19.1 us -> 17.5 us  [gather(): return [value] + [lax.ppermute(value, axis, pair) for pair in pairs]]
    pallas_call x10 -> x11, Pallas kernels: 31.8 us -> 32 us  [call(): pl.pallas_call(kernel, out_shape=list(out_shape), in_specs=[ANY if i in a...]
  transfers between devices with their start and end apart: 18 -> 18, of which waited for: 10 -> 9; matrix products, arithmetic and copies ran while one was open for 0% -> 0% of each run, Pallas kernels for 14% -> 15%
where the time goes in v3:
time: 71.8 us; the launch traced here: 71.6 us
  Pallas kernels  32 us (45%)
  starting transfers between devices  20.6 us (29%)
  waiting for transfers between devices  17.5 us (24%)
  between operations  1.54 us (2%)
    pallas_call x11, Pallas kernels, call(): pl.pallas_call(kernel, out_shape=list(out_shape), in_specs=[ANY if i in a...  32 us
    ppermute x18, starting transfers between devices, gather(): return [value] + [lax.ppermute(value, axis, pair) for pair in pairs]  20.6 us
    ppermute x18, waiting for transfers between devices, gather(): return [value] + [lax.ppermute(value, axis, pair) for pair in pairs]  17.5 us
  transfers between devices with their start and end apart: 18, of which 9 were waited for; matrix products, arithmetic and copies ran while one was open for 0% of the time, Pallas kernels for 15%

profile of v3, /device:TPU:0, one launch (start us, length us, event | category | flops | bytes accessed | tf_op | source)
XLA Modules:
  0.0 71.6 jit_solution(7903029490980557517)
XLA Ops:
  1.3 3.3 %setup.1 = (f32[152,128]{1,0:T(8,128)S(1)}, f32[64,2048]{1,0:T(8,128)S(1)}, bf16[2048,16]{1,0:T(8,128)(2,1)S(1)}, bf16[2048,80]{1,0:T(8,128)(2,1)S(1)}, bf16[16,...) custom-call(f32[6,2048]{1,0:T(8,128)} %refs_0_.1, ...), custom_call_target="tpu_custom_call" | custom-call | tf_op jit(solution)/shard_map/setup/pallas_call | solution.py:42
  4.5 2.4 %collective-permute-start.2 = (f32[152,128]{1,0:T(8,128)S(1)}, f32[152,128]{1,0:T(8,128)S(1)}, u32[]{:S(2)}, u32[]{:S(2)}) collective-permute-start(f32[152,128]{1,0:T(8,128)S(1)} %get-tuple-element.45.refs_0_), channel_id=1, source_target_pairs={{0,3},{1,2},{2,1},{3,0},{4,7},{5,6},{6,5},{7,4},{8,11},{9,10},{10,... | collective-permute-start | bytes 233480 | tf_op jit(solution)/shard_map/ppermute | solution.py:556
  7.7 4.2 %dense.2 = (bf16[2048,768]{1,0:T(8,128)(2,1)S(1)}, bf16[2048,768]{1,0:T(8,128)(2,1)S(1)}, f32[64,768]{1,0:T(8,128)S(1)}) custom-call(bf16[2048,16]{1,0:T(8,128)(2,1)S(1)} %get-tuple-element.48.la, bf16[2048,80]{1,0:T(8,128)(2,1)S(1)} %get-tuple-element.49.lb, bf16[16,2048]{1,0:T(8,128)(2,1)S(1)} %get-tuple-element.50.ra, ...), custom_call_target="tpu_custom_call" | custom-call | flops 905969664 | bytes 7806976 | tf_op jit(solution)/shard_map/dense/pallas_call | solution.py:42
  11.9 2.2 %lower_first.1 = (f32[152,128]{1,0:T(8,128)S(1)}, f32[2,64,256]{2,1,0:T(8,128)S(1)}, bf16[3,512,256]{2,1,0:T(8,128)(2,1)S(1)}, bf16[3,512,256]{2,1,0:T(8,128)(2,...) custom-call(f32[152,128]{1,0:T(8,128)S(1)} %get-tuple-element.45.refs_0_, ...), custom_call_target="tpu_custom_call" | custom-call | tf_op jit(solution)/shard_map/lower_first/pallas_call | solution.py:42
  14.1 4.1 %collective-permute-start.5 = (f32[152,128]{1,0:T(8,128)S(1)}, f32[152,128]{1,0:T(8,128)S(1)}, u32[]{:S(2)}, u32[]{:S(2)}) collective-permute-start(f32[152,128]{1,0:T(8,128)S(1)} %get-tuple-element.54.refs_0_.tie), channel_id=1, source_target_pairs={{0,12},{4,8},{8,4},{12,0},{1,13},{5,9},{9,5},{13,1},{2,14},{6,10},... | collective-permute-start | bytes 233480 | tf_op jit(solution)/shard_map/ppermute | solution.py:556
  18.9 6.1 %dense.3 = (bf16[2048,1280]{1,0:T(8,128)(2,1)S(1)}, bf16[2048,1280]{1,0:T(8,128)(2,1)S(1)}, f32[64,1280]{1,0:T(8,128)S(1)}) custom-call(bf16[2048,16]{1,0:T(8,128)(2,1)S(1)} %get-tuple-element.48.la, bf16[2048,80]{1,0:T(8,128)(2,1)S(1)} %get-tuple-element.49.lb, bf16[16,2048]{1,0:T(8,128)(2,1)S(1)} %get-tuple-element.50.ra, ...), custom_call_target="tpu_custom_call" | custom-call | flops 1509949440 | bytes 12206080 | tf_op jit(solution)/shard_map/dense/pallas_call | solution.py:42
  25.0 1.3 %upper_build.1 = (bf16[3,512,256]{2,1,0:T(8,128)(2,1)S(1)}, bf16[3,512,256]{2,1,0:T(8,128)(2,1)S(1)}, bf16[3,256,256]{2,1,0:T(8,128)(2,1)S(1)}, bf16[3,256,256]{2,1,0:T(8,128)(2,1)S(1)}) custom-call(f32[152,128]{1,0:T(8,128)S(1)} %get-tuple-element.54.refs_0_.tie, f32[152,128]{1,0:T(8,128)S(1)} %collective-permute-done.3.refs_1_, ...), custom_call_target="tpu_custom_call" | custom-call | tf_op jit(solution)/shard_map/upper_build/pallas_call | solution.py:42
  26.3 5.0 %first.1 = (f32[136,128]{1,0:T(8,128)S(1)}, f32[64,2048]{1,0:T(8,128)S(1)}, f32[64,2048]{1,0:T(8,128)S(1)}, f32[64,128]{1,0:T(8,128)S(1)}) custom-call(f32[152,128]{1,0:T(8,128)S(1)} %get-tuple-element.54.refs_0_.tie, f32[152,128]{1,0:T(8,128)S(1)} %collective-permute-done.3.refs_1_, f32[152,128]{1,0:T(8,128)S(1)} %collective-permute-done.4.refs_2_, ...), custom_call_target="tpu_custom_call" | custom-call | tf_op jit(solution)/shard_map/first/pallas_call | solution.py:42
  32.0 1.1 %collective-permute-start.7 = (f32[136,128]{1,0:T(8,128)S(1)}, f32[136,128]{1,0:T(8,128)S(1)}, u32[]{:S(2)}, u32[]{:S(2)}) collective-permute-start(f32[136,128]{1,0:T(8,128)S(1)} %get-tuple-element.69.refs_0_), channel_id=1, source_target_pairs={{0,2},{1,3},{2,0},{3,1},{4,6},{5,7},{6,4},{7,5},{8,10},{9,11},{10,... | collective-permute-start | bytes 208904 | tf_op jit(solution)/shard_map/ppermute | solution.py:556
  33.2 2.4 %collective-permute-done.8.refs_3_ = f32[136,128]{1,0:T(8,128)S(1)} collective-permute-done((f32[136,128]{1,0:T(8,128)S(1)}, f32[136,128]{1,0:T(8,128)S(1)}, u32[]{:S(2)}, u32[]{:S(2)}) %collective-permute-start.8) | collective-permute-done | bytes 69664 | tf_op jit(solution)/shard_map/ppermute | solution.py:556
  35.7 1.7 %collective-permute-done.7.refs_2_ = f32[136,128]{1,0:T(8,128)S(1)} collective-permute-done((f32[136,128]{1,0:T(8,128)S(1)}, f32[136,128]{1,0:T(8,128)S(1)}, u32[]{:S(2)}, u32[]{:S(2)}) %collective-permute-start.7) | collective-permute-done | bytes 69664 | tf_op jit(solution)/shard_map/ppermute | solution.py:556
  38.1 3.8 %collective-permute-start.11 = (f32[136,128]{1,0:T(8,128)S(1)}, f32[136,128]{1,0:T(8,128)S(1)}, u32[]{:S(2)}, u32[]{:S(2)}) collective-permute-start(f32[136,128]{1,0:T(8,128)S(1)} %get-tuple-element.72.refs_0_), channel_id=1, source_target_pairs={{0,12},{4,8},{8,4},{12,0},{1,13},{5,9},{9,5},{13,1},{2,14},{6,10},... | collective-permute-start | bytes 208904 | tf_op jit(solution)/shard_map/ppermute | solution.py:556
  43.2 1.8 %collective-permute-done.11.refs_3_ = f32[136,128]{1,0:T(8,128)S(1)} collective-permute-done((f32[136,128]{1,0:T(8,128)S(1)}, f32[136,128]{1,0:T(8,128)S(1)}, u32[]{:S(2)}, u32[]{:S(2)}) %collective-permute-start.11) | collective-permute-done | bytes 69664 | tf_op jit(solution)/shard_map/ppermute | solution.py:556
  45.0 2.8 %collective-permute-done.10.refs_2_ = f32[136,128]{1,0:T(8,128)S(1)} collective-permute-done((f32[136,128]{1,0:T(8,128)S(1)}, f32[136,128]{1,0:T(8,128)S(1)}, u32[]{:S(2)}, u32[]{:S(2)}) %collective-permute-start.10) | collective-permute-done | bytes 69664 | tf_op jit(solution)/shard_map/ppermute | solution.py:556
  47.8 5.2 %second.1 = (f32[136,128]{1,0:T(8,128)S(1)}, f32[64,2048]{1,0:T(8,128)S(1)}, f32[64,2048]{1,0:T(8,128)S(1)}, f32[64,2048]{1,0:T(8,128)S(1)}, f32[64,2048]{1,0:T(...) custom-call(f32[136,128]{1,0:T(8,128)S(1)} %get-tuple-element.72.refs_0_, ...), custom_call_target="tpu_custom_call" | custom-call | tf_op jit(solution)/shard_map/second/pallas_call | solution.py:42
  53.1 1.3 %collective-permute-start.13 = (f32[136,128]{1,0:T(8,128)S(1)}, f32[136,128]{1,0:T(8,128)S(1)}, u32[]{:S(2)}, u32[]{:S(2)}) collective-permute-start(f32[136,128]{1,0:T(8,128)S(1)} %get-tuple-element.79.refs_0_), channel_id=1, source_target_pairs={{0,2},{1,3},{2,0},{3,1},{4,6},{5,7},{6,4},{7,5},{8,10},{9,11},{10,... | collective-permute-start | bytes 208904 | tf_op jit(solution)/shard_map/ppermute | solution.py:556
  54.9 2.6 %collective-permute-done.14.refs_3_ = f32[136,128]{1,0:T(8,128)S(1)} collective-permute-done((f32[136,128]{1,0:T(8,128)S(1)}, f32[136,128]{1,0:T(8,128)S(1)}, u32[]{:S(2)}, u32[]{:S(2)}) %collective-permute-start.14) | collective-permute-done | bytes 69664 | tf_op jit(solution)/shard_map/ppermute | solution.py:556
  57.5 1.5 %collective-permute-done.13.refs_2_ = f32[136,128]{1,0:T(8,128)S(1)} collective-permute-done((f32[136,128]{1,0:T(8,128)S(1)}, f32[136,128]{1,0:T(8,128)S(1)}, u32[]{:S(2)}, u32[]{:S(2)}) %collective-permute-start.13) | collective-permute-done | bytes 69664 | tf_op jit(solution)/shard_map/ppermute | solution.py:556
  59.0 0.8 %lower.3 = (f32[136,128]{1,0:T(8,128)S(1)}, f32[2,64,256]{2,1,0:T(8,128)S(1)}) custom-call(f32[136,128]{1,0:T(8,128)S(1)} %get-tuple-element.79.refs_0_, f32[136,128]{1,0:T(8,128)S(1)} %collective-permute-done.12.refs_1_, f32[136,128]{1,0:T(8,128)S(1)} %collective-permute-done.13.refs_2_, f32[136,128]{1,0:T(8,128)S(1)} %collective-permute-done.14.refs_3_, ...), custom_call_target="tpu_custom_call" | custom-call | tf_op jit(solution)/shard_map/lower/pallas_call | solution.py:42
  59.7 1.8 %collective-permute-start.17 = (f32[136,128]{1,0:T(8,128)S(1)}, f32[136,128]{1,0:T(8,128)S(1)}, u32[]{:S(2)}, u32[]{:S(2)}) collective-permute-start(f32[136,128]{1,0:T(8,128)S(1)} %get-tuple-element.80.refs_0_), channel_id=1, source_target_pairs={{0,12},{4,8},{8,4},{12,0},{1,13},{5,9},{9,5},{13,1},{2,14},{6,10},... | collective-permute-start | bytes 208904 | tf_op jit(solution)/shard_map/ppermute | solution.py:556
  61.7 2.5 %collective-permute-start.15 = (f32[136,128]{1,0:T(8,128)S(1)}, f32[136,128]{1,0:T(8,128)S(1)}, u32[]{:S(2)}, u32[]{:S(2)}) collective-permute-start(f32[136,128]{1,0:T(8,128)S(1)} %get-tuple-element.80.refs_0_), channel_id=1, source_target_pairs={{0,4},{4,0},{8,12},{12,8},{1,5},{5,1},{9,13},{13,9},{2,6},{6,2},{1... | collective-permute-start | bytes 208904 | tf_op jit(solution)/shard_map/ppermute | solution.py:556
  64.2 2.5 %collective-permute-done.17.refs_3_ = f32[136,128]{1,0:T(8,128)S(1)} collective-permute-done((f32[136,128]{1,0:T(8,128)S(1)}, f32[136,128]{1,0:T(8,128)S(1)}, u32[]{:S(2)}, u32[]{:S(2)}) %collective-permute-start.17) | collective-permute-done | bytes 69664 | tf_op jit(solution)/shard_map/ppermute | solution.py:556
  66.7 2.1 %collective-permute-done.16.refs_2_ = f32[136,128]{1,0:T(8,128)S(1)} collective-permute-done((f32[136,128]{1,0:T(8,128)S(1)}, f32[136,128]{1,0:T(8,128)S(1)}, u32[]{:S(2)}, u32[]{:S(2)}) %collective-permute-start.16) | collective-permute-done | bytes 69664 | tf_op jit(solution)/shard_map/ppermute | solution.py:556
  68.8 2.7 %last.1 = (f32[64,2048]{1,0:T(8,128)}, f32[64,2048]{1,0:T(8,128)}) custom-call(f32[136,128]{1,0:T(8,128)S(1)} %get-tuple-element.80.refs_0_, f32[136,128]{1,0:T(8,128)S(1)} %collective-permute-done.15.refs_1_, f32[136,128]{1,0:T(8,128)S(1)} %collective-permute-done.16.refs_2_, f32[136,128]{1,0:T(8,128)S(1)} %collective-permute-done.17.refs_3_, ...), custom_call_target="tpu_custom_call" | custom-call | tf_op jit(solution)/shard_map/last/pallas_call | solution.py:42
  (23 shorter events, 4.9 us)
Async XLA Ops:
  4.5 7.3 %collective-permute-start.2 = (f32[152,128]{1,0:T(8,128)S(1)}, f32[152,128]{1,0:T(8,128)S(1)}, u32[]{:S(2)}, u32[]{:S(2)}) collective-permute-start(f32[152,128]{1,0:T(8,128)S(1)} %get-tuple-element.45.refs_0_), channel_id=1, source_target_pairs={{0,3},{1,2},{2,1},{3,0},{4,7},{5,6},{6,5},{7,4},{8,11},{9,10},{10,... | collective-permute-start | bytes 233480 | tf_op jit(solution)/shard_map/ppermute | solution.py:556
  7.0 4.9 %collective-permute-start.1 = (f32[152,128]{1,0:T(8,128)S(1)}, f32[152,128]{1,0:T(8,128)S(1)}, u32[]{:S(2)}, u32[]{:S(2)}) collective-permute-start(f32[152,128]{1,0:T(8,128)S(1)} %get-tuple-element.45.refs_0_), channel_id=1, source_target_pairs={{0,2},{1,3},{2,0},{3,1},{4,6},{5,7},{6,4},{7,5},{8,10},{9,11},{10,... | collective-permute-start | bytes 233480 | tf_op jit(solution)/shard_map/ppermute | solution.py:556
  7.6 4.3 %collective-permute-start = (f32[152,128]{1,0:T(8,128)S(1)}, f32[152,128]{1,0:T(8,128)S(1)}, u32[]{:S(2)}, u32[]{:S(2)}) collective-permute-start(f32[152,128]{1,0:T(8,128)S(1)} %get-tuple-element.45.refs_0_), channel_id=1, source_target_pairs={{0,1},{1,0},{2,3},{3,2},{4,5},{5,4},{6,7},{7,6},{8,9},{9,8},{10,11... | collective-permute-start | bytes 233480 | tf_op jit(solution)/shard_map/ppermute | solution.py:556
  14.1 10.9 %collective-permute-start.5 = (f32[152,128]{1,0:T(8,128)S(1)}, f32[152,128]{1,0:T(8,128)S(1)}, u32[]{:S(2)}, u32[]{:S(2)}) collective-permute-start(f32[152,128]{1,0:T(8,128)S(1)} %get-tuple-element.54.refs_0_.tie), channel_id=1, source_target_pairs={{0,12},{4,8},{8,4},{12,0},{1,13},{5,9},{9,5},{13,1},{2,14},{6,10},... | collective-permute-start | bytes 233480 | tf_op jit(solution)/shard_map/ppermute | solution.py:556
  18.3 6.8 %collective-permute-start.4 = (f32[152,128]{1,0:T(8,128)S(1)}, f32[152,128]{1,0:T(8,128)S(1)}, u32[]{:S(2)}, u32[]{:S(2)}) collective-permute-start(f32[152,128]{1,0:T(8,128)S(1)} %get-tuple-element.54.refs_0_.tie), channel_id=1, source_target_pairs={{0,8},{4,12},{8,0},{12,4},{1,9},{5,13},{9,1},{13,5},{2,10},{6,14},... | collective-permute-start | bytes 233480 | tf_op jit(solution)/shard_map/ppermute | solution.py:556
  18.3 6.8 %collective-permute-start.3 = (f32[152,128]{1,0:T(8,128)S(1)}, f32[152,128]{1,0:T(8,128)S(1)}, u32[]{:S(2)}, u32[]{:S(2)}) collective-permute-start(f32[152,128]{1,0:T(8,128)S(1)} %get-tuple-element.54.refs_0_.tie), channel_id=1, source_target_pairs={{0,4},{4,0},{8,12},{12,8},{1,5},{5,1},{9,13},{13,9},{2,6},{6,2},{1... | collective-permute-start | bytes 233480 | tf_op jit(solution)/shard_map/ppermute | solution.py:556
  31.3 4.3 %collective-permute-start.8 = (f32[136,128]{1,0:T(8,128)S(1)}, f32[136,128]{1,0:T(8,128)S(1)}, u32[]{:S(2)}, u32[]{:S(2)}) collective-permute-start(f32[136,128]{1,0:T(8,128)S(1)} %get-tuple-element.69.refs_0_), channel_id=1, source_target_pairs={{0,3},{1,2},{2,1},{3,0},{4,7},{5,6},{6,5},{7,4},{8,11},{9,10},{10,... | collective-permute-start | bytes 208904 | tf_op jit(solution)/shard_map/ppermute | solution.py:556
  32.0 5.3 %collective-permute-start.7 = (f32[136,128]{1,0:T(8,128)S(1)}, f32[136,128]{1,0:T(8,128)S(1)}, u32[]{:S(2)}, u32[]{:S(2)}) collective-permute-start(f32[136,128]{1,0:T(8,128)S(1)} %get-tuple-element.69.refs_0_), channel_id=1, source_target_pairs={{0,2},{1,3},{2,0},{3,1},{4,6},{5,7},{6,4},{7,5},{8,10},{9,11},{10,... | collective-permute-start | bytes 208904 | tf_op jit(solution)/shard_map/ppermute | solution.py:556
  33.1 4.3 %collective-permute-start.6 = (f32[136,128]{1,0:T(8,128)S(1)}, f32[136,128]{1,0:T(8,128)S(1)}, u32[]{:S(2)}, u32[]{:S(2)}) collective-permute-start(f32[136,128]{1,0:T(8,128)S(1)} %get-tuple-element.69.refs_0_), channel_id=1, source_target_pairs={{0,1},{1,0},{2,3},{3,2},{4,5},{5,4},{6,7},{7,6},{8,9},{9,8},{10,11... | collective-permute-start | bytes 208904 | tf_op jit(solution)/shard_map/ppermute | solution.py:556
  38.1 6.9 %collective-permute-start.11 = (f32[136,128]{1,0:T(8,128)S(1)}, f32[136,128]{1,0:T(8,128)S(1)}, u32[]{:S(2)}, u32[]{:S(2)}) collective-permute-start(f32[136,128]{1,0:T(8,128)S(1)} %get-tuple-element.72.refs_0_), channel_id=1, source_target_pairs={{0,12},{4,8},{8,4},{12,0},{1,13},{5,9},{9,5},{13,1},{2,14},{6,10},... | collective-permute-start | bytes 208904 | tf_op jit(solution)/shard_map/ppermute | solution.py:556
  41.9 5.9 %collective-permute-start.10 = (f32[136,128]{1,0:T(8,128)S(1)}, f32[136,128]{1,0:T(8,128)S(1)}, u32[]{:S(2)}, u32[]{:S(2)}) collective-permute-start(f32[136,128]{1,0:T(8,128)S(1)} %get-tuple-element.72.refs_0_), channel_id=1, source_target_pairs={{0,8},{4,12},{8,0},{12,4},{1,9},{5,13},{9,1},{13,5},{2,10},{6,14},... | collective-permute-start | bytes 208904 | tf_op jit(solution)/shard_map/ppermute | solution.py:556
  41.9 5.9 %collective-permute-start.9 = (f32[136,128]{1,0:T(8,128)S(1)}, f32[136,128]{1,0:T(8,128)S(1)}, u32[]{:S(2)}, u32[]{:S(2)}) collective-permute-start(f32[136,128]{1,0:T(8,128)S(1)} %get-tuple-element.72.refs_0_), channel_id=1, source_target_pairs={{0,4},{4,0},{8,12},{12,8},{1,5},{5,1},{9,13},{13,9},{2,6},{6,2},{1... | collective-permute-start | bytes 208904 | tf_op jit(solution)/shard_map/ppermute | solution.py:556
  53.0 4.5 %collective-permute-start.14 = (f32[136,128]{1,0:T(8,128)S(1)}, f32[136,128]{1,0:T(8,128)S(1)}, u32[]{:S(2)}, u32[]{:S(2)}) collective-permute-start(f32[136,128]{1,0:T(8,128)S(1)} %get-tuple-element.79.refs_0_), channel_id=1, source_target_pairs={{0,3},{1,2},{2,1},{3,0},{4,7},{5,6},{6,5},{7,4},{8,11},{9,10},{10,... | collective-permute-start | bytes 208904 | tf_op jit(solution)/shard_map/ppermute | solution.py:556
  53.1 5.9 %collective-permute-start.13 = (f32[136,128]{1,0:T(8,128)S(1)}, f32[136,128]{1,0:T(8,128)S(1)}, u32[]{:S(2)}, u32[]{:S(2)}) collective-permute-start(f32[136,128]{1,0:T(8,128)S(1)} %get-tuple-element.79.refs_0_), channel_id=1, source_target_pairs={{0,2},{1,3},{2,0},{3,1},{4,6},{5,7},{6,4},{7,5},{8,10},{9,11},{10,... | collective-permute-start | bytes 208904 | tf_op jit(solution)/shard_map/ppermute | solution.py:556
  54.5 4.5 %collective-permute-start.12 = (f32[136,128]{1,0:T(8,128)S(1)}, f32[136,128]{1,0:T(8,128)S(1)}, u32[]{:S(2)}, u32[]{:S(2)}) collective-permute-start(f32[136,128]{1,0:T(8,128)S(1)} %get-tuple-element.79.refs_0_), channel_id=1, source_target_pairs={{0,1},{1,0},{2,3},{3,2},{4,5},{5,4},{6,7},{7,6},{8,9},{9,8},{10,11... | collective-permute-start | bytes 208904 | tf_op jit(solution)/shard_map/ppermute | solution.py:556
  59.7 6.9 %collective-permute-start.17 = (f32[136,128]{1,0:T(8,128)S(1)}, f32[136,128]{1,0:T(8,128)S(1)}, u32[]{:S(2)}, u32[]{:S(2)}) collective-permute-start(f32[136,128]{1,0:T(8,128)S(1)} %get-tuple-element.80.refs_0_), channel_id=1, source_target_pairs={{0,12},{4,8},{8,4},{12,0},{1,13},{5,9},{9,5},{13,1},{2,14},{6,10},... | collective-permute-start | bytes 208904 | tf_op jit(solution)/shard_map/ppermute | solution.py:556
  61.5 7.3 %collective-permute-start.16 = (f32[136,128]{1,0:T(8,128)S(1)}, f32[136,128]{1,0:T(8,128)S(1)}, u32[]{:S(2)}, u32[]{:S(2)}) collective-permute-start(f32[136,128]{1,0:T(8,128)S(1)} %get-tuple-element.80.refs_0_), channel_id=1, source_target_pairs={{0,8},{4,12},{8,0},{12,4},{1,9},{5,13},{9,1},{13,5},{2,10},{6,14},... | collective-permute-start | bytes 208904 | tf_op jit(solution)/shard_map/ppermute | solution.py:556
  61.7 7.1 %collective-permute-start.15 = (f32[136,128]{1,0:T(8,128)S(1)}, f32[136,128]{1,0:T(8,128)S(1)}, u32[]{:S(2)}, u32[]{:S(2)}) collective-permute-start(f32[136,128]{1,0:T(8,128)S(1)} %get-tuple-element.80.refs_0_), channel_id=1, source_target_pairs={{0,4},{4,0},{8,12},{12,8},{1,5},{5,1},{9,13},{13,9},{2,6},{6,2},{1... | collective-permute-start | bytes 208904 | tf_op jit(solution)/shard_map/ppermute | solution.py:556

commit v4 on v3

--- a/solution.py
+++ b/solution.py
@@ -72,13 +72,19 @@
     return high, middle, (rest - middle.astype(F32)).astype(BF16)
 
 
-def dot3(value, high, low, dims=NN):
-    rows = value.shape[0]
-    vh, vl = split(value)
-    both = lax.dot_general(
-        jnp.concatenate([vh, vl], axis=0), high, dims, preferred_element_type=F32
-    )
-    return both[:rows] + both[rows:] + lax.dot_general(vh, low, dims, preferred_element_type=F32)
+def doubled(value):
+    both = jnp.concatenate(split(value), axis=0)
+    return jnp.concatenate([both, both], axis=1)
+
+
+def apply(wide, stacked, dims=NN):
+    rows = wide.shape[0] // 2
+    both = lax.dot_general(wide, stacked, dims, preferred_element_type=F32)
+    return both[:rows] + both[rows:]
+
+
+def product(value, stacked, dims=NN):
+    return apply(doubled(value), stacked, dims)
 
 
 def stack_scalars(first, second):
@@ -175,8 +181,8 @@
 
 def setup_kernel(stages, total, anchors, *refs):
     sources, refs = refs[:6], refs[6:]
-    message, rhs, la, lb, ra, rb, basis_h, basis_l, chosen_out, params = refs[:10]
-    pts, skel, keep, scales, noise, sems = refs[10:]
+    message, rhs, la, lb, ra, rb, basis, chosen_out, params = refs[:9]
+    pts, skel, keep, scales, noise, sems = refs[9:]
     targets = (pts, rhs, skel, keep, scales, noise)
     copies = [
         pltpu.make_async_copy(source, target, sems.at[i])
@@ -208,11 +214,11 @@
     for i in range(count // STRIP):
         strip = slice(i * STRIP, (i + 1) * STRIP)
         high, low = split(gauss((la[strip, :], lb[strip, :]), own, unit))
-        basis_h[strip, :] = high
-        basis_l[strip, :] = low
+        basis[strip, :] = high
+        basis[count + i * STRIP : count + (i + 1) * STRIP, :] = low
     copies[1].wait()
     value = rhs[...]
-    write_wide(message, 0, dot3(value, basis_h[...], basis_l[...]))
+    write_wide(message, 0, product(value, basis[...]))
     message[dots : dots + 8, :] = to_rows([row_sum(value * value)])
     copies[3].wait()
     copies[5].wait()
@@ -233,29 +239,33 @@
                 slot += 1
 
 
-def near_blocks(value, parts):
-    return jnp.concatenate([dot3(value, high[...], low[...]) for high, low in parts], axis=1)
-
-
-def dense_kernel(start, la, lb, ra, rb, rhs, params, tie, high, low, near):
-    size = la.shape[0]
-    width = high.shape[1]
+def dense_kernel(start, la, lb, ra, rb, rhs, params, tie, stacked, near):
+    size, width = la.shape[0], stacked.shape[1]
     unit = params[0:1, 3:4]
 
     def body(k, carry):
-        strip = pl.ds(pl.multiple_of(k * STRIP, STRIP), STRIP)
+        top = pl.multiple_of(k * STRIP, STRIP)
+        strip, below = pl.ds(top, STRIP), pl.ds(pl.multiple_of(size + top, STRIP), STRIP)
         left = la[strip, :], lb[strip, :]
         for j in range(0, width, BLOCK):
             cut = slice(start + j, start + j + BLOCK)
-            h, l = split(gauss(left, (ra[:, cut], rb[:, cut]), unit))
-            high[strip, j : j + BLOCK] = h
-            low[strip, j : j + BLOCK] = l
+            high, low = split(gauss(left, (ra[:, cut], rb[:, cut]), unit))
+            stacked[strip, j : j + BLOCK] = high
+            stacked[below, j : j + BLOCK] = low
         return carry
 
-    lax.fori_loop(0, size // STRIP, body, 0)
+    lax.fori_loop(0, size // STRIP, body, 0, unroll=True)
     value = rhs[...]
     here = value[:, start : start + width]
-    near[...] = params[0:1, 2:3] * here + dot3(value, high[...], low[...])
+    near[...] = params[0:1, 2:3] * here + product(value, stacked[...])
+
+
+def flip_kernel(basis, tie, out):
+    size, rank = basis.shape[0] // 2, basis.shape[1]
+    for part in range(2):
+        for i in range(0, size, STRIP):
+            strip = basis[part * size + i : part * size + i + STRIP, :]
+            out[part * rank : (part + 1) * rank, i : i + STRIP] = strip.T
 
 
 def levels_of(count):
@@ -280,16 +290,21 @@
         for p in range(count >> level):
             slot = slots[level, p]
             first, second = weights[2 * p], weights[2 * p + 1]
-            crossed = dot3(second, couple[0][slot], couple[1][slot])
+            crossed = product(second, couple[slot])
             term = row_sum(first * crossed)
             energy = term if energy is None else energy + term
             if p == 0:
                 own_terms.append(crossed)
             if level < levels_of(count) or top:
                 joined = jnp.concatenate([first, second], axis=1)
-                parents.append(dot3(joined, transfer[0][slot], transfer[1][slot]))
+                parents.append(product(joined, transfer[slot]))
         weights = parents
     return weights, own_terms, 2.0 * energy
+
+
+def own_half(transfer, slot):
+    rank = transfer.shape[2]
+    return transfer[slot, :rank, :], transfer[slot, 2 * rank : 3 * rank, :]
 
 
 def sweep_down(search, own_terms, transfer, count):
@@ -297,9 +312,8 @@
     for level in range(levels_of(count), 0, -1):
         own = own_terms[level - 1]
         if search is not None:
-            slot = slots[level, 0]
-            half = own.shape[1]
-            own = own + dot3(search, transfer[0][slot, :half], transfer[1][slot, :half], NT)
+            half = jnp.concatenate(own_half(transfer, slots[level, 0]), axis=1)
+            own = own + product(search, half, NT)
         search = own
     return search
 
@@ -317,8 +331,8 @@
         for p in range(count >> level):
             slot = slots[level, p]
             high, low = split(gauss(sides[2 * p + 1][0], sides[2 * p][1], unit))
-            couple[0][slot] = high
-            couple[1][slot] = low
+            couple[slot, :rank, :] = high
+            couple[slot, rank:, :] = low
             if level == levels_of(count) and not top:
                 continue
             joined = jnp.concatenate([coords[2 * p], coords[2 * p + 1]], axis=1)
@@ -326,8 +340,8 @@
             parent_side = features((parent - shift) * inverse, unit)
             for side in range(2):
                 high, low = split(gauss(sides[2 * p + side][0], parent_side[1], unit))
-                transfer[0][slot, side * rank : (side + 1) * rank, :] = high
-                transfer[1][slot, side * rank : (side + 1) * rank, :] = low
+                transfer[slot, side * rank : (side + 1) * rank, :] = high
+                transfer[slot, (side + 2) * rank : (side + 3) * rank, :] = low
             parents.append(parent)
             parent_sides.append(parent_side)
         coords, sides = parents, parent_sides
@@ -353,9 +367,8 @@
 def lower_first_kernel(rows, count, offset, refs):
     messages = refs[:count]
     params, chosen = refs[count : count + 2]
-    message, terms, transfer_h, transfer_l, couple_h, couple_l = refs[-6:]
-    transfer, couple = (transfer_h, transfer_l), (couple_h, couple_l)
-    rank = couple_h.shape[2]
+    message, terms, transfer, couple = refs[-4:]
+    rank = couple.shape[2]
     coords = coords_of(messages, rows, rank)
     picks = chosen[offset : offset + count - 1, :]
     coords = build_tree(coords, picks, params, transfer, couple, True)
@@ -364,7 +377,7 @@
 
 
 def lower_finish(rows, messages, message, terms, transfer, couple, top):
-    rank = couple[0].shape[2]
+    rank = couple.shape[2]
     weights = weights_of(messages, rows, rank)
     weights, own_terms, energy = sweep_up(weights, transfer, couple, top)
     for i, term in enumerate(own_terms):
@@ -376,70 +389,57 @@
 
 
 def lower_kernel(rows, count, top, refs):
-    messages = refs[:count]
-    transfer_h, transfer_l, couple_h, couple_l = refs[count : count + 4]
-    message, terms = refs[count + 4 :]
-    lower_finish(
-        rows, messages, message, terms, (transfer_h, transfer_l), (couple_h, couple_l), top
-    )
+    transfer, couple, message, terms = refs[count:]
+    lower_finish(rows, refs[:count], message, terms, transfer, couple, top)
 
 
 def upper_build(rows, count, offset, refs):
-    messages = refs[:count]
-    params, chosen, transfer_h, transfer_l, couple_h, couple_l = refs[count:]
-    coords = coords_of(messages, rows, couple_h.shape[2])
+    params, chosen, transfer, couple = refs[count:]
+    coords = coords_of(refs[:count], rows, couple.shape[2])
     picks = chosen[offset : offset + count - 1, :]
-    build_tree(
-        coords, picks, params, (transfer_h, transfer_l), (couple_h, couple_l), False
-    )
-
-
-def own_chain(upper, lower):
+    build_tree(coords, picks, params, transfer, couple, False)
+
+
+def compose_kernel(counts, refs):
+    out = refs[-1]
     halves = []
-    for high, low, count in lower + [upper]:
+    for transfer, count in zip(refs, counts):
         slots = tree_slots(count)
-        half = high.shape[2]
-        for level in range(1, levels_of(count) + 1):
-            slot = slots[level, 0]
-            halves.append((high[slot, :half], low[slot, :half]))
-    return halves[:-1]
-
-
-def compose_kernel(counts, refs):
-    high_out, low_out = refs[-2:]
-    trees = [(refs[2 * i], refs[2 * i + 1], count) for i, count in enumerate(counts)]
-    chain = own_chain(trees[-1], trees[:-1])
-    rank = chain[0][0].shape[0]
-    high, low = chain[0]
-    for i in range(len(chain)):
+        halves += [own_half(transfer, slots[i, 0]) for i in range(1, levels_of(count) + 1)]
+    halves = halves[:-1]
+    rank = out.shape[1]
+    high, low = halves[0]
+    for i, half in enumerate(halves):
         if i:
-            product = high.astype(F32) + low.astype(F32)
-            high, low = split(dot3(product, *chain[i]))
-        high_out[:, i * rank : (i + 1) * rank] = high
-        low_out[:, i * rank : (i + 1) * rank] = low
+            chained = high.astype(F32) + low.astype(F32)
+            high, low = split(product(chained, jnp.concatenate(half, axis=0)))
+        out[i * rank : (i + 1) * rank, :] = high.T
+        out[(len(halves) + i) * rank : (len(halves) + i + 1) * rank, :] = low.T
 
 
 def far_field(rows, messages, upper, lower, path=None):
     count = len(messages)
-    rank = upper[2].shape[2]
+    transfer, couple = upper
+    rank = couple.shape[2]
     weights = weights_of(messages, rows, rank)
-    _, own_terms, energy = sweep_up(weights, upper[:2], upper[2:], False)
+    _, own_terms, energy = sweep_up(weights, transfer, couple, False)
     sums = to_columns(add_dots(messages, rows, rank), rows)
     if path is None:
-        search = sweep_down(None, own_terms, upper[:2], count)
-        for terms, high, low in reversed(lower):
+        search = sweep_down(None, own_terms, transfer, count)
+        for terms, below_transfer in reversed(lower):
             depth = terms.shape[0]
             below = [terms[i] for i in range(depth)]
-            search = sweep_down(search, below, (high, low), 1 << depth)
+            search = sweep_down(search, below, below_transfer, 1 << depth)
     else:
         below = [terms[i] for terms in lower for i in range(terms.shape[0])]
         search, *above = below + own_terms
-        search = search + dot3(jnp.concatenate(above, axis=1), path[0][...], path[1][...], NT)
+        search = search + product(jnp.concatenate(above, axis=1), path[...])
     return search, sums, sums[:, 7:8] + energy
 
 
-def near_field(value, params, parts):
-    return params[0:1, 2:3] * value + near_blocks(value, parts)
+def near_field(wide, value, params, parts):
+    cuts = [apply(wide, part[...]) for part in parts]
+    return params[0:1, 2:3] * value + jnp.concatenate(cuts, axis=1)
 
 
 def column_state(columns):
@@ -462,32 +462,29 @@
 
 
 def open_refs(rows, count, stages, refs):
-    messages, lower, upper, basis, rest = take_refs(refs, count, 3 * stages, 4, 2)
-    lower = [lower[i : i + 3] for i in range(0, 3 * stages, 3)]
+    messages, lower, upper, basis, rest = take_refs(refs, count, 2 * stages, 2, 2)
+    lower = [lower[i : i + 2] for i in range(0, 2 * stages, 2)]
     return far_field(rows, messages, upper, lower), basis, rest
 
 
 def open_composed(rows, count, stages, refs):
-    messages, terms, upper, path, basis, rest = take_refs(refs, count, stages, 4, 2, 2)
-    return far_field(rows, messages, upper, terms, path), basis, rest
-
-
-def dense_parts(refs):
-    return list(zip(refs[0::2], refs[1::2]))
+    messages, terms, upper, path, basis, rest = take_refs(refs, count, stages, 2, 1, 2)
+    return far_field(rows, messages, upper, terms, path[0]), basis, rest
 
 
 def first_kernel(rows, count, stages, parts, refs):
     (search, sums, far), basis, rest = open_refs(rows, count, stages, refs)
-    dense, rest = take_refs(rest, 2 * parts)
+    dense, rest = take_refs(rest, parts)
     params, rhs = rest[:2]
     near_parts, (message, q_out, near_out, state) = take_refs(rest[2:], parts)
     near_b = jnp.concatenate([n[...] for n in near_parts], axis=1)
     norm = sums[:, 0:1]
     rate = norm / (params[0:1, 2:3] * norm + jnp.abs(far))
-    q = rate * (near_b + dot3(search, basis[0][...], basis[1][...], NT))
+    q = rate * (near_b + product(search, basis[1][...]))
     q_out[...] = q
-    write_wide(message, 0, dot3(q, basis[0][...], basis[1][...]))
-    near_q = near_field(q, params, dense_parts(dense))
+    wide = doubled(q)
+    write_wide(message, 0, apply(wide, basis[0][...]))
+    near_q = near_field(wide, q, params, dense)
     near_out[...] = near_q
     dots = [row_sum(rhs[...] * q), row_sum(q * q), row_sum(q * near_q)]
     message[message.shape[0] - 8 :, :] = to_rows(dots)
@@ -496,9 +493,9 @@
 
 def second_kernel(rows, count, stages, parts, refs):
     (search, sums, far), basis, rest = open_composed(rows, count, stages, refs)
-    dense, rest = take_refs(rest, 2 * parts)
+    dense, rest = take_refs(rest, parts)
     params, rhs, q_in, near_in, state_in = rest[:5]
-    message, x_out, r_out, d_out, q_out, near_out, state = rest[5:]
+    message, r_out, q_out, near_out, state = rest[5:]
     norm0, rate = state_in[:, 0:1], state_in[:, 1:2]
     bq, qq, qaq = sums[:, 0:1], sums[:, 1:2], sums[:, 2:3] + far
     step = norm0 / bq
@@ -508,25 +505,31 @@
     back = 1.0 / rate
     rhs_v, q = rhs[...], q_in[...]
     r1 = rhs_v - step * q
-    d1 = r1 + beta * rhs_v
     q0 = back * q
-    aq = near_in[...] + dot3(search, basis[0][...], basis[1][...], NT)
+    aq = near_in[...] + product(search, basis[1][...])
     q1 = (1.0 + beta) * q0 - step * aq
     rar = back * (bq - 2.0 * step * qq) + step * step * qaq
     cross = back * (bq - step * qq)
     curve = rar + 2.0 * beta * cross + beta * beta * (back * bq)
     alpha1 = norm1 / curve
-    x_out[...] = alpha0 * rhs_v + alpha1 * d1
     r2 = r1 - alpha1 * q1
     r_out[...] = r2
-    d_out[...] = d1
     q_out[...] = q1
-    write_wide(message, 0, dot3(r2, basis[0][...], basis[1][...]))
-    near = near_field(r2, params, dense_parts(dense))
+    wide = doubled(r2)
+    write_wide(message, 0, apply(wide, basis[0][...]))
+    near = near_field(wide, r2, params, dense)
     near_out[...] = near
     dots = [row_sum(r2 * r2), row_sum(r2 * q1), row_sum(r2 * near)]
     message[message.shape[0] - 8 :, :] = to_rows(dots)
-    state[...] = column_state([norm1, curve])
+    state[...] = column_state([norm1, curve, alpha0, alpha1, step, beta])
+
+
+def update_kernel(rhs, q, state, x_out, d_out):
+    alpha0, alpha1, step, beta = (state[:, i : i + 1] for i in range(2, 6))
+    rhs_v = rhs[...]
+    d1 = rhs_v - step * q[...] + beta * rhs_v
+    d_out[...] = d1
+    x_out[...] = alpha0 * rhs_v + alpha1 * d1
 
 
 def last_kernel(rows, count, stages, refs):
@@ -541,7 +544,7 @@
     x_done[...] = x_in[...] + alpha * (r2 + beta * d_in[...])
     x_copy = pltpu.make_async_copy(x_done, x_out, sems.at[0])
     x_copy.start()
-    image = near_in[...] + dot3(search, basis[0][...], basis[1][...], NT) + beta * q_in[...]
+    image = near_in[...] + product(search, basis[1][...]) + beta * q_in[...]
     r_done[...] = r2 - alpha * image
     r_copy = pltpu.make_async_copy(r_done, r_out, sems.at[1])
     r_copy.start()
@@ -580,7 +583,7 @@
     offsets = [sum(counts[:i]) - i for i in range(len(counts))]
     stage_count = len(stages) - 1
 
-    message, rhs, la, lb, ra, rb, basis_h, basis_l, chosen, params = call(
+    message, rhs, la, lb, ra, rb, basis, chosen, params = call(
         functools.partial(setup_kernel, bases, total, subs),
         [
             f32_shape(message_rows(rows, rank, True), LANES),
@@ -589,8 +592,7 @@
             bf16_shape(size, 80),
             bf16_shape(16, size),
             bf16_shape(80, size),
-            bf16_shape(size, rank),
-            bf16_shape(size, rank),
+            bf16_shape(2 * size, rank),
             jax.ShapeDtypeStruct((slots, rank), jnp.int32),
             f32_shape(8, 128),
         ],
@@ -614,25 +616,24 @@
         ],
         name="setup",
     )
-    basis = [basis_h, basis_l]
 
     def tree_shapes(count):
         nodes = count - 1
-        return [bf16_shape(nodes, 2 * rank, rank)] * 2 + [bf16_shape(nodes, rank, rank)] * 2
+        return [bf16_shape(nodes, 4 * rank, rank), bf16_shape(nodes, 2 * rank, rank)]
 
     first_width = size // BLOCK * 3 // 8 * BLOCK
     widths = [first_width, size - first_width]
     dense, near_parts = [], []
 
     def build_dense(start, width, tie):
-        high, low, near = call(
+        stacked, near = call(
             functools.partial(dense_kernel, start),
-            [resident_shape(size, width)] * 2 + [f32_shape(rows, width)],
+            [resident_shape(2 * size, width), f32_shape(rows, width)],
             [la, lb, ra, rb, rhs, params, tie],
             cost=(6 * rows * size * width + 192 * size * width, size * width),
             name="dense",
         )
-        dense.extend([high, low])
+        dense.append(stacked)
         near_parts.append(near)
 
     trees = []
@@ -654,6 +655,14 @@
         terms_all.append(terms)
     messages = gather(message, hops[-1])
     build_dense(widths[0], widths[1], message)
+    (flipped,) = call(
+        flip_kernel,
+        [bf16_shape(2 * rank, size)],
+        [basis, message],
+        cost=(64 * size * rank, 0),
+        name="flip",
+    )
+    basis = [basis, flipped]
     upper = call(
         refs_of(upper_build, rows, counts[-1], offsets[-1]),
         tree_shapes(counts[-1]),
@@ -666,7 +675,7 @@
     message_shape = f32_shape(message_rows(rows, rank, False), LANES)
 
     def lower_of(terms_all):
-        return [a for terms, tree in zip(terms_all, trees) for a in (terms, tree[0], tree[1])]
+        return [a for terms, tree in zip(terms_all, trees) for a in (terms, tree[0])]
 
     def exchange(message, shadow=None):
         terms_all = []
@@ -694,24 +703,35 @@
     )
 
     def compose():
-        pairs = [a for tree in trees + [upper] for a in tree[:2]]
+        pairs = [tree[0] for tree in trees + [upper]]
         return call(
             refs_of(compose_kernel, counts),
-            [bf16_shape(rank, (total - 1) * rank)] * 2,
+            [bf16_shape(2 * (total - 1) * rank, rank)],
             pairs + [state],
             cost=(12 * rank * rank * rank, 0),
             name="compose",
         )
 
     arrived, path = exchange(message, compose)
-    message, x, r, d, q, near, state = call(
+    first_q = q
+    message, r, q, near, state = call(
         refs_of(second_kernel, *fixed, len(widths)),
-        [message_shape, vector, vector, vector, vector, vector, state_shape],
+        [message_shape, vector, vector, vector, state_shape],
         arrived + upper + path + basis + dense + [params, rhs, q, near, state],
         resident=dense,
         name="second",
     )
-    arrived, _ = exchange(message)
+
+    def update():
+        return call(
+            update_kernel,
+            [vector, vector],
+            [rhs, first_q, state],
+            cost=(8 * rows * size, 0),
+            name="update",
+        )
+
+    arrived, (x, d) = exchange(message, update)
     return tuple(
         call(
             refs_of(last_kernel, *fixed),

time: 71.8 us -> 70.1 us (0.976)
  Pallas kernels: 32 us -> 29.2 us
  waiting for transfers between devices: 17.5 us -> 18.7 us
    pallas_call x11 -> x13, Pallas kernels: 32 us -> 29.2 us  [call(): pl.pallas_call(kernel, out_shape=list(out_shape), in_specs=[ANY if i in a...]
    ppermute x18, waiting for transfers between devices: 17.5 us -> 18.7 us  [gather(): return [value] + [lax.ppermute(value, axis, pair) for pair in pairs]]
  transfers between devices with their start and end apart: 18 -> 18, of which waited for: 9 -> 10; matrix products, arithmetic and copies ran while one was open for 0% -> 0% of each run, Pallas kernels for 15% -> 13%
where the time goes in v4:
time: 70.1 us; the launch traced here: 69.9 us
  Pallas kernels  29.2 us (42%)
  starting transfers between devices  20.6 us (29%)
  waiting for transfers between devices  18.7 us (27%)
  between operations  1.54 us (2%)
    pallas_call x13, Pallas kernels, call(): pl.pallas_call(kernel, out_shape=list(out_shape), in_specs=[ANY if i in a...  29.2 us
    ppermute x18, starting transfers between devices, gather(): return [value] + [lax.ppermute(value, axis, pair) for pair in pairs]  20.6 us
    ppermute x18, waiting for transfers between devices, gather(): return [value] + [lax.ppermute(value, axis, pair) for pair in pairs]  18.7 us
  transfers between devices with their start and end apart: 18, of which 10 were waited for; matrix products, arithmetic and copies ran while one was open for 0% of the time, Pallas kernels for 13%

profile of v4, /device:TPU:0, one launch (start us, length us, event | category | flops | bytes accessed | tf_op | source)
XLA Modules:
  0.0 69.9 jit_solution(11023844253401065705)
XLA Ops:
  1.3 3.3 %setup.1 = (f32[152,128]{1,0:T(8,128)S(1)}, f32[64,2048]{1,0:T(8,128)S(1)}, bf16[2048,16]{1,0:T(8,128)(2,1)S(1)}, bf16[2048,80]{1,0:T(8,128)(2,1)S(1)}, bf16[16,...) custom-call(f32[6,2048]{1,0:T(8,128)} %refs_0_.1, ...), custom_call_target="tpu_custom_call" | custom-call | tf_op jit(solution)/shard_map/setup/pallas_call | solution.py:42
  4.6 2.4 %collective-permute-start.2 = (f32[152,128]{1,0:T(8,128)S(1)}, f32[152,128]{1,0:T(8,128)S(1)}, u32[]{:S(2)}, u32[]{:S(2)}) collective-permute-start(f32[152,128]{1,0:T(8,128)S(1)} %get-tuple-element.36.refs_0_), channel_id=1, source_target_pairs={{0,3},{1,2},{2,1},{3,0},{4,7},{5,6},{6,5},{7,4},{8,11},{9,10},{10,... | collective-permute-start | bytes 233480 | tf_op jit(solution)/shard_map/ppermute | solution.py:559
  7.7 2.9 %dense.2 = (bf16[4096,768]{1,0:T(8,128)(2,1)S(1)}, f32[64,768]{1,0:T(8,128)S(1)}) custom-call(bf16[2048,16]{1,0:T(8,128)(2,1)S(1)} %get-tuple-element.39.la, bf16[2048,80]{1,0:T(8,128)(2,1)S(1)} %get-tuple-element.40.lb, bf16[16,2048]{1,0:T(8,128)(2,1)S(1)} %get-tuple-element.41.ra, bf16[80,2048]{1,0:T(8,128)(2,1)S(1)} %get-tuple-element.42.rb, ...), custom_call_target="tpu_custom_call" | custom-call | flops 905969664 | bytes 7806976 | tf_op jit(solution)/shard_map/dense/pallas_call | solution.py:42
  10.6 1.3 %collective-permute-done.1.refs_2_ = f32[152,128]{1,0:T(8,128)S(1)} collective-permute-done((f32[152,128]{1,0:T(8,128)S(1)}, f32[152,128]{1,0:T(8,128)S(1)}, u32[]{:S(2)}, u32[]{:S(2)}) %collective-permute-start.1) | collective-permute-done | bytes 77856 | tf_op jit(solution)/shard_map/ppermute | solution.py:559
  11.9 2.2 %lower_first.1 = (f32[152,128]{1,0:T(8,128)S(1)}, f32[2,64,256]{2,1,0:T(8,128)S(1)}, bf16[3,1024,256]{2,1,0:T(8,128)(2,1)S(1)}, bf16[3,512,256]{2,1,0:T(8,128)(2,1)S(1)}) custom-call(f32[152,128]{1,0:T(8,128)S(1)} %get-tuple-element.36.refs_0_, f32[152,128]{1,0:T(8,128)S(1)} %collective-permute-done.refs_1_, f32[152,128]{1,0:T(8,128)S(1)} %collective-permute-done.1.refs_2_, ...), custom_call_target="tpu_custom_call" | custom-call | tf_op jit(solution)/shard_map/lower_first/pallas_call | solution.py:42
  14.2 4.1 %collective-permute-start.5 = (f32[152,128]{1,0:T(8,128)S(1)}, f32[152,128]{1,0:T(8,128)S(1)}, u32[]{:S(2)}, u32[]{:S(2)}) collective-permute-start(f32[152,128]{1,0:T(8,128)S(1)} %get-tuple-element.45.refs_0_.tie), channel_id=1, source_target_pairs={{0,12},{4,8},{8,4},{12,0},{1,13},{5,9},{9,5},{13,1},{2,14},{6,10},... | collective-permute-start | bytes 233480 | tf_op jit(solution)/shard_map/ppermute | solution.py:559
  19.6 4.4 %dense.3 = (bf16[4096,1280]{1,0:T(8,128)(2,1)S(1)}, f32[64,1280]{1,0:T(8,128)S(1)}) custom-call(bf16[2048,16]{1,0:T(8,128)(2,1)S(1)} %get-tuple-element.39.la, bf16[2048,80]{1,0:T(8,128)(2,1)S(1)} %get-tuple-element.40.lb, bf16[16,2048]{1,0:T(8,128)(2,1)S(1)} %get-tuple-element.41.ra, bf16[80,2048]{1,0:T(8,128)(2,1)S(1)} %get-tuple-element.42.rb, ...), custom_call_target="tpu_custom_call" | custom-call | flops 1509949440 | bytes 12206080 | tf_op jit(solution)/shard_map/dense/pallas_call | solution.py:42
  25.1 1.3 %upper_build.1 = (bf16[3,1024,256]{2,1,0:T(8,128)(2,1)S(1)}, bf16[3,512,256]{2,1,0:T(8,128)(2,1)S(1)}) custom-call(f32[152,128]{1,0:T(8,128)S(1)} %get-tuple-element.45.refs_0_.tie, f32[152,128]{1,0:T(8,128)S(1)} %collective-permute-done.3.refs_1_, f32[152,128]{1,0:T(8,128)S(1)} %collective-permute-done.4.refs_2_, ...), custom_call_target="tpu_custom_call" | custom-call | tf_op jit(solution)/shard_map/upper_build/pallas_call | solution.py:42
  26.3 4.8 %first.1 = (f32[136,128]{1,0:T(8,128)S(1)}, f32[64,2048]{1,0:T(8,128)S(1)}, f32[64,2048]{1,0:T(8,128)S(1)}, f32[64,128]{1,0:T(8,128)S(1)}) custom-call(f32[152,128]{1,0:T(8,128)S(1)} %get-tuple-element.45.refs_0_.tie, f32[152,128]{1,0:T(8,128)S(1)} %collective-permute-done.3.refs_1_, f32[152,128]{1,0:T(8,128)S(1)} %collective-permute-done.4.refs_2_, ...), custom_call_target="tpu_custom_call" | custom-call | tf_op jit(solution)/shard_map/first/pallas_call | solution.py:42
  33.0 2.5 %collective-permute-done.8.refs_3_ = f32[136,128]{1,0:T(8,128)S(1)} collective-permute-done((f32[136,128]{1,0:T(8,128)S(1)}, f32[136,128]{1,0:T(8,128)S(1)}, u32[]{:S(2)}, u32[]{:S(2)}) %collective-permute-start.8) | collective-permute-done | bytes 69664 | tf_op jit(solution)/shard_map/ppermute | solution.py:559
  35.5 1.6 %collective-permute-done.7.refs_2_ = f32[136,128]{1,0:T(8,128)S(1)} collective-permute-done((f32[136,128]{1,0:T(8,128)S(1)}, f32[136,128]{1,0:T(8,128)S(1)}, u32[]{:S(2)}, u32[]{:S(2)}) %collective-permute-start.7) | collective-permute-done | bytes 69664 | tf_op jit(solution)/shard_map/ppermute | solution.py:559
  37.9 2.8 %collective-permute-start.11 = (f32[136,128]{1,0:T(8,128)S(1)}, f32[136,128]{1,0:T(8,128)S(1)}, u32[]{:S(2)}, u32[]{:S(2)}) collective-permute-start(f32[136,128]{1,0:T(8,128)S(1)} %get-tuple-element.56.refs_0_), channel_id=1, source_target_pairs={{0,12},{4,8},{8,4},{12,0},{1,13},{5,9},{9,5},{13,1},{2,14},{6,10},... | collective-permute-start | bytes 208904 | tf_op jit(solution)/shard_map/ppermute | solution.py:559
  40.8 1.6 %collective-permute-start.9 = (f32[136,128]{1,0:T(8,128)S(1)}, f32[136,128]{1,0:T(8,128)S(1)}, u32[]{:S(2)}, u32[]{:S(2)}) collective-permute-start(f32[136,128]{1,0:T(8,128)S(1)} %get-tuple-element.56.refs_0_), channel_id=1, source_target_pairs={{0,4},{4,0},{8,12},{12,8},{1,5},{5,1},{9,13},{13,9},{2,6},{6,2},{1... | collective-permute-start | bytes 208904 | tf_op jit(solution)/shard_map/ppermute | solution.py:559
  43.2 1.6 %collective-permute-done.11.refs_3_ = f32[136,128]{1,0:T(8,128)S(1)} collective-permute-done((f32[136,128]{1,0:T(8,128)S(1)}, f32[136,128]{1,0:T(8,128)S(1)}, u32[]{:S(2)}, u32[]{:S(2)}) %collective-permute-start.11) | collective-permute-done | bytes 69664 | tf_op jit(solution)/shard_map/ppermute | solution.py:559
  44.8 2.4 %collective-permute-done.10.refs_2_ = f32[136,128]{1,0:T(8,128)S(1)} collective-permute-done((f32[136,128]{1,0:T(8,128)S(1)}, f32[136,128]{1,0:T(8,128)S(1)}, u32[]{:S(2)}, u32[]{:S(2)}) %collective-permute-start.10) | collective-permute-done | bytes 69664 | tf_op jit(solution)/shard_map/ppermute | solution.py:559
  47.2 4.6 %second.1 = (f32[136,128]{1,0:T(8,128)S(1)}, f32[64,2048]{1,0:T(8,128)S(1)}, f32[64,2048]{1,0:T(8,128)S(1)}, f32[64,2048]{1,0:T(8,128)S(1)}, f32[64,128]{1,0:T(8,128)S(1)}) custom-call(f32[136,128]{1,0:T(8,128)S(1)} %get-tuple-element.56.refs_0_, f32[136,128]{1,0:T(8,128)S(1)} %collective-permute-done.9.refs_1_, ...), custom_call_target="tpu_custom_call" | custom-call | tf_op jit(solution)/shard_map/second/pallas_call | solution.py:42
  52.1 1.3 %collective-permute-start.13 = (f32[136,128]{1,0:T(8,128)S(1)}, f32[136,128]{1,0:T(8,128)S(1)}, u32[]{:S(2)}, u32[]{:S(2)}) collective-permute-start(f32[136,128]{1,0:T(8,128)S(1)} %get-tuple-element.61.refs_0_), channel_id=1, source_target_pairs={{0,2},{1,3},{2,0},{3,1},{4,6},{5,7},{6,4},{7,5},{8,10},{9,11},{10,... | collective-permute-start | bytes 208904 | tf_op jit(solution)/shard_map/ppermute | solution.py:559
  53.7 2.4 %collective-permute-done.14.refs_3_ = f32[136,128]{1,0:T(8,128)S(1)} collective-permute-done((f32[136,128]{1,0:T(8,128)S(1)}, f32[136,128]{1,0:T(8,128)S(1)}, u32[]{:S(2)}, u32[]{:S(2)}) %collective-permute-start.14) | collective-permute-done | bytes 69664 | tf_op jit(solution)/shard_map/ppermute | solution.py:559
  56.1 1.7 %collective-permute-done.13.refs_2_ = f32[136,128]{1,0:T(8,128)S(1)} collective-permute-done((f32[136,128]{1,0:T(8,128)S(1)}, f32[136,128]{1,0:T(8,128)S(1)}, u32[]{:S(2)}, u32[]{:S(2)}) %collective-permute-start.13) | collective-permute-done | bytes 69664 | tf_op jit(solution)/shard_map/ppermute | solution.py:559
  58.6 2.4 %collective-permute-start.17 = (f32[136,128]{1,0:T(8,128)S(1)}, f32[136,128]{1,0:T(8,128)S(1)}, u32[]{:S(2)}, u32[]{:S(2)}) collective-permute-start(f32[136,128]{1,0:T(8,128)S(1)} %get-tuple-element.62.refs_0_), channel_id=1, source_target_pairs={{0,12},{4,8},{8,4},{12,0},{1,13},{5,9},{9,5},{13,1},{2,14},{6,10},... | collective-permute-start | bytes 208904 | tf_op jit(solution)/shard_map/ppermute | solution.py:559
  61.0 2.0 %collective-permute-start.15 = (f32[136,128]{1,0:T(8,128)S(1)}, f32[136,128]{1,0:T(8,128)S(1)}, u32[]{:S(2)}, u32[]{:S(2)}) collective-permute-start(f32[136,128]{1,0:T(8,128)S(1)} %get-tuple-element.62.refs_0_), channel_id=1, source_target_pairs={{0,4},{4,0},{8,12},{12,8},{1,5},{5,1},{9,13},{13,9},{2,6},{6,2},{1... | collective-permute-start | bytes 208904 | tf_op jit(solution)/shard_map/ppermute | solution.py:559
  63.3 2.0 %collective-permute-done.17.refs_3_ = f32[136,128]{1,0:T(8,128)S(1)} collective-permute-done((f32[136,128]{1,0:T(8,128)S(1)}, f32[136,128]{1,0:T(8,128)S(1)}, u32[]{:S(2)}, u32[]{:S(2)}) %collective-permute-start.17) | collective-permute-done | bytes 69664 | tf_op jit(solution)/shard_map/ppermute | solution.py:559
  65.4 2.1 %collective-permute-done.16.refs_2_ = f32[136,128]{1,0:T(8,128)S(1)} collective-permute-done((f32[136,128]{1,0:T(8,128)S(1)}, f32[136,128]{1,0:T(8,128)S(1)}, u32[]{:S(2)}, u32[]{:S(2)}) %collective-permute-start.16) | collective-permute-done | bytes 69664 | tf_op jit(solution)/shard_map/ppermute | solution.py:559
  67.5 2.3 %last.1 = (f32[64,2048]{1,0:T(8,128)}, f32[64,2048]{1,0:T(8,128)}) custom-call(f32[136,128]{1,0:T(8,128)S(1)} %get-tuple-element.62.refs_0_, f32[136,128]{1,0:T(8,128)S(1)} %collective-permute-done.15.refs_1_, f32[136,128]{1,0:T(8,128)S(1)} %collective-permute-done.16.refs_2_, f32[136,128]{1,0:T(8,128)S(1)} %collective-permute-done.17.refs_3_, ...), custom_call_target="tpu_custom_call" | custom-call | tf_op jit(solution)/shard_map/last/pallas_call | solution.py:42
  (25 shorter events, 8.1 us)
Async XLA Ops:
  4.6 6.1 %collective-permute-start.2 = (f32[152,128]{1,0:T(8,128)S(1)}, f32[152,128]{1,0:T(8,128)S(1)}, u32[]{:S(2)}, u32[]{:S(2)}) collective-permute-start(f32[152,128]{1,0:T(8,128)S(1)} %get-tuple-element.36.refs_0_), channel_id=1, source_target_pairs={{0,3},{1,2},{2,1},{3,0},{4,7},{5,6},{6,5},{7,4},{8,11},{9,10},{10,... | collective-permute-start | bytes 233480 | tf_op jit(solution)/shard_map/ppermute | solution.py:559
  7.0 4.9 %collective-permute-start.1 = (f32[152,128]{1,0:T(8,128)S(1)}, f32[152,128]{1,0:T(8,128)S(1)}, u32[]{:S(2)}, u32[]{:S(2)}) collective-permute-start(f32[152,128]{1,0:T(8,128)S(1)} %get-tuple-element.36.refs_0_), channel_id=1, source_target_pairs={{0,2},{1,3},{2,0},{3,1},{4,6},{5,7},{6,4},{7,5},{8,10},{9,11},{10,... | collective-permute-start | bytes 233480 | tf_op jit(solution)/shard_map/ppermute | solution.py:559
  7.6 4.3 %collective-permute-start = (f32[152,128]{1,0:T(8,128)S(1)}, f32[152,128]{1,0:T(8,128)S(1)}, u32[]{:S(2)}, u32[]{:S(2)}) collective-permute-start(f32[152,128]{1,0:T(8,128)S(1)} %get-tuple-element.36.refs_0_), channel_id=1, source_target_pairs={{0,1},{1,0},{2,3},{3,2},{4,5},{5,4},{6,7},{7,6},{8,9},{9,8},{10,11... | collective-permute-start | bytes 233480 | tf_op jit(solution)/shard_map/ppermute | solution.py:559
  14.2 9.8 %collective-permute-start.5 = (f32[152,128]{1,0:T(8,128)S(1)}, f32[152,128]{1,0:T(8,128)S(1)}, u32[]{:S(2)}, u32[]{:S(2)}) collective-permute-start(f32[152,128]{1,0:T(8,128)S(1)} %get-tuple-element.45.refs_0_.tie), channel_id=1, source_target_pairs={{0,12},{4,8},{8,4},{12,0},{1,13},{5,9},{9,5},{13,1},{2,14},{6,10},... | collective-permute-start | bytes 233480 | tf_op jit(solution)/shard_map/ppermute | solution.py:559
  18.3 6.8 %collective-permute-start.4 = (f32[152,128]{1,0:T(8,128)S(1)}, f32[152,128]{1,0:T(8,128)S(1)}, u32[]{:S(2)}, u32[]{:S(2)}) collective-permute-start(f32[152,128]{1,0:T(8,128)S(1)} %get-tuple-element.45.refs_0_.tie), channel_id=1, source_target_pairs={{0,8},{4,12},{8,0},{12,4},{1,9},{5,13},{9,1},{13,5},{2,10},{6,14},... | collective-permute-start | bytes 233480 | tf_op jit(solution)/shard_map/ppermute | solution.py:559
  18.3 6.8 %collective-permute-start.3 = (f32[152,128]{1,0:T(8,128)S(1)}, f32[152,128]{1,0:T(8,128)S(1)}, u32[]{:S(2)}, u32[]{:S(2)}) collective-permute-start(f32[152,128]{1,0:T(8,128)S(1)} %get-tuple-element.45.refs_0_.tie), channel_id=1, source_target_pairs={{0,4},{4,0},{8,12},{12,8},{1,5},{5,1},{9,13},{13,9},{2,6},{6,2},{1... | collective-permute-start | bytes 233480 | tf_op jit(solution)/shard_map/ppermute | solution.py:559
  31.1 4.4 %collective-permute-start.8 = (f32[136,128]{1,0:T(8,128)S(1)}, f32[136,128]{1,0:T(8,128)S(1)}, u32[]{:S(2)}, u32[]{:S(2)}) collective-permute-start(f32[136,128]{1,0:T(8,128)S(1)} %get-tuple-element.54.refs_0_), channel_id=1, source_target_pairs={{0,3},{1,2},{2,1},{3,0},{4,7},{5,6},{6,5},{7,4},{8,11},{9,10},{10,... | collective-permute-start | bytes 208904 | tf_op jit(solution)/shard_map/ppermute | solution.py:559
  31.6 5.5 %collective-permute-start.7 = (f32[136,128]{1,0:T(8,128)S(1)}, f32[136,128]{1,0:T(8,128)S(1)}, u32[]{:S(2)}, u32[]{:S(2)}) collective-permute-start(f32[136,128]{1,0:T(8,128)S(1)} %get-tuple-element.54.refs_0_), channel_id=1, source_target_pairs={{0,2},{1,3},{2,0},{3,1},{4,6},{5,7},{6,4},{7,5},{8,10},{9,11},{10,... | collective-permute-start | bytes 208904 | tf_op jit(solution)/shard_map/ppermute | solution.py:559
  32.7 4.4 %collective-permute-start.6 = (f32[136,128]{1,0:T(8,128)S(1)}, f32[136,128]{1,0:T(8,128)S(1)}, u32[]{:S(2)}, u32[]{:S(2)}) collective-permute-start(f32[136,128]{1,0:T(8,128)S(1)} %get-tuple-element.54.refs_0_), channel_id=1, source_target_pairs={{0,1},{1,0},{2,3},{3,2},{4,5},{5,4},{6,7},{7,6},{8,9},{9,8},{10,11... | collective-permute-start | bytes 208904 | tf_op jit(solution)/shard_map/ppermute | solution.py:559
  37.9 6.8 %collective-permute-start.11 = (f32[136,128]{1,0:T(8,128)S(1)}, f32[136,128]{1,0:T(8,128)S(1)}, u32[]{:S(2)}, u32[]{:S(2)}) collective-permute-start(f32[136,128]{1,0:T(8,128)S(1)} %get-tuple-element.56.refs_0_), channel_id=1, source_target_pairs={{0,12},{4,8},{8,4},{12,0},{1,13},{5,9},{9,5},{13,1},{2,14},{6,10},... | collective-permute-start | bytes 208904 | tf_op jit(solution)/shard_map/ppermute | solution.py:559
  40.7 6.4 %collective-permute-start.10 = (f32[136,128]{1,0:T(8,128)S(1)}, f32[136,128]{1,0:T(8,128)S(1)}, u32[]{:S(2)}, u32[]{:S(2)}) collective-permute-start(f32[136,128]{1,0:T(8,128)S(1)} %get-tuple-element.56.refs_0_), channel_id=1, source_target_pairs={{0,8},{4,12},{8,0},{12,4},{1,9},{5,13},{9,1},{13,5},{2,10},{6,14},... | collective-permute-start | bytes 208904 | tf_op jit(solution)/shard_map/ppermute | solution.py:559
  40.8 6.4 %collective-permute-start.9 = (f32[136,128]{1,0:T(8,128)S(1)}, f32[136,128]{1,0:T(8,128)S(1)}, u32[]{:S(2)}, u32[]{:S(2)}) collective-permute-start(f32[136,128]{1,0:T(8,128)S(1)} %get-tuple-element.56.refs_0_), channel_id=1, source_target_pairs={{0,4},{4,0},{8,12},{12,8},{1,5},{5,1},{9,13},{13,9},{2,6},{6,2},{1... | collective-permute-start | bytes 208904 | tf_op jit(solution)/shard_map/ppermute | solution.py:559
  51.8 4.3 %collective-permute-start.14 = (f32[136,128]{1,0:T(8,128)S(1)}, f32[136,128]{1,0:T(8,128)S(1)}, u32[]{:S(2)}, u32[]{:S(2)}) collective-permute-start(f32[136,128]{1,0:T(8,128)S(1)} %get-tuple-element.61.refs_0_), channel_id=1, source_target_pairs={{0,3},{1,2},{2,1},{3,0},{4,7},{5,6},{6,5},{7,4},{8,11},{9,10},{10,... | collective-permute-start | bytes 208904 | tf_op jit(solution)/shard_map/ppermute | solution.py:559
  52.1 5.7 %collective-permute-start.13 = (f32[136,128]{1,0:T(8,128)S(1)}, f32[136,128]{1,0:T(8,128)S(1)}, u32[]{:S(2)}, u32[]{:S(2)}) collective-permute-start(f32[136,128]{1,0:T(8,128)S(1)} %get-tuple-element.61.refs_0_), channel_id=1, source_target_pairs={{0,2},{1,3},{2,0},{3,1},{4,6},{5,7},{6,4},{7,5},{8,10},{9,11},{10,... | collective-permute-start | bytes 208904 | tf_op jit(solution)/shard_map/ppermute | solution.py:559
  53.5 4.3 %collective-permute-start.12 = (f32[136,128]{1,0:T(8,128)S(1)}, f32[136,128]{1,0:T(8,128)S(1)}, u32[]{:S(2)}, u32[]{:S(2)}) collective-permute-start(f32[136,128]{1,0:T(8,128)S(1)} %get-tuple-element.61.refs_0_), channel_id=1, source_target_pairs={{0,1},{1,0},{2,3},{3,2},{4,5},{5,4},{6,7},{7,6},{8,9},{9,8},{10,11... | collective-permute-start | bytes 208904 | tf_op jit(solution)/shard_map/ppermute | solution.py:559
  58.6 6.7 %collective-permute-start.17 = (f32[136,128]{1,0:T(8,128)S(1)}, f32[136,128]{1,0:T(8,128)S(1)}, u32[]{:S(2)}, u32[]{:S(2)}) collective-permute-start(f32[136,128]{1,0:T(8,128)S(1)} %get-tuple-element.62.refs_0_), channel_id=1, source_target_pairs={{0,12},{4,8},{8,4},{12,0},{1,13},{5,9},{9,5},{13,1},{2,14},{6,10},... | collective-permute-start | bytes 208904 | tf_op jit(solution)/shard_map/ppermute | solution.py:559
  61.0 6.4 %collective-permute-start.16 = (f32[136,128]{1,0:T(8,128)S(1)}, f32[136,128]{1,0:T(8,128)S(1)}, u32[]{:S(2)}, u32[]{:S(2)}) collective-permute-start(f32[136,128]{1,0:T(8,128)S(1)} %get-tuple-element.62.refs_0_), channel_id=1, source_target_pairs={{0,8},{4,12},{8,0},{12,4},{1,9},{5,13},{9,1},{13,5},{2,10},{6,14},... | collective-permute-start | bytes 208904 | tf_op jit(solution)/shard_map/ppermute | solution.py:559
  61.0 6.4 %collective-permute-start.15 = (f32[136,128]{1,0:T(8,128)S(1)}, f32[136,128]{1,0:T(8,128)S(1)}, u32[]{:S(2)}, u32[]{:S(2)}) collective-permute-start(f32[136,128]{1,0:T(8,128)S(1)} %get-tuple-element.62.refs_0_), channel_id=1, source_target_pairs={{0,4},{4,0},{8,12},{12,8},{1,5},{5,1},{9,13},{13,9},{2,6},{6,2},{1... | collective-permute-start | bytes 208904 | tf_op jit(solution)/shard_map/ppermute | solution.py:559

commit v5 on v4

--- a/solution.py
+++ b/solution.py
@@ -280,7 +280,7 @@
     return slots
 
 
-def sweep_up(weights, transfer, couple, top):
+def sweep_up(weights, transfer, couple, top, measured=True):
     count = len(weights)
     slots = tree_slots(count)
     own_terms = []
@@ -290,16 +290,20 @@
         for p in range(count >> level):
             slot = slots[level, p]
             first, second = weights[2 * p], weights[2 * p + 1]
-            crossed = product(second, couple[slot])
-            term = row_sum(first * crossed)
-            energy = term if energy is None else energy + term
-            if p == 0:
-                own_terms.append(crossed)
-            if level < levels_of(count) or top:
+            if couple is not None and (measured or p == 0):
+                crossed = product(second, couple[slot])
+                if p == 0:
+                    own_terms.append(crossed)
+                if measured:
+                    term = row_sum(first * crossed)
+                    energy = term if energy is None else energy + term
+            parent = None
+            if (level < levels_of(count) or top) and (measured or top or p > 0):
                 joined = jnp.concatenate([first, second], axis=1)
-                parents.append(product(joined, transfer[slot]))
+                parent = product(joined, transfer[slot])
+            parents.append(parent)
         weights = parents
-    return weights, own_terms, 2.0 * energy
+    return weights, own_terms, None if energy is None else 2.0 * energy
 
 
 def own_half(transfer, slot):
@@ -318,7 +322,7 @@
     return search
 
 
-def build_tree(coords, chosen, params, transfer, couple, top):
+def build_tree(coords, picks, params, transfer, couple, nodes, top, partial=False):
     count = len(coords)
     slots = tree_slots(count)
     rank = coords[0].shape[1]
@@ -330,15 +334,21 @@
         parents, parent_sides = [], []
         for p in range(count >> level):
             slot = slots[level, p]
-            high, low = split(gauss(sides[2 * p + 1][0], sides[2 * p][1], unit))
-            couple[slot, :rank, :] = high
-            couple[slot, rank:, :] = low
-            if level == levels_of(count) and not top:
+            if couple is not None and (p == 0 or not partial):
+                high, low = split(gauss(sides[2 * p + 1][0], sides[2 * p][1], unit))
+                couple[slot, :rank, :] = high
+                couple[slot, rank:, :] = low
+            if level == levels_of(count) and (not top or transfer is None):
                 continue
-            joined = jnp.concatenate([coords[2 * p], coords[2 * p + 1]], axis=1)
-            parent = pick(joined, chosen[slot : slot + 1, :])
+            if picks is None:
+                parent = nodes[slot]
+            else:
+                joined = jnp.concatenate([coords[2 * p], coords[2 * p + 1]], axis=1)
+                parent = pick(joined, picks[slot : slot + 1, :])
+                if nodes is not None:
+                    nodes[slot] = parent
             parent_side = features((parent - shift) * inverse, unit)
-            for side in range(2):
+            for side in range(0 if transfer is None else 1 if partial and p == 0 else 2):
                 high, low = split(gauss(sides[2 * p + side][0], parent_side[1], unit))
                 transfer[slot, side * rank : (side + 1) * rank, :] = high
                 transfer[slot, (side + 2) * rank : (side + 3) * rank, :] = low
@@ -367,13 +377,29 @@
 def lower_first_kernel(rows, count, offset, refs):
     messages = refs[:count]
     params, chosen = refs[count : count + 2]
-    message, terms, transfer, couple = refs[-4:]
+    message, transfer, nodes = refs[-3:]
+    rank = transfer.shape[2]
+    picks = chosen[offset : offset + count - 1, :]
+    coords = coords_of(messages, rows, rank)
+    coords = build_tree(coords, picks, params, transfer, None, nodes, True)
+    weights = weights_of(messages, rows, rank)
+    weights, _, _ = sweep_up(weights, transfer, None, True)
+    write_wide(message, 0, weights[0])
+    dots = dots_at(rows, rank)
+    message[dots : dots + 8, :] = add_dots(messages, rows, rank)
+    write_wide(message, dots + 8, coords[0])
+
+
+def lower_rest_kernel(rows, count, refs):
+    messages = refs[:count]
+    params, transfer, nodes, couple, terms = refs[count:]
     rank = couple.shape[2]
     coords = coords_of(messages, rows, rank)
-    picks = chosen[offset : offset + count - 1, :]
-    coords = build_tree(coords, picks, params, transfer, couple, True)
-    lower_finish(rows, messages, message, terms, transfer, couple, True)
-    write_wide(message, dots_at(rows, rank) + 8, coords[0])
+    build_tree(coords, None, params, None, couple, nodes, False)
+    weights = weights_of(messages, rows, rank)
+    _, own_terms, _ = sweep_up(weights, transfer, couple, False, measured=False)
+    for i, term in enumerate(own_terms):
+        terms[i] = term
 
 
 def lower_finish(rows, messages, message, terms, transfer, couple, top):
@@ -393,11 +419,12 @@
     lower_finish(rows, refs[:count], message, terms, transfer, couple, top)
 
 
-def upper_build(rows, count, offset, refs):
-    params, chosen, transfer, couple = refs[count:]
+def upper_build(rows, count, offset, partial, refs):
+    params, chosen = refs[count : count + 2]
+    transfer, couple = refs[-2:]
     coords = coords_of(refs[:count], rows, couple.shape[2])
     picks = chosen[offset : offset + count - 1, :]
-    build_tree(coords, picks, params, transfer, couple, False)
+    build_tree(coords, picks, params, transfer, couple, None, False, partial)
 
 
 def compose_kernel(counts, refs):
@@ -417,23 +444,29 @@
         out[(len(halves) + i) * rank : (len(halves) + i + 1) * rank, :] = low.T
 
 
-def far_field(rows, messages, upper, lower, path=None):
-    count = len(messages)
+def far_search(rows, messages, upper, lower):
+    transfer, couple = upper
+    rank = couple.shape[2]
+    weights = weights_of(messages, rows, rank)
+    _, own_terms, _ = sweep_up(weights, transfer, couple, False, measured=False)
+    search = sweep_down(None, own_terms, transfer, len(messages))
+    for terms, below_transfer in reversed(lower):
+        depth = terms.shape[0]
+        below = [terms[i] for i in range(depth)]
+        search = sweep_down(search, below, below_transfer, 1 << depth)
+    size = sum(row_sum(w * w) for w in weights)
+    return search, to_columns(add_dots(messages, rows, rank), rows), size
+
+
+def far_field(rows, messages, upper, lower, path):
     transfer, couple = upper
     rank = couple.shape[2]
     weights = weights_of(messages, rows, rank)
     _, own_terms, energy = sweep_up(weights, transfer, couple, False)
     sums = to_columns(add_dots(messages, rows, rank), rows)
-    if path is None:
-        search = sweep_down(None, own_terms, transfer, count)
-        for terms, below_transfer in reversed(lower):
-            depth = terms.shape[0]
-            below = [terms[i] for i in range(depth)]
-            search = sweep_down(search, below, below_transfer, 1 << depth)
-    else:
-        below = [terms[i] for terms in lower for i in range(terms.shape[0])]
-        search, *above = below + own_terms
-        search = search + product(jnp.concatenate(above, axis=1), path[...])
+    below = [terms[i] for terms in lower for i in range(terms.shape[0])]
+    search, *above = below + own_terms
+    search = search + product(jnp.concatenate(above, axis=1), path[...])
     return search, sums, sums[:, 7:8] + energy
 
 
@@ -464,7 +497,7 @@
 def open_refs(rows, count, stages, refs):
     messages, lower, upper, basis, rest = take_refs(refs, count, 2 * stages, 2, 2)
     lower = [lower[i : i + 2] for i in range(0, 2 * stages, 2)]
-    return far_field(rows, messages, upper, lower), basis, rest
+    return far_search(rows, messages, upper, lower), basis, rest
 
 
 def open_composed(rows, count, stages, refs):
@@ -473,13 +506,13 @@
 
 
 def first_kernel(rows, count, stages, parts, refs):
-    (search, sums, far), basis, rest = open_refs(rows, count, stages, refs)
+    (search, sums, size), basis, rest = open_refs(rows, count, stages, refs)
     dense, rest = take_refs(rest, parts)
     params, rhs = rest[:2]
     near_parts, (message, q_out, near_out, state) = take_refs(rest[2:], parts)
     near_b = jnp.concatenate([n[...] for n in near_parts], axis=1)
     norm = sums[:, 0:1]
-    rate = norm / (params[0:1, 2:3] * norm + jnp.abs(far))
+    rate = norm / (params[0:1, 2:3] * norm + size)
     q = rate * (near_b + product(search, basis[1][...]))
     q_out[...] = q
     wide = doubled(q)
@@ -636,7 +669,7 @@
         dense.append(stacked)
         near_parts.append(near)
 
-    trees = []
+    trees, pending = [], []
     terms_all = []
     for i in range(stage_count):
         messages = gather(message, hops[i])
@@ -644,15 +677,18 @@
         if i == 0:
             build_dense(0, widths[0], params)
             extra = near_parts[:1]
-        message, terms, *tree = call(
+        next_message, transfer, nodes = call(
             refs_of(lower_first_kernel, rows, counts[i], offsets[i]),
-            [f32_shape(message_rows(rows, rank, True), LANES), f32_shape(bases[i][1], rows, rank)]
-            + tree_shapes(counts[i]),
+            [
+                f32_shape(message_rows(rows, rank, True), LANES),
+                tree_shapes(counts[i])[0],
+                f32_shape(counts[i] - 1, 8, rank),
+            ],
             messages + [params, chosen] + extra,
             name="lower_first",
         )
-        trees.append(tree)
-        terms_all.append(terms)
+        pending.append((i, messages, transfer, nodes))
+        message = next_message
     messages = gather(message, hops[-1])
     build_dense(widths[0], widths[1], message)
     (flipped,) = call(
@@ -663,12 +699,28 @@
         name="flip",
     )
     basis = [basis, flipped]
-    upper = call(
-        refs_of(upper_build, rows, counts[-1], offsets[-1]),
-        tree_shapes(counts[-1]),
-        messages + [params, chosen],
-        name="upper_build",
-    )
+    for i, arrived, transfer, nodes in pending:
+        couple, terms = call(
+            refs_of(lower_rest_kernel, rows, counts[i]),
+            [tree_shapes(counts[i])[1], f32_shape(bases[i][1], rows, rank)],
+            arrived + [params, transfer, nodes],
+            cost=(48 * rank * rank * rank, rank * rank * counts[i]),
+            name="lower_rest",
+        )
+        trees.append([transfer, couple])
+        terms_all.append(terms)
+
+    def build_upper(partial, extra):
+        return call(
+            refs_of(upper_build, rows, counts[-1], offsets[-1], partial),
+            tree_shapes(counts[-1]),
+            messages_first + [params, chosen] + extra,
+            cost=None if partial else (48 * rank * rank * rank, rank * rank * counts[-1]),
+            name="upper_build",
+        )
+
+    messages_first = messages
+    upper = build_upper(True, [])
 
     state_shape = f32_shape(rows, 128)
     vector = f32_shape(rows, size)
@@ -703,16 +755,18 @@
     )
 
     def compose():
+        upper = build_upper(False, [state])
         pairs = [tree[0] for tree in trees + [upper]]
-        return call(
+        path = call(
             refs_of(compose_kernel, counts),
             [bf16_shape(2 * (total - 1) * rank, rank)],
             pairs + [state],
             cost=(12 * rank * rank * rank, 0),
             name="compose",
         )
-
-    arrived, path = exchange(message, compose)
+        return upper, path
+
+    arrived, (upper, path) = exchange(message, compose)
     first_q = q
     message, r, q, near, state = call(
         refs_of(second_kernel, *fixed, len(widths)),

time: 70.1 us -> 69.6 us (level)
  waiting for transfers between devices: 18.7 us -> 16.9 us
  Pallas kernels: 29.2 us -> 30.4 us
    ppermute x18, waiting for transfers between devices: 18.7 us -> 16.9 us  [gather(): return [value] + [lax.ppermute(value, axis, pair) for pair in pairs]]
    pallas_call x13 -> x15, Pallas kernels: 29.2 us -> 30.4 us  [call(): pl.pallas_call(kernel, out_shape=list(out_shape), in_specs=[ANY if i in a...]
  transfers between devices with their start and end apart: 18 -> 18, of which waited for: 10 -> 9; matrix products, arithmetic and copies ran while one was open for 0% -> 0% of each run, Pallas kernels for 13% -> 16%
where the time goes in v5:
time: 69.6 us; the launch traced here: 69.5 us
  Pallas kernels  30.4 us (44%)
  starting transfers between devices  20.6 us (30%)
  waiting for transfers between devices  16.9 us (24%)
  between operations  1.57 us (2%)
    pallas_call x15, Pallas kernels, call(): pl.pallas_call(kernel, out_shape=list(out_shape), in_specs=[ANY if i in a...  30.4 us
    ppermute x18, starting transfers between devices, gather(): return [value] + [lax.ppermute(value, axis, pair) for pair in pairs]  20.6 us
    ppermute x18, waiting for transfers between devices, gather(): return [value] + [lax.ppermute(value, axis, pair) for pair in pairs]  16.9 us
  transfers between devices with their start and end apart: 18, of which 9 were waited for; matrix products, arithmetic and copies ran while one was open for 0% of the time, Pallas kernels for 16%

profile of v5, /device:TPU:0, one launch (start us, length us, event | category | flops | bytes accessed | tf_op | source)
XLA Modules:
  0.0 69.5 jit_solution(789181953482803537)
XLA Ops:
  1.3 3.3 %setup.1 = (f32[152,128]{1,0:T(8,128)S(1)}, f32[64,2048]{1,0:T(8,128)S(1)}, bf16[2048,16]{1,0:T(8,128)(2,1)S(1)}, bf16[2048,80]{1,0:T(8,128)(2,1)S(1)}, bf16[16,...) custom-call(f32[6,2048]{1,0:T(8,128)} %refs_0_.1, ...), custom_call_target="tpu_custom_call" | custom-call | tf_op jit(solution)/shard_map/setup/pallas_call | solution.py:42
  4.6 2.4 %collective-permute-start.2 = (f32[152,128]{1,0:T(8,128)S(1)}, f32[152,128]{1,0:T(8,128)S(1)}, u32[]{:S(2)}, u32[]{:S(2)}) collective-permute-start(f32[152,128]{1,0:T(8,128)S(1)} %get-tuple-element.39.refs_0_), channel_id=1, source_target_pairs={{0,3},{1,2},{2,1},{3,0},{4,7},{5,6},{6,5},{7,4},{8,11},{9,10},{10,... | collective-permute-start | bytes 233480 | tf_op jit(solution)/shard_map/ppermute | solution.py:592
  7.7 2.9 %dense.2 = (bf16[4096,768]{1,0:T(8,128)(2,1)S(1)}, f32[64,768]{1,0:T(8,128)S(1)}) custom-call(bf16[2048,16]{1,0:T(8,128)(2,1)S(1)} %get-tuple-element.42.la, bf16[2048,80]{1,0:T(8,128)(2,1)S(1)} %get-tuple-element.43.lb, bf16[16,2048]{1,0:T(8,128)(2,1)S(1)} %get-tuple-element.44.ra, bf16[80,2048]{1,0:T(8,128)(2,1)S(1)} %get-tuple-element.45.rb, ...), custom_call_target="tpu_custom_call" | custom-call | flops 905969664 | bytes 7806976 | tf_op jit(solution)/shard_map/dense/pallas_call | solution.py:42
  10.6 1.3 %collective-permute-done.1.refs_2_ = f32[152,128]{1,0:T(8,128)S(1)} collective-permute-done((f32[152,128]{1,0:T(8,128)S(1)}, f32[152,128]{1,0:T(8,128)S(1)}, u32[]{:S(2)}, u32[]{:S(2)}) %collective-permute-start.1) | collective-permute-done | bytes 77856 | tf_op jit(solution)/shard_map/ppermute | solution.py:592
  12.0 1.6 %lower_first.1 = (f32[152,128]{1,0:T(8,128)S(1)}, bf16[3,1024,256]{2,1,0:T(8,128)(2,1)S(1)}, f32[3,8,256]{2,1,0:T(8,128)S(1)}) custom-call(f32[152,128]{1,0:T(8,128)S(1)} %get-tuple-element.39.refs_0_, f32[152,128]{1,0:T(8,128)S(1)} %collective-permute-done.refs_1_, f32[152,128]{1,0:T(8,128)S(1)} %collective-permute-done.1.refs_2_, ...), custom_call_target="tpu_custom_call" | custom-call | tf_op jit(solution)/shard_map/lower_first/pallas_call | solution.py:42
  13.6 4.1 %collective-permute-start.5 = (f32[152,128]{1,0:T(8,128)S(1)}, f32[152,128]{1,0:T(8,128)S(1)}, u32[]{:S(2)}, u32[]{:S(2)}) collective-permute-start(f32[152,128]{1,0:T(8,128)S(1)} %get-tuple-element.48.refs_0_.tie), channel_id=1, source_target_pairs={{0,12},{4,8},{8,4},{12,0},{1,13},{5,9},{9,5},{13,1},{2,14},{6,10},... | collective-permute-start | bytes 233480 | tf_op jit(solution)/shard_map/ppermute | solution.py:592
  18.3 4.4 %dense.3 = (bf16[4096,1280]{1,0:T(8,128)(2,1)S(1)}, f32[64,1280]{1,0:T(8,128)S(1)}) custom-call(bf16[2048,16]{1,0:T(8,128)(2,1)S(1)} %get-tuple-element.42.la, bf16[2048,80]{1,0:T(8,128)(2,1)S(1)} %get-tuple-element.43.lb, bf16[16,2048]{1,0:T(8,128)(2,1)S(1)} %get-tuple-element.44.ra, bf16[80,2048]{1,0:T(8,128)(2,1)S(1)} %get-tuple-element.45.rb, ...), custom_call_target="tpu_custom_call" | custom-call | flops 1509949440 | bytes 12206080 | tf_op jit(solution)/shard_map/dense/pallas_call | solution.py:42
  23.4 1.0 %lower_rest.1 = (bf16[3,512,256]{2,1,0:T(8,128)(2,1)S(1)}, f32[2,64,256]{2,1,0:T(8,128)S(1)}) custom-call(f32[152,128]{1,0:T(8,128)S(1)} %get-tuple-element.39.refs_0_, f32[152,128]{1,0:T(8,128)S(1)} %collective-permute-done.refs_1_, f32[152,128]{1,0:T(8,128)S(1)} %collective-permute-done.1.refs_2_, f32[152,128]{1,0:T(8,128)S(1)} %collective-permute-done.2.refs_3_, ...), custom_call_target="tpu_custom_call" | custom-call | flops 805306368 | bytes 2830336 | tf_op jit(solution)/shard_map/lower_rest/pallas_call | solution.py:42
  25.5 4.6 %first.1 = (f32[136,128]{1,0:T(8,128)S(1)}, f32[64,2048]{1,0:T(8,128)S(1)}, f32[64,2048]{1,0:T(8,128)S(1)}, f32[64,128]{1,0:T(8,128)S(1)}) custom-call(f32[152,128]{1,0:T(8,128)S(1)} %get-tuple-element.48.refs_0_.tie, f32[152,128]{1,0:T(8,128)S(1)} %collective-permute-done.3.refs_1_, f32[152,128]{1,0:T(8,128)S(1)} %collective-permute-done.4.refs_2_, ...), custom_call_target="tpu_custom_call" | custom-call | tf_op jit(solution)/shard_map/first/pallas_call | solution.py:42
  30.8 1.1 %collective-permute-start.7 = (f32[136,128]{1,0:T(8,128)S(1)}, f32[136,128]{1,0:T(8,128)S(1)}, u32[]{:S(2)}, u32[]{:S(2)}) collective-permute-start(f32[136,128]{1,0:T(8,128)S(1)} %get-tuple-element.58.refs_0_), channel_id=1, source_target_pairs={{0,2},{1,3},{2,0},{3,1},{4,6},{5,7},{6,4},{7,5},{8,10},{9,11},{10,... | collective-permute-start | bytes 208904 | tf_op jit(solution)/shard_map/ppermute | solution.py:592
  32.0 2.4 %collective-permute-done.8.refs_3_ = f32[136,128]{1,0:T(8,128)S(1)} collective-permute-done((f32[136,128]{1,0:T(8,128)S(1)}, f32[136,128]{1,0:T(8,128)S(1)}, u32[]{:S(2)}, u32[]{:S(2)}) %collective-permute-start.8) | collective-permute-done | bytes 69664 | tf_op jit(solution)/shard_map/ppermute | solution.py:592
  34.4 1.7 %collective-permute-done.7.refs_2_ = f32[136,128]{1,0:T(8,128)S(1)} collective-permute-done((f32[136,128]{1,0:T(8,128)S(1)}, f32[136,128]{1,0:T(8,128)S(1)}, u32[]{:S(2)}, u32[]{:S(2)}) %collective-permute-start.7) | collective-permute-done | bytes 69664 | tf_op jit(solution)/shard_map/ppermute | solution.py:592
  36.9 3.8 %collective-permute-start.11 = (f32[136,128]{1,0:T(8,128)S(1)}, f32[136,128]{1,0:T(8,128)S(1)}, u32[]{:S(2)}, u32[]{:S(2)}) collective-permute-start(f32[136,128]{1,0:T(8,128)S(1)} %get-tuple-element.60.refs_0_), channel_id=1, source_target_pairs={{0,12},{4,8},{8,4},{12,0},{1,13},{5,9},{9,5},{13,1},{2,14},{6,10},... | collective-permute-start | bytes 208904 | tf_op jit(solution)/shard_map/ppermute | solution.py:592
  41.3 1.3 %upper_build.3 = (bf16[3,1024,256]{2,1,0:T(8,128)(2,1)S(1)}, bf16[3,512,256]{2,1,0:T(8,128)(2,1)S(1)}) custom-call(f32[152,128]{1,0:T(8,128)S(1)} %get-tuple-element.48.refs_0_.tie, f32[152,128]{1,0:T(8,128)S(1)} %collective-permute-done.3.refs_1_, f32[152,128]{1,0:T(8,128)S(1)} %collective-permute-done.4.refs_2_, ...), custom_call_target="tpu_custom_call" | custom-call | flops 805306368 | bytes 2713600 | tf_op jit(solution)/shard_map/upper_build/pallas_call | solution.py:42
  43.8 2.8 %collective-permute-done.10.refs_2_ = f32[136,128]{1,0:T(8,128)S(1)} collective-permute-done((f32[136,128]{1,0:T(8,128)S(1)}, f32[136,128]{1,0:T(8,128)S(1)}, u32[]{:S(2)}, u32[]{:S(2)}) %collective-permute-start.10) | collective-permute-done | bytes 69664 | tf_op jit(solution)/shard_map/ppermute | solution.py:592
  46.6 4.6 %second.1 = (f32[136,128]{1,0:T(8,128)S(1)}, f32[64,2048]{1,0:T(8,128)S(1)}, f32[64,2048]{1,0:T(8,128)S(1)}, f32[64,2048]{1,0:T(8,128)S(1)}, f32[64,128]{1,0:T(8,128)S(1)}) custom-call(f32[136,128]{1,0:T(8,128)S(1)} %get-tuple-element.60.refs_0_, f32[136,128]{1,0:T(8,128)S(1)} %collective-permute-done.9.refs_1_, ...), custom_call_target="tpu_custom_call" | custom-call | tf_op jit(solution)/shard_map/second/pallas_call | solution.py:42
  51.4 1.3 %collective-permute-start.13 = (f32[136,128]{1,0:T(8,128)S(1)}, f32[136,128]{1,0:T(8,128)S(1)}, u32[]{:S(2)}, u32[]{:S(2)}) collective-permute-start(f32[136,128]{1,0:T(8,128)S(1)} %get-tuple-element.67.refs_0_), channel_id=1, source_target_pairs={{0,2},{1,3},{2,0},{3,1},{4,6},{5,7},{6,4},{7,5},{8,10},{9,11},{10,... | collective-permute-start | bytes 208904 | tf_op jit(solution)/shard_map/ppermute | solution.py:592
  53.1 2.6 %collective-permute-done.14.refs_3_ = f32[136,128]{1,0:T(8,128)S(1)} collective-permute-done((f32[136,128]{1,0:T(8,128)S(1)}, f32[136,128]{1,0:T(8,128)S(1)}, u32[]{:S(2)}, u32[]{:S(2)}) %collective-permute-start.14) | collective-permute-done | bytes 69664 | tf_op jit(solution)/shard_map/ppermute | solution.py:592
  55.7 1.5 %collective-permute-done.13.refs_2_ = f32[136,128]{1,0:T(8,128)S(1)} collective-permute-done((f32[136,128]{1,0:T(8,128)S(1)}, f32[136,128]{1,0:T(8,128)S(1)}, u32[]{:S(2)}, u32[]{:S(2)}) %collective-permute-start.13) | collective-permute-done | bytes 69664 | tf_op jit(solution)/shard_map/ppermute | solution.py:592
  58.0 1.7 %collective-permute-start.17 = (f32[136,128]{1,0:T(8,128)S(1)}, f32[136,128]{1,0:T(8,128)S(1)}, u32[]{:S(2)}, u32[]{:S(2)}) collective-permute-start(f32[136,128]{1,0:T(8,128)S(1)} %get-tuple-element.68.refs_0_), channel_id=1, source_target_pairs={{0,12},{4,8},{8,4},{12,0},{1,13},{5,9},{9,5},{13,1},{2,14},{6,10},... | collective-permute-start | bytes 208904 | tf_op jit(solution)/shard_map/ppermute | solution.py:592
  59.9 2.5 %collective-permute-start.15 = (f32[136,128]{1,0:T(8,128)S(1)}, f32[136,128]{1,0:T(8,128)S(1)}, u32[]{:S(2)}, u32[]{:S(2)}) collective-permute-start(f32[136,128]{1,0:T(8,128)S(1)} %get-tuple-element.68.refs_0_), channel_id=1, source_target_pairs={{0,4},{4,0},{8,12},{12,8},{1,5},{5,1},{9,13},{13,9},{2,6},{6,2},{1... | collective-permute-start | bytes 208904 | tf_op jit(solution)/shard_map/ppermute | solution.py:592
  62.7 2.2 %collective-permute-done.17.refs_3_ = f32[136,128]{1,0:T(8,128)S(1)} collective-permute-done((f32[136,128]{1,0:T(8,128)S(1)}, f32[136,128]{1,0:T(8,128)S(1)}, u32[]{:S(2)}, u32[]{:S(2)}) %collective-permute-start.17) | collective-permute-done | bytes 69664 | tf_op jit(solution)/shard_map/ppermute | solution.py:592
  64.9 2.1 %collective-permute-done.16.refs_2_ = f32[136,128]{1,0:T(8,128)S(1)} collective-permute-done((f32[136,128]{1,0:T(8,128)S(1)}, f32[136,128]{1,0:T(8,128)S(1)}, u32[]{:S(2)}, u32[]{:S(2)}) %collective-permute-start.16) | collective-permute-done | bytes 69664 | tf_op jit(solution)/shard_map/ppermute | solution.py:592
  67.0 2.3 %last.1 = (f32[64,2048]{1,0:T(8,128)}, f32[64,2048]{1,0:T(8,128)}) custom-call(f32[136,128]{1,0:T(8,128)S(1)} %get-tuple-element.68.refs_0_, f32[136,128]{1,0:T(8,128)S(1)} %collective-permute-done.15.refs_1_, f32[136,128]{1,0:T(8,128)S(1)} %collective-permute-done.16.refs_2_, f32[136,128]{1,0:T(8,128)S(1)} %collective-permute-done.17.refs_3_, ...), custom_call_target="tpu_custom_call" | custom-call | tf_op jit(solution)/shard_map/last/pallas_call | solution.py:42
  (27 shorter events, 8.2 us)
Async XLA Ops:
  4.6 6.1 %collective-permute-start.2 = (f32[152,128]{1,0:T(8,128)S(1)}, f32[152,128]{1,0:T(8,128)S(1)}, u32[]{:S(2)}, u32[]{:S(2)}) collective-permute-start(f32[152,128]{1,0:T(8,128)S(1)} %get-tuple-element.39.refs_0_), channel_id=1, source_target_pairs={{0,3},{1,2},{2,1},{3,0},{4,7},{5,6},{6,5},{7,4},{8,11},{9,10},{10,... | collective-permute-start | bytes 233480 | tf_op jit(solution)/shard_map/ppermute | solution.py:592
  7.0 4.9 %collective-permute-start.1 = (f32[152,128]{1,0:T(8,128)S(1)}, f32[152,128]{1,0:T(8,128)S(1)}, u32[]{:S(2)}, u32[]{:S(2)}) collective-permute-start(f32[152,128]{1,0:T(8,128)S(1)} %get-tuple-element.39.refs_0_), channel_id=1, source_target_pairs={{0,2},{1,3},{2,0},{3,1},{4,6},{5,7},{6,4},{7,5},{8,10},{9,11},{10,... | collective-permute-start | bytes 233480 | tf_op jit(solution)/shard_map/ppermute | solution.py:592
  7.7 4.3 %collective-permute-start = (f32[152,128]{1,0:T(8,128)S(1)}, f32[152,128]{1,0:T(8,128)S(1)}, u32[]{:S(2)}, u32[]{:S(2)}) collective-permute-start(f32[152,128]{1,0:T(8,128)S(1)} %get-tuple-element.39.refs_0_), channel_id=1, source_target_pairs={{0,1},{1,0},{2,3},{3,2},{4,5},{5,4},{6,7},{7,6},{8,9},{9,8},{10,11... | collective-permute-start | bytes 233480 | tf_op jit(solution)/shard_map/ppermute | solution.py:592
  13.6 10.9 %collective-permute-start.5 = (f32[152,128]{1,0:T(8,128)S(1)}, f32[152,128]{1,0:T(8,128)S(1)}, u32[]{:S(2)}, u32[]{:S(2)}) collective-permute-start(f32[152,128]{1,0:T(8,128)S(1)} %get-tuple-element.48.refs_0_.tie), channel_id=1, source_target_pairs={{0,12},{4,8},{8,4},{12,0},{1,13},{5,9},{9,5},{13,1},{2,14},{6,10},... | collective-permute-start | bytes 233480 | tf_op jit(solution)/shard_map/ppermute | solution.py:592
  17.7 6.8 %collective-permute-start.4 = (f32[152,128]{1,0:T(8,128)S(1)}, f32[152,128]{1,0:T(8,128)S(1)}, u32[]{:S(2)}, u32[]{:S(2)}) collective-permute-start(f32[152,128]{1,0:T(8,128)S(1)} %get-tuple-element.48.refs_0_.tie), channel_id=1, source_target_pairs={{0,8},{4,12},{8,0},{12,4},{1,9},{5,13},{9,1},{13,5},{2,10},{6,14},... | collective-permute-start | bytes 233480 | tf_op jit(solution)/shard_map/ppermute | solution.py:592
  17.7 6.8 %collective-permute-start.3 = (f32[152,128]{1,0:T(8,128)S(1)}, f32[152,128]{1,0:T(8,128)S(1)}, u32[]{:S(2)}, u32[]{:S(2)}) collective-permute-start(f32[152,128]{1,0:T(8,128)S(1)} %get-tuple-element.48.refs_0_.tie), channel_id=1, source_target_pairs={{0,4},{4,0},{8,12},{12,8},{1,5},{5,1},{9,13},{13,9},{2,6},{6,2},{1... | collective-permute-start | bytes 233480 | tf_op jit(solution)/shard_map/ppermute | solution.py:592
  30.1 4.3 %collective-permute-start.8 = (f32[136,128]{1,0:T(8,128)S(1)}, f32[136,128]{1,0:T(8,128)S(1)}, u32[]{:S(2)}, u32[]{:S(2)}) collective-permute-start(f32[136,128]{1,0:T(8,128)S(1)} %get-tuple-element.58.refs_0_), channel_id=1, source_target_pairs={{0,3},{1,2},{2,1},{3,0},{4,7},{5,6},{6,5},{7,4},{8,11},{9,10},{10,... | collective-permute-start | bytes 208904 | tf_op jit(solution)/shard_map/ppermute | solution.py:592
  30.8 5.3 %collective-permute-start.7 = (f32[136,128]{1,0:T(8,128)S(1)}, f32[136,128]{1,0:T(8,128)S(1)}, u32[]{:S(2)}, u32[]{:S(2)}) collective-permute-start(f32[136,128]{1,0:T(8,128)S(1)} %get-tuple-element.58.refs_0_), channel_id=1, source_target_pairs={{0,2},{1,3},{2,0},{3,1},{4,6},{5,7},{6,4},{7,5},{8,10},{9,11},{10,... | collective-permute-start | bytes 208904 | tf_op jit(solution)/shard_map/ppermute | solution.py:592
  31.8 4.3 %collective-permute-start.6 = (f32[136,128]{1,0:T(8,128)S(1)}, f32[136,128]{1,0:T(8,128)S(1)}, u32[]{:S(2)}, u32[]{:S(2)}) collective-permute-start(f32[136,128]{1,0:T(8,128)S(1)} %get-tuple-element.58.refs_0_), channel_id=1, source_target_pairs={{0,1},{1,0},{2,3},{3,2},{4,5},{5,4},{6,7},{7,6},{8,9},{9,8},{10,11... | collective-permute-start | bytes 208904 | tf_op jit(solution)/shard_map/ppermute | solution.py:592
  36.9 6.9 %collective-permute-start.11 = (f32[136,128]{1,0:T(8,128)S(1)}, f32[136,128]{1,0:T(8,128)S(1)}, u32[]{:S(2)}, u32[]{:S(2)}) collective-permute-start(f32[136,128]{1,0:T(8,128)S(1)} %get-tuple-element.60.refs_0_), channel_id=1, source_target_pairs={{0,12},{4,8},{8,4},{12,0},{1,13},{5,9},{9,5},{13,1},{2,14},{6,10},... | collective-permute-start | bytes 208904 | tf_op jit(solution)/shard_map/ppermute | solution.py:592
  40.7 5.9 %collective-permute-start.10 = (f32[136,128]{1,0:T(8,128)S(1)}, f32[136,128]{1,0:T(8,128)S(1)}, u32[]{:S(2)}, u32[]{:S(2)}) collective-permute-start(f32[136,128]{1,0:T(8,128)S(1)} %get-tuple-element.60.refs_0_), channel_id=1, source_target_pairs={{0,8},{4,12},{8,0},{12,4},{1,9},{5,13},{9,1},{13,5},{2,10},{6,14},... | collective-permute-start | bytes 208904 | tf_op jit(solution)/shard_map/ppermute | solution.py:592
  40.7 5.9 %collective-permute-start.9 = (f32[136,128]{1,0:T(8,128)S(1)}, f32[136,128]{1,0:T(8,128)S(1)}, u32[]{:S(2)}, u32[]{:S(2)}) collective-permute-start(f32[136,128]{1,0:T(8,128)S(1)} %get-tuple-element.60.refs_0_), channel_id=1, source_target_pairs={{0,4},{4,0},{8,12},{12,8},{1,5},{5,1},{9,13},{13,9},{2,6},{6,2},{1... | collective-permute-start | bytes 208904 | tf_op jit(solution)/shard_map/ppermute | solution.py:592
  51.2 4.5 %collective-permute-start.14 = (f32[136,128]{1,0:T(8,128)S(1)}, f32[136,128]{1,0:T(8,128)S(1)}, u32[]{:S(2)}, u32[]{:S(2)}) collective-permute-start(f32[136,128]{1,0:T(8,128)S(1)} %get-tuple-element.67.refs_0_), channel_id=1, source_target_pairs={{0,3},{1,2},{2,1},{3,0},{4,7},{5,6},{6,5},{7,4},{8,11},{9,10},{10,... | collective-permute-start | bytes 208904 | tf_op jit(solution)/shard_map/ppermute | solution.py:592
  51.4 5.8 %collective-permute-start.13 = (f32[136,128]{1,0:T(8,128)S(1)}, f32[136,128]{1,0:T(8,128)S(1)}, u32[]{:S(2)}, u32[]{:S(2)}) collective-permute-start(f32[136,128]{1,0:T(8,128)S(1)} %get-tuple-element.67.refs_0_), channel_id=1, source_target_pairs={{0,2},{1,3},{2,0},{3,1},{4,6},{5,7},{6,4},{7,5},{8,10},{9,11},{10,... | collective-permute-start | bytes 208904 | tf_op jit(solution)/shard_map/ppermute | solution.py:592
  52.7 4.5 %collective-permute-start.12 = (f32[136,128]{1,0:T(8,128)S(1)}, f32[136,128]{1,0:T(8,128)S(1)}, u32[]{:S(2)}, u32[]{:S(2)}) collective-permute-start(f32[136,128]{1,0:T(8,128)S(1)} %get-tuple-element.67.refs_0_), channel_id=1, source_target_pairs={{0,1},{1,0},{2,3},{3,2},{4,5},{5,4},{6,7},{7,6},{8,9},{9,8},{10,11... | collective-permute-start | bytes 208904 | tf_op jit(solution)/shard_map/ppermute | solution.py:592
  58.0 6.9 %collective-permute-start.17 = (f32[136,128]{1,0:T(8,128)S(1)}, f32[136,128]{1,0:T(8,128)S(1)}, u32[]{:S(2)}, u32[]{:S(2)}) collective-permute-start(f32[136,128]{1,0:T(8,128)S(1)} %get-tuple-element.68.refs_0_), channel_id=1, source_target_pairs={{0,12},{4,8},{8,4},{12,0},{1,13},{5,9},{9,5},{13,1},{2,14},{6,10},... | collective-permute-start | bytes 208904 | tf_op jit(solution)/shard_map/ppermute | solution.py:592
  59.7 7.3 %collective-permute-start.16 = (f32[136,128]{1,0:T(8,128)S(1)}, f32[136,128]{1,0:T(8,128)S(1)}, u32[]{:S(2)}, u32[]{:S(2)}) collective-permute-start(f32[136,128]{1,0:T(8,128)S(1)} %get-tuple-element.68.refs_0_), channel_id=1, source_target_pairs={{0,8},{4,12},{8,0},{12,4},{1,9},{5,13},{9,1},{13,5},{2,10},{6,14},... | collective-permute-start | bytes 208904 | tf_op jit(solution)/shard_map/ppermute | solution.py:592
  59.9 7.1 %collective-permute-start.15 = (f32[136,128]{1,0:T(8,128)S(1)}, f32[136,128]{1,0:T(8,128)S(1)}, u32[]{:S(2)}, u32[]{:S(2)}) collective-permute-start(f32[136,128]{1,0:T(8,128)S(1)} %get-tuple-element.68.refs_0_), channel_id=1, source_target_pairs={{0,4},{4,0},{8,12},{12,8},{1,5},{5,1},{9,13},{13,9},{2,6},{6,2},{1... | collective-permute-start | bytes 208904 | tf_op jit(solution)/shard_map/ppermute | solution.py:592

commit v6 on v5

--- a/solution.py
+++ b/solution.py
@@ -181,8 +181,8 @@
 
 def setup_kernel(stages, total, anchors, *refs):
     sources, refs = refs[:6], refs[6:]
-    message, rhs, la, lb, ra, rb, basis, chosen_out, params = refs[:9]
-    pts, skel, keep, scales, noise, sems = refs[9:]
+    message, rhs, la, lb, moved, basis, chosen_out, params = refs[:8]
+    pts, skel, keep, scales, noise, sems = refs[8:]
     targets = (pts, rhs, skel, keep, scales, noise)
     copies = [
         pltpu.make_async_copy(source, target, sems.at[i])
@@ -209,7 +209,8 @@
     write_wide(message, dots + 8, chosen)
     scaled = (points - shift) * inverse
     unit = unit_of(scaled)
-    (la[...], lb[...]), (ra[...], rb[...]) = features(scaled, unit)
+    moved[...] = scaled
+    (la[...], lb[...]), _ = features(scaled, unit)
     _, own = features((chosen - shift) * inverse, unit)
     for i in range(count // STRIP):
         strip = slice(i * STRIP, (i + 1) * STRIP)
@@ -239,16 +240,17 @@
                 slot += 1
 
 
-def dense_kernel(start, la, lb, ra, rb, rhs, params, tie, stacked, near):
+def dense_kernel(start, la, lb, moved, rhs, params, tie, stacked, near):
     size, width = la.shape[0], stacked.shape[1]
     unit = params[0:1, 3:4]
+    _, (ra, rb) = features(moved[:, start : start + width], unit)
 
     def body(k, carry):
         top = pl.multiple_of(k * STRIP, STRIP)
         strip, below = pl.ds(top, STRIP), pl.ds(pl.multiple_of(size + top, STRIP), STRIP)
         left = la[strip, :], lb[strip, :]
         for j in range(0, width, BLOCK):
-            cut = slice(start + j, start + j + BLOCK)
+            cut = slice(j, j + BLOCK)
             high, low = split(gauss(left, (ra[:, cut], rb[:, cut]), unit))
             stacked[strip, j : j + BLOCK] = high
             stacked[below, j : j + BLOCK] = low
@@ -616,15 +618,14 @@
     offsets = [sum(counts[:i]) - i for i in range(len(counts))]
     stage_count = len(stages) - 1
 
-    message, rhs, la, lb, ra, rb, basis, chosen, params = call(
+    message, rhs, la, lb, moved, basis, chosen, params = call(
         functools.partial(setup_kernel, bases, total, subs),
         [
             f32_shape(message_rows(rows, rank, True), LANES),
             f32_shape(rows, size),
             bf16_shape(size, 16),
             bf16_shape(size, 80),
-            bf16_shape(16, size),
-            bf16_shape(80, size),
+            f32_shape(8, size),
             bf16_shape(2 * size, rank),
             jax.ShapeDtypeStruct((slots, rank), jnp.int32),
             f32_shape(8, 128),
@@ -654,7 +655,7 @@
         nodes = count - 1
         return [bf16_shape(nodes, 4 * rank, rank), bf16_shape(nodes, 2 * rank, rank)]
 
-    first_width = size // BLOCK * 3 // 8 * BLOCK
+    first_width = size // BLOCK // 2 * BLOCK
     widths = [first_width, size - first_width]
     dense, near_parts = [], []
 
@@ -662,7 +663,7 @@
         stacked, near = call(
             functools.partial(dense_kernel, start),
             [resident_shape(2 * size, width), f32_shape(rows, width)],
-            [la, lb, ra, rb, rhs, params, tie],
+            [la, lb, moved, rhs, params, tie],
             cost=(6 * rows * size * width + 192 * size * width, size * width),
             name="dense",
         )

time: 69.6 us -> 68.8 us (0.989)
  transfers between devices with their start and end apart: 18 -> 18, of which waited for: 9 -> 10; matrix products, arithmetic and copies ran while one was open for 0% -> 0% of each run, Pallas kernels for 16% -> 17%
where the time goes in v6:
time: 68.8 us; the launch traced here: 68.7 us
  Pallas kernels  30.2 us (44%)
  starting transfers between devices  20.6 us (30%)
  waiting for transfers between devices  16.3 us (24%)
  between operations  1.56 us (2%)
    pallas_call x15, Pallas kernels, call(): pl.pallas_call(kernel, out_shape=list(out_shape), in_specs=[ANY if i in a...  30.2 us
    ppermute x18, starting transfers between devices, gather(): return [value] + [lax.ppermute(value, axis, pair) for pair in pairs]  20.6 us
    ppermute x18, waiting for transfers between devices, gather(): return [value] + [lax.ppermute(value, axis, pair) for pair in pairs]  16.3 us
  transfers between devices with their start and end apart: 18, of which 10 were waited for; matrix products, arithmetic and copies ran while one was open for 0% of the time, Pallas kernels for 17%

profile of v6, /device:TPU:0, one launch (start us, length us, event | category | flops | bytes accessed | tf_op | source)
XLA Modules:
  0.0 68.7 jit_solution(9605361747025227943)
XLA Ops:
  1.3 3.2 %setup.1 = (f32[152,128]{1,0:T(8,128)S(1)}, f32[64,2048]{1,0:T(8,128)S(1)}, bf16[2048,16]{1,0:T(8,128)(2,1)S(1)}, bf16[2048,80]{1,0:T(8,128)(2,1)S(1)}, f32[8,20...) custom-call(f32[6,2048]{1,0:T(8,128)} %refs_0_.1, ...), custom_call_target="tpu_custom_call" | custom-call | tf_op jit(solution)/shard_map/setup/pallas_call | solution.py:42
  4.5 2.4 %collective-permute-start.2 = (f32[152,128]{1,0:T(8,128)S(1)}, f32[152,128]{1,0:T(8,128)S(1)}, u32[]{:S(2)}, u32[]{:S(2)}) collective-permute-start(f32[152,128]{1,0:T(8,128)S(1)} %get-tuple-element.38.refs_0_), channel_id=1, source_target_pairs={{0,3},{1,2},{2,1},{3,0},{4,7},{5,6},{6,5},{7,4},{8,11},{9,10},{10,... | collective-permute-start | bytes 233480 | tf_op jit(solution)/shard_map/ppermute | solution.py:594
  7.7 3.7 %dense.2 = (bf16[4096,1024]{1,0:T(8,128)(2,1)S(1)}, f32[64,1024]{1,0:T(8,128)S(1)}) custom-call(bf16[2048,16]{1,0:T(8,128)(2,1)S(1)} %get-tuple-element.41.la, bf16[2048,80]{1,0:T(8,128)(2,1)S(1)} %get-tuple-element.42.lb, f32[8,2048]{1,0:T(8,128)S(1)} %get-tuple-element.43.moved, f32[64,2048]{1,0:T(8,128)S(1)} %get-tuple-element.44.rhs.refs_13_, ...), custom_call_target="tpu_custom_call" | custom-call | flops 1207959552 | bytes 9641984 | tf_op jit(solution)/shard_map/dense/pallas_call | solution.py:42
  11.9 1.6 %lower_first.1 = (f32[152,128]{1,0:T(8,128)S(1)}, bf16[3,1024,256]{2,1,0:T(8,128)(2,1)S(1)}, f32[3,8,256]{2,1,0:T(8,128)S(1)}) custom-call(f32[152,128]{1,0:T(8,128)S(1)} %get-tuple-element.38.refs_0_, f32[152,128]{1,0:T(8,128)S(1)} %collective-permute-done.refs_1_, f32[152,128]{1,0:T(8,128)S(1)} %collective-permute-done.1.refs_2_, ...), custom_call_target="tpu_custom_call" | custom-call | tf_op jit(solution)/shard_map/lower_first/pallas_call | solution.py:42
  13.5 4.1 %collective-permute-start.5 = (f32[152,128]{1,0:T(8,128)S(1)}, f32[152,128]{1,0:T(8,128)S(1)}, u32[]{:S(2)}, u32[]{:S(2)}) collective-permute-start(f32[152,128]{1,0:T(8,128)S(1)} %get-tuple-element.46.refs_0_.tie), channel_id=1, source_target_pairs={{0,12},{4,8},{8,4},{12,0},{1,13},{5,9},{9,5},{13,1},{2,14},{6,10},... | collective-permute-start | bytes 233480 | tf_op jit(solution)/shard_map/ppermute | solution.py:594
  18.3 3.7 %dense.3 = (bf16[4096,1024]{1,0:T(8,128)(2,1)S(1)}, f32[64,1024]{1,0:T(8,128)S(1)}) custom-call(bf16[2048,16]{1,0:T(8,128)(2,1)S(1)} %get-tuple-element.41.la, bf16[2048,80]{1,0:T(8,128)(2,1)S(1)} %get-tuple-element.42.lb, f32[8,2048]{1,0:T(8,128)S(1)} %get-tuple-element.43.moved, f32[64,2048]{1,0:T(8,128)S(1)} %get-tuple-element.44.rhs.refs_13_, ...), custom_call_target="tpu_custom_call" | custom-call | flops 1207959552 | bytes 9715712 | tf_op jit(solution)/shard_map/dense/pallas_call | solution.py:42
  22.6 1.0 %lower_rest.1 = (bf16[3,512,256]{2,1,0:T(8,128)(2,1)S(1)}, f32[2,64,256]{2,1,0:T(8,128)S(1)}) custom-call(f32[152,128]{1,0:T(8,128)S(1)} %get-tuple-element.38.refs_0_, f32[152,128]{1,0:T(8,128)S(1)} %collective-permute-done.refs_1_, f32[152,128]{1,0:T(8,128)S(1)} %collective-permute-done.1.refs_2_, f32[152,128]{1,0:T(8,128)S(1)} %collective-permute-done.2.refs_3_, ...), custom_call_target="tpu_custom_call" | custom-call | flops 805306368 | bytes 2830336 | tf_op jit(solution)/shard_map/lower_rest/pallas_call | solution.py:42
  25.4 4.6 %first.1 = (f32[136,128]{1,0:T(8,128)S(1)}, f32[64,2048]{1,0:T(8,128)S(1)}, f32[64,2048]{1,0:T(8,128)S(1)}, f32[64,128]{1,0:T(8,128)S(1)}) custom-call(f32[152,128]{1,0:T(8,128)S(1)} %get-tuple-element.46.refs_0_.tie, f32[152,128]{1,0:T(8,128)S(1)} %collective-permute-done.3.refs_1_, f32[152,128]{1,0:T(8,128)S(1)} %collective-permute-done.4.refs_2_, ...), custom_call_target="tpu_custom_call" | custom-call | tf_op jit(solution)/shard_map/first/pallas_call | solution.py:42
  30.5 1.1 %collective-permute-start.7 = (f32[136,128]{1,0:T(8,128)S(1)}, f32[136,128]{1,0:T(8,128)S(1)}, u32[]{:S(2)}, u32[]{:S(2)}) collective-permute-start(f32[136,128]{1,0:T(8,128)S(1)} %get-tuple-element.56.refs_0_), channel_id=1, source_target_pairs={{0,2},{1,3},{2,0},{3,1},{4,6},{5,7},{6,4},{7,5},{8,10},{9,11},{10,... | collective-permute-start | bytes 208904 | tf_op jit(solution)/shard_map/ppermute | solution.py:594
  31.9 2.5 %collective-permute-done.8.refs_3_ = f32[136,128]{1,0:T(8,128)S(1)} collective-permute-done((f32[136,128]{1,0:T(8,128)S(1)}, f32[136,128]{1,0:T(8,128)S(1)}, u32[]{:S(2)}, u32[]{:S(2)}) %collective-permute-start.8) | collective-permute-done | bytes 69664 | tf_op jit(solution)/shard_map/ppermute | solution.py:594
  34.4 1.6 %collective-permute-done.7.refs_2_ = f32[136,128]{1,0:T(8,128)S(1)} collective-permute-done((f32[136,128]{1,0:T(8,128)S(1)}, f32[136,128]{1,0:T(8,128)S(1)}, u32[]{:S(2)}, u32[]{:S(2)}) %collective-permute-start.7) | collective-permute-done | bytes 69664 | tf_op jit(solution)/shard_map/ppermute | solution.py:594
  36.8 3.1 %collective-permute-start.11 = (f32[136,128]{1,0:T(8,128)S(1)}, f32[136,128]{1,0:T(8,128)S(1)}, u32[]{:S(2)}, u32[]{:S(2)}) collective-permute-start(f32[136,128]{1,0:T(8,128)S(1)} %get-tuple-element.58.refs_0_), channel_id=1, source_target_pairs={{0,12},{4,8},{8,4},{12,0},{1,13},{5,9},{9,5},{13,1},{2,14},{6,10},... | collective-permute-start | bytes 208904 | tf_op jit(solution)/shard_map/ppermute | solution.py:594
  39.9 1.4 %collective-permute-start.9 = (f32[136,128]{1,0:T(8,128)S(1)}, f32[136,128]{1,0:T(8,128)S(1)}, u32[]{:S(2)}, u32[]{:S(2)}) collective-permute-start(f32[136,128]{1,0:T(8,128)S(1)} %get-tuple-element.58.refs_0_), channel_id=1, source_target_pairs={{0,4},{4,0},{8,12},{12,8},{1,5},{5,1},{9,13},{13,9},{2,6},{6,2},{1... | collective-permute-start | bytes 208904 | tf_op jit(solution)/shard_map/ppermute | solution.py:594
  41.2 1.3 %upper_build.3 = (bf16[3,1024,256]{2,1,0:T(8,128)(2,1)S(1)}, bf16[3,512,256]{2,1,0:T(8,128)(2,1)S(1)}) custom-call(f32[152,128]{1,0:T(8,128)S(1)} %get-tuple-element.46.refs_0_.tie, f32[152,128]{1,0:T(8,128)S(1)} %collective-permute-done.3.refs_1_, f32[152,128]{1,0:T(8,128)S(1)} %collective-permute-done.4.refs_2_, ...), custom_call_target="tpu_custom_call" | custom-call | flops 805306368 | bytes 2713600 | tf_op jit(solution)/shard_map/upper_build/pallas_call | solution.py:42
  43.6 2.4 %collective-permute-done.10.refs_2_ = f32[136,128]{1,0:T(8,128)S(1)} collective-permute-done((f32[136,128]{1,0:T(8,128)S(1)}, f32[136,128]{1,0:T(8,128)S(1)}, u32[]{:S(2)}, u32[]{:S(2)}) %collective-permute-start.10) | collective-permute-done | bytes 69664 | tf_op jit(solution)/shard_map/ppermute | solution.py:594
  46.0 4.6 %second.1 = (f32[136,128]{1,0:T(8,128)S(1)}, f32[64,2048]{1,0:T(8,128)S(1)}, f32[64,2048]{1,0:T(8,128)S(1)}, f32[64,2048]{1,0:T(8,128)S(1)}, f32[64,128]{1,0:T(8,128)S(1)}) custom-call(f32[136,128]{1,0:T(8,128)S(1)} %get-tuple-element.58.refs_0_, f32[136,128]{1,0:T(8,128)S(1)} %collective-permute-done.9.refs_1_, ...), custom_call_target="tpu_custom_call" | custom-call | tf_op jit(solution)/shard_map/second/pallas_call | solution.py:42
  50.9 1.4 %collective-permute-start.13 = (f32[136,128]{1,0:T(8,128)S(1)}, f32[136,128]{1,0:T(8,128)S(1)}, u32[]{:S(2)}, u32[]{:S(2)}) collective-permute-start(f32[136,128]{1,0:T(8,128)S(1)} %get-tuple-element.65.refs_0_), channel_id=1, source_target_pairs={{0,2},{1,3},{2,0},{3,1},{4,6},{5,7},{6,4},{7,5},{8,10},{9,11},{10,... | collective-permute-start | bytes 208904 | tf_op jit(solution)/shard_map/ppermute | solution.py:594
  52.5 2.4 %collective-permute-done.14.refs_3_ = f32[136,128]{1,0:T(8,128)S(1)} collective-permute-done((f32[136,128]{1,0:T(8,128)S(1)}, f32[136,128]{1,0:T(8,128)S(1)}, u32[]{:S(2)}, u32[]{:S(2)}) %collective-permute-start.14) | collective-permute-done | bytes 69664 | tf_op jit(solution)/shard_map/ppermute | solution.py:594
  54.9 1.7 %collective-permute-done.13.refs_2_ = f32[136,128]{1,0:T(8,128)S(1)} collective-permute-done((f32[136,128]{1,0:T(8,128)S(1)}, f32[136,128]{1,0:T(8,128)S(1)}, u32[]{:S(2)}, u32[]{:S(2)}) %collective-permute-start.13) | collective-permute-done | bytes 69664 | tf_op jit(solution)/shard_map/ppermute | solution.py:594
  57.4 1.8 %collective-permute-start.17 = (f32[136,128]{1,0:T(8,128)S(1)}, f32[136,128]{1,0:T(8,128)S(1)}, u32[]{:S(2)}, u32[]{:S(2)}) collective-permute-start(f32[136,128]{1,0:T(8,128)S(1)} %get-tuple-element.66.refs_0_), channel_id=1, source_target_pairs={{0,12},{4,8},{8,4},{12,0},{1,13},{5,9},{9,5},{13,1},{2,14},{6,10},... | collective-permute-start | bytes 208904 | tf_op jit(solution)/shard_map/ppermute | solution.py:594
  59.2 2.7 %collective-permute-start.15 = (f32[136,128]{1,0:T(8,128)S(1)}, f32[136,128]{1,0:T(8,128)S(1)}, u32[]{:S(2)}, u32[]{:S(2)}) collective-permute-start(f32[136,128]{1,0:T(8,128)S(1)} %get-tuple-element.66.refs_0_), channel_id=1, source_target_pairs={{0,4},{4,0},{8,12},{12,8},{1,5},{5,1},{9,13},{13,9},{2,6},{6,2},{1... | collective-permute-start | bytes 208904 | tf_op jit(solution)/shard_map/ppermute | solution.py:594
  62.2 2.2 %collective-permute-done.17.refs_3_ = f32[136,128]{1,0:T(8,128)S(1)} collective-permute-done((f32[136,128]{1,0:T(8,128)S(1)}, f32[136,128]{1,0:T(8,128)S(1)}, u32[]{:S(2)}, u32[]{:S(2)}) %collective-permute-start.17) | collective-permute-done | bytes 69664 | tf_op jit(solution)/shard_map/ppermute | solution.py:594
  64.4 1.9 %collective-permute-done.16.refs_2_ = f32[136,128]{1,0:T(8,128)S(1)} collective-permute-done((f32[136,128]{1,0:T(8,128)S(1)}, f32[136,128]{1,0:T(8,128)S(1)}, u32[]{:S(2)}, u32[]{:S(2)}) %collective-permute-start.16) | collective-permute-done | bytes 69664 | tf_op jit(solution)/shard_map/ppermute | solution.py:594
  66.3 2.2 %last.1 = (f32[64,2048]{1,0:T(8,128)}, f32[64,2048]{1,0:T(8,128)}) custom-call(f32[136,128]{1,0:T(8,128)S(1)} %get-tuple-element.66.refs_0_, f32[136,128]{1,0:T(8,128)S(1)} %collective-permute-done.15.refs_1_, f32[136,128]{1,0:T(8,128)S(1)} %collective-permute-done.16.refs_2_, f32[136,128]{1,0:T(8,128)S(1)} %collective-permute-done.17.refs_3_, ...), custom_call_target="tpu_custom_call" | custom-call | tf_op jit(solution)/shard_map/last/pallas_call | solution.py:42
  (27 shorter events, 8.5 us)
Async XLA Ops:
  4.5 6.8 %collective-permute-start.2 = (f32[152,128]{1,0:T(8,128)S(1)}, f32[152,128]{1,0:T(8,128)S(1)}, u32[]{:S(2)}, u32[]{:S(2)}) collective-permute-start(f32[152,128]{1,0:T(8,128)S(1)} %get-tuple-element.38.refs_0_), channel_id=1, source_target_pairs={{0,3},{1,2},{2,1},{3,0},{4,7},{5,6},{6,5},{7,4},{8,11},{9,10},{10,... | collective-permute-start | bytes 233480 | tf_op jit(solution)/shard_map/ppermute | solution.py:594
  7.0 4.9 %collective-permute-start.1 = (f32[152,128]{1,0:T(8,128)S(1)}, f32[152,128]{1,0:T(8,128)S(1)}, u32[]{:S(2)}, u32[]{:S(2)}) collective-permute-start(f32[152,128]{1,0:T(8,128)S(1)} %get-tuple-element.38.refs_0_), channel_id=1, source_target_pairs={{0,2},{1,3},{2,0},{3,1},{4,6},{5,7},{6,4},{7,5},{8,10},{9,11},{10,... | collective-permute-start | bytes 233480 | tf_op jit(solution)/shard_map/ppermute | solution.py:594
  7.6 4.3 %collective-permute-start = (f32[152,128]{1,0:T(8,128)S(1)}, f32[152,128]{1,0:T(8,128)S(1)}, u32[]{:S(2)}, u32[]{:S(2)}) collective-permute-start(f32[152,128]{1,0:T(8,128)S(1)} %get-tuple-element.38.refs_0_), channel_id=1, source_target_pairs={{0,1},{1,0},{2,3},{3,2},{4,5},{5,4},{6,7},{7,6},{8,9},{9,8},{10,11... | collective-permute-start | bytes 233480 | tf_op jit(solution)/shard_map/ppermute | solution.py:594
  13.5 10.1 %collective-permute-start.5 = (f32[152,128]{1,0:T(8,128)S(1)}, f32[152,128]{1,0:T(8,128)S(1)}, u32[]{:S(2)}, u32[]{:S(2)}) collective-permute-start(f32[152,128]{1,0:T(8,128)S(1)} %get-tuple-element.46.refs_0_.tie), channel_id=1, source_target_pairs={{0,12},{4,8},{8,4},{12,0},{1,13},{5,9},{9,5},{13,1},{2,14},{6,10},... | collective-permute-start | bytes 233480 | tf_op jit(solution)/shard_map/ppermute | solution.py:594
  17.6 6.8 %collective-permute-start.4 = (f32[152,128]{1,0:T(8,128)S(1)}, f32[152,128]{1,0:T(8,128)S(1)}, u32[]{:S(2)}, u32[]{:S(2)}) collective-permute-start(f32[152,128]{1,0:T(8,128)S(1)} %get-tuple-element.46.refs_0_.tie), channel_id=1, source_target_pairs={{0,8},{4,12},{8,0},{12,4},{1,9},{5,13},{9,1},{13,5},{2,10},{6,14},... | collective-permute-start | bytes 233480 | tf_op jit(solution)/shard_map/ppermute | solution.py:594
  17.7 6.8 %collective-permute-start.3 = (f32[152,128]{1,0:T(8,128)S(1)}, f32[152,128]{1,0:T(8,128)S(1)}, u32[]{:S(2)}, u32[]{:S(2)}) collective-permute-start(f32[152,128]{1,0:T(8,128)S(1)} %get-tuple-element.46.refs_0_.tie), channel_id=1, source_target_pairs={{0,4},{4,0},{8,12},{12,8},{1,5},{5,1},{9,13},{13,9},{2,6},{6,2},{1... | collective-permute-start | bytes 233480 | tf_op jit(solution)/shard_map/ppermute | solution.py:594
  30.0 4.4 %collective-permute-start.8 = (f32[136,128]{1,0:T(8,128)S(1)}, f32[136,128]{1,0:T(8,128)S(1)}, u32[]{:S(2)}, u32[]{:S(2)}) collective-permute-start(f32[136,128]{1,0:T(8,128)S(1)} %get-tuple-element.56.refs_0_), channel_id=1, source_target_pairs={{0,3},{1,2},{2,1},{3,0},{4,7},{5,6},{6,5},{7,4},{8,11},{9,10},{10,... | collective-permute-start | bytes 208904 | tf_op jit(solution)/shard_map/ppermute | solution.py:594
  30.5 5.5 %collective-permute-start.7 = (f32[136,128]{1,0:T(8,128)S(1)}, f32[136,128]{1,0:T(8,128)S(1)}, u32[]{:S(2)}, u32[]{:S(2)}) collective-permute-start(f32[136,128]{1,0:T(8,128)S(1)} %get-tuple-element.56.refs_0_), channel_id=1, source_target_pairs={{0,2},{1,3},{2,0},{3,1},{4,6},{5,7},{6,4},{7,5},{8,10},{9,11},{10,... | collective-permute-start | bytes 208904 | tf_op jit(solution)/shard_map/ppermute | solution.py:594
  31.6 4.4 %collective-permute-start.6 = (f32[136,128]{1,0:T(8,128)S(1)}, f32[136,128]{1,0:T(8,128)S(1)}, u32[]{:S(2)}, u32[]{:S(2)}) collective-permute-start(f32[136,128]{1,0:T(8,128)S(1)} %get-tuple-element.56.refs_0_), channel_id=1, source_target_pairs={{0,1},{1,0},{2,3},{3,2},{4,5},{5,4},{6,7},{7,6},{8,9},{9,8},{10,11... | collective-permute-start | bytes 208904 | tf_op jit(solution)/shard_map/ppermute | solution.py:594
  36.8 6.9 %collective-permute-start.11 = (f32[136,128]{1,0:T(8,128)S(1)}, f32[136,128]{1,0:T(8,128)S(1)}, u32[]{:S(2)}, u32[]{:S(2)}) collective-permute-start(f32[136,128]{1,0:T(8,128)S(1)} %get-tuple-element.58.refs_0_), channel_id=1, source_target_pairs={{0,12},{4,8},{8,4},{12,0},{1,13},{5,9},{9,5},{13,1},{2,14},{6,10},... | collective-permute-start | bytes 208904 | tf_op jit(solution)/shard_map/ppermute | solution.py:594
  39.9 6.2 %collective-permute-start.10 = (f32[136,128]{1,0:T(8,128)S(1)}, f32[136,128]{1,0:T(8,128)S(1)}, u32[]{:S(2)}, u32[]{:S(2)}) collective-permute-start(f32[136,128]{1,0:T(8,128)S(1)} %get-tuple-element.58.refs_0_), channel_id=1, source_target_pairs={{0,8},{4,12},{8,0},{12,4},{1,9},{5,13},{9,1},{13,5},{2,10},{6,14},... | collective-permute-start | bytes 208904 | tf_op jit(solution)/shard_map/ppermute | solution.py:594
  39.9 6.2 %collective-permute-start.9 = (f32[136,128]{1,0:T(8,128)S(1)}, f32[136,128]{1,0:T(8,128)S(1)}, u32[]{:S(2)}, u32[]{:S(2)}) collective-permute-start(f32[136,128]{1,0:T(8,128)S(1)} %get-tuple-element.58.refs_0_), channel_id=1, source_target_pairs={{0,4},{4,0},{8,12},{12,8},{1,5},{5,1},{9,13},{13,9},{2,6},{6,2},{1... | collective-permute-start | bytes 208904 | tf_op jit(solution)/shard_map/ppermute | solution.py:594
  50.6 4.3 %collective-permute-start.14 = (f32[136,128]{1,0:T(8,128)S(1)}, f32[136,128]{1,0:T(8,128)S(1)}, u32[]{:S(2)}, u32[]{:S(2)}) collective-permute-start(f32[136,128]{1,0:T(8,128)S(1)} %get-tuple-element.65.refs_0_), channel_id=1, source_target_pairs={{0,3},{1,2},{2,1},{3,0},{4,7},{5,6},{6,5},{7,4},{8,11},{9,10},{10,... | collective-permute-start | bytes 208904 | tf_op jit(solution)/shard_map/ppermute | solution.py:594
  50.9 5.7 %collective-permute-start.13 = (f32[136,128]{1,0:T(8,128)S(1)}, f32[136,128]{1,0:T(8,128)S(1)}, u32[]{:S(2)}, u32[]{:S(2)}) collective-permute-start(f32[136,128]{1,0:T(8,128)S(1)} %get-tuple-element.65.refs_0_), channel_id=1, source_target_pairs={{0,2},{1,3},{2,0},{3,1},{4,6},{5,7},{6,4},{7,5},{8,10},{9,11},{10,... | collective-permute-start | bytes 208904 | tf_op jit(solution)/shard_map/ppermute | solution.py:594
  52.3 4.3 %collective-permute-start.12 = (f32[136,128]{1,0:T(8,128)S(1)}, f32[136,128]{1,0:T(8,128)S(1)}, u32[]{:S(2)}, u32[]{:S(2)}) collective-permute-start(f32[136,128]{1,0:T(8,128)S(1)} %get-tuple-element.65.refs_0_), channel_id=1, source_target_pairs={{0,1},{1,0},{2,3},{3,2},{4,5},{5,4},{6,7},{7,6},{8,9},{9,8},{10,11... | collective-permute-start | bytes 208904 | tf_op jit(solution)/shard_map/ppermute | solution.py:594
  57.4 7.0 %collective-permute-start.17 = (f32[136,128]{1,0:T(8,128)S(1)}, f32[136,128]{1,0:T(8,128)S(1)}, u32[]{:S(2)}, u32[]{:S(2)}) collective-permute-start(f32[136,128]{1,0:T(8,128)S(1)} %get-tuple-element.66.refs_0_), channel_id=1, source_target_pairs={{0,12},{4,8},{8,4},{12,0},{1,13},{5,9},{9,5},{13,1},{2,14},{6,10},... | collective-permute-start | bytes 208904 | tf_op jit(solution)/shard_map/ppermute | solution.py:594
  59.2 7.1 %collective-permute-start.16 = (f32[136,128]{1,0:T(8,128)S(1)}, f32[136,128]{1,0:T(8,128)S(1)}, u32[]{:S(2)}, u32[]{:S(2)}) collective-permute-start(f32[136,128]{1,0:T(8,128)S(1)} %get-tuple-element.66.refs_0_), channel_id=1, source_target_pairs={{0,8},{4,12},{8,0},{12,4},{1,9},{5,13},{9,1},{13,5},{2,10},{6,14},... | collective-permute-start | bytes 208904 | tf_op jit(solution)/shard_map/ppermute | solution.py:594
  59.2 7.1 %collective-permute-start.15 = (f32[136,128]{1,0:T(8,128)S(1)}, f32[136,128]{1,0:T(8,128)S(1)}, u32[]{:S(2)}, u32[]{:S(2)}) collective-permute-start(f32[136,128]{1,0:T(8,128)S(1)} %get-tuple-element.66.refs_0_), channel_id=1, source_target_pairs={{0,4},{4,0},{8,12},{12,8},{1,5},{5,1},{9,13},{13,9},{2,6},{6,2},{1... | collective-permute-start | bytes 208904 | tf_op jit(solution)/shard_map/ppermute | solution.py:594
